TPU v7x, 512 devices: a whole 4x8x8 slice. The times are simulated.
512 devices in a mesh: aux: 32 (over x, z), row: 16 (over y, core).
Axes of the slice: x: 4, y: 8, z: 8, core: 2. Of those that a mesh axis runs over, the one named last changes fastest.
Arguments:
- slabs: bfloat16 [256, 400, 2048], P('aux', None, 'row'), may hold values from -0.33398438 to 0.33398438
- significant: int32 [256, 32], P('aux'), may hold values from 0 to 1, as said below
Outputs:
- exchange: float32 [2048, 2048], P('row', 'aux')
Inputs may be any that keep to these rules, and one draw needn't show every extreme that they name: `significant`: each entry is 0 or 1; the share of ones differs between the auxiliary functions of different devices.
All inputs are finite; a program needn't handle non-finite values.
Results may differ from a plain program's by a relative error of at most 0.0003.
Values may be sent and summed in bfloat16 or wider, within the bound.
No kernel may reach another device: no remote copies, remote signals or barrier semaphores. Data moves between devices by JAX's collectives and lax.ppermute only.
A program may use at most 64 MiB of HBM per device.

v0:
```python
import jax
import jax.numpy as jnp
from jax import lax
from jax.sharding import PartitionSpec as P

BS = 64


def in_order(parts, dim):
    parts = jnp.moveaxis(parts, 0, dim)
    dims = parts.shape
    return parts.reshape(*dims[:dim], dims[dim] * dims[dim + 1], *dims[dim + 2 :])


def piecewise(shard, axis, dim, work, out_dim):
    span = shard.shape[dim]
    pieces = jnp.split(shard, 2, axis=dim) if span % 2 == 0 else [shard]
    first = jnp.arange(lax.axis_size(axis)) * span
    parts = [lax.all_gather(slab, axis) for slab in pieces]
    made = [jax.vmap(work)(b, first + k * (span // len(pieces))) for k, b in enumerate(parts)]
    return in_order(jnp.concatenate(made, axis=out_dim + 1), out_dim)


def in_blocks(shard, dim, length):
    before, after = (shard.shape[:dim], shard.shape[dim + 1 :])
    return jnp.moveaxis(shard.reshape(*before, length, -1, *after), dim, 0)


def sum_at_owner(shard, axis, dim):
    parts = in_blocks(shard, dim, lax.axis_size(axis))
    arrived = lax.all_to_all(parts, axis, split_axis=0, concat_axis=0, tiled=True)
    return arrived.sum(axis=0)


def local(slabs, significant):
    aux_here, occupied, rows_here = slabs.shape
    blocks_here = rows_here // BS
    first_block = lax.axis_index("row") * blocks_here
    local_mask = lax.dynamic_slice_in_dim(significant, first_block, blocks_here, 1).astype(
        jnp.float32
    )
    block_of = lax.broadcasted_iota(jnp.int32, (blocks_here, rows_here), 1) // BS
    block_id = lax.broadcasted_iota(jnp.int32, (blocks_here, rows_here), 0)
    expand_table = (block_of == block_id).astype(jnp.float32)
    column_mask = jnp.dot(local_mask, expand_table).astype(jnp.bfloat16)
    masked = (slabs * column_mask[:, None, :]).reshape(aux_here * occupied, rows_here)

    def contract(column_piece, offset):
        return lax.dot_general(
            masked, column_piece, (((0,), (0,)), ((), ())), preferred_element_type=jnp.float32
        )

    partial_rows = piecewise(masked, "row", 1, contract, 1)
    return sum_at_owner(partial_rows, "aux", 1)


def solution(mesh):
    return jax.shard_map(
        local,
        mesh=mesh,
        in_specs=(P("aux", None, "row"), P("aux", None)),
        out_specs=P("row", "aux"),
        check_vma=False,
    )
```

profile of v0, /device:TPU:24, one launch (start us, length us, event | category | flops | bytes accessed | tf_op | source)
XLA Modules:
  0.0 166.9 jit_solution(14229258155580685952)
XLA Ops:
  6.5 0.0 all-gather.5.cloned.1.call-start
  6.6 0.9 convolution_convert_fusion
  7.4 1.2 broadcast_multiply_fusion
  8.6 0.3 fusion.9
  8.9 1.0 copy.7
  10.0 0.0 all-gather.5.cloned.1.call-update
  10.0 0.0 all-gather.7.cloned.1.call-start
  10.1 1.1 copy.8
  11.2 0.0 all-gather.7.cloned.1.call-update
  11.2 52.8 %all-gather.5.cloned.1.call-done = bf16[51200,64]{0,1:T(8,128)(2,1)} async-done(((bf16[3200,64]{0,1:T(8,128)(2,1)}), bf16[51200,64]{0,1:T(8,128)(2,1)}) %all-gather.5.cloned.1.call-update) | async-done | bytes 6553616 | tf_op jit(solution)/shard_map/all_gather | solution.py:19
  63.9 3.7 %copy.14 = bf16[8,16,8,3200]{3,2,0,1:T(8,128)(2,1)S(1)} copy(bf16[8,16,8,3200]{3,2,1,0:T(8,128)(2,1)} %bitcast.33) | data formatting | bytes 13107200 | tf_op jit(solution)/shard_map/all_gather | solution.py:19
  67.7 1.9 %fusion.10 = f32[128,1024]{0,1:S(1)} fusion(bf16[3200,1024]{0,1:T(8,128)(2,1)S(1)} %bitcast.36, bf16[3200,128]{1,0:T(8,128)(2,1)S(1)} %bitcast.31), kind=kOutput, calls=%fused_computation.20 | convolution fusion | flops 838860800 | bytes 7897088
  69.6 45.1 %all-gather.7.cloned.1.call-done = bf16[51200,64]{0,1:T(8,128)(2,1)} async-done(((bf16[3200,64]{0,1:T(8,128)(2,1)}), bf16[51200,64]{0,1:T(8,128)(2,1)}) %all-gather.7.cloned.1.call-update) | async-done | bytes 6553616 | tf_op jit(solution)/shard_map/all_gather | solution.py:19
  114.7 3.7 %copy.13 = bf16[8,16,8,3200]{3,2,0,1:T(8,128)(2,1)S(1)} copy(bf16[8,16,8,3200]{3,2,1,0:T(8,128)(2,1)} %bitcast.34) | data formatting | bytes 13107200 | tf_op jit(solution)/shard_map/all_gather | solution.py:19
  118.4 1.9 %fusion.11 = f32[128,1024]{0,1:S(1)} fusion(bf16[3200,1024]{0,1:T(8,128)(2,1)S(1)} %bitcast.35, bf16[3200,128]{1,0:T(8,128)(2,1)S(1)} %bitcast.32), kind=kOutput, calls=%fused_computation.21 | convolution fusion | flops 838860800 | bytes 7897088
  120.3 0.1 pad_maximum_fusion
  120.4 39.0 %all_to_all.5 = f32[32,128,64]{1,2,0:T(8,128)S(1)} all-to-all(f32[32,128,64]{1,2,0:T(8,128)S(1)} %bitcast.37), channel_id=1, replica_groups=mesh['aux'=32,'row'=16] {'aux'}, dimensions={0} | all-to-all | bytes 2097152 | tf_op jit(solution)/shard_map/all_to_all | solution.py:31
  159.4 0.7 reduce_sum.9
  (2 shorter events, 0.0 us)
Async XLA Ops:
  6.5 57.4 %all-gather.5.cloned.1.call-start = ((), (), s32[]{:S(2)}) async-start(), calls=%async_computation.1 | async-start | bytes 6963200 | tf_op jit(solution)/shard_map/all_gather | solution.py:19
  10.0 104.7 %all-gather.7.cloned.1.call-start = ((), (), s32[]{:S(2)}) async-start(), calls=%async_computation.2 | async-start | bytes 6963200 | tf_op jit(solution)/shard_map/all_gather | solution.py:19
Sparse Core Ops, SparseCore 0:
  10.1 53.7 all-gather.4
  66.0 48.6 all-gather.6
where the time goes:
time: 167 us
  waiting for transfers between devices  97.9 us (59%)
  blocking collectives  39 us (23%)
  between operations  13.4 us (8%)
  local copies, waits for them, and re-layouts  9.94 us (6%)
  matrix products  4.6 us (3%)
  other arithmetic  1.98 us (1%)
    all_gather x2, waiting for transfers between devices, piecewise(): parts = [lax.all_gather(slab, axis) for slab in pieces]  97.9 us
    all_to_all x1, blocking collectives, sum_at_owner(): lax.all_to_all(parts, axis, split_axis=0, concat_axis=0, tiled=True)  39 us
    all_gather x2, local copies, waits for them, and re-layouts, piecewise(): parts = [lax.all_gather(slab, axis) for slab in pieces]  7.49 us
    unnamed x2, matrix products  3.72 us
  transfers between devices with their start and end apart: 2, of which 2 were waited for; matrix products, arithmetic and copies ran while one was open for 4% of the time, Pallas kernels for 0%

commit v1 on v0

v1 whole, which is shorter than its diff:
```python
import jax
import jax.numpy as jnp
from jax import lax
from jax.sharding import PartitionSpec as P

BS = 64
AX, AZ = 4, 8
CHIPS = 8


def dev(aux, chip, core):
    return aux * 2 * CHIPS + (chip % CHIPS) * 2 + core


def block_at(core, step, row, col):
    return 2 + 4 * (step - 1) + 2 * (col != core) + (row != core)


def sources(X, j, Y, i):
    d = (X - Y) % CHIPS
    if d == 0:
        return ((i, 0), None) if i == j else ((i, 1), (j, 1))
    if d == CHIPS // 2:
        if i != j:
            return (i, 14), (j, 14)
        low = Y < CHIPS // 2
        return (i if low else 1 - i, 15), (1 - i if low else i, 15)
    s, up = (d, 1) if d < CHIPS // 2 else (CHIPS - d, 0)
    return (up, block_at(up, s, i, j)), (1 - up, block_at(1 - up, s, j, i))


def deliveries():
    direct = ([], [])
    mirrored = []
    for A in range(AX * AZ):
        X, j, h = A // 4, A // 2 % 2, A % 2
        for Y in range(CHIPS):
            for i in range(2):
                own, other = sources(X, j, Y, i)
                for p in range(2):
                    direct[p].append((dev(2 * own[1] + (h ^ p), Y, own[0]), dev(A, Y, i)))
                if other is not None:
                    mirrored.append((dev(2 * other[1] + h, X, other[0]), dev(A, Y, i)))
    return direct[0], direct[1], mirrored


def local(slabs, significant):
    aux_here, occupied, cols = slabs.shape
    half = aux_here // 2
    depth = half * occupied
    row = lax.axis_index("row")
    aux = lax.axis_index("aux")
    chip, core = row // 2, row % 2

    blocks = cols // BS
    mine = lax.dynamic_slice_in_dim(significant, row * blocks, blocks, 1)
    lane = lax.broadcasted_iota(jnp.int32, (aux_here, cols), 1) // BS
    keep = jnp.where(lane == 0, mine[:, :1], mine[:, 1:2]) != 0
    masked = jnp.where(keep[:, None, :], slabs, jnp.zeros_like(slabs))

    own = lax.dynamic_slice_in_dim(masked, core * half, half, 0).reshape(depth, cols)
    give = lax.dynamic_slice_in_dim(masked, (1 - core) * half, half, 0).reshape(depth, cols)
    swap = [(r, r ^ 1) for r in range(2 * CHIPS)]
    ring = [
        (2 * y + c, 2 * ((y + (1 if c == 0 else -1)) % CHIPS) + c)
        for y in range(CHIPS)
        for c in range(2)
    ]
    a, b = own, lax.ppermute(give, "row", swap)
    left = jnp.concatenate([own.T, b.T], axis=0)
    whole = masked.reshape(2 * depth, cols)

    def dot(x, y):
        return jnp.dot(x, y, preferred_element_type=jnp.float32)

    made = [dot(whole.T, whole), dot(own.T, b)]
    for step in range(1, CHIPS // 2 + 1):
        a = lax.ppermute(a, "row", ring)
        b = lax.ppermute(b, "row", ring)
        if step < CHIPS // 2:
            made += [dot(left, a), dot(left, b)]
        else:
            low = chip < CHIPS // 2
            made.append(dot(left[:cols], b))
            made.append(dot(jnp.where(low, left[:cols], left[cols:]), jnp.where(low, a, b)))
    pieces = jnp.concatenate(made, axis=0).reshape(AX, AZ, BS, cols)

    over_x = [[x * AZ + z for x in range(AX)] for z in range(AZ)]
    over_z = [[x * AZ + z for z in range(AZ)] for x in range(AX)]
    got = lax.all_to_all(pieces, "aux", 0, 0, axis_index_groups=over_x, tiled=True).sum(axis=0)
    got = lax.all_to_all(got, "aux", 0, 0, axis_index_groups=over_z, tiled=True).sum(axis=0)

    first, second, mirrored = deliveries()
    d0 = lax.ppermute(got, ("aux", "row"), first)
    d1 = lax.ppermute(got, ("aux", "row"), second)
    t = lax.ppermute(got, ("aux", "row"), mirrored)
    odd = aux % 2 == 1
    whole_rows = jnp.concatenate([jnp.where(odd, d1, d0), jnp.where(odd, d0, d1)], axis=0)
    direct = jnp.where(odd, whole_rows[:, BS:], whole_rows[:, :BS])
    return direct + t.T


def solution(mesh):
    return jax.shard_map(
        local,
        mesh=mesh,
        in_specs=(P("aux", None, "row"), P("aux", None)),
        out_specs=P("row", "aux"),
        check_vma=False,
    )
```

time: 167 us -> 115 us (0.69)
  the two profiles are of different devices: /device:TPU:24 before, /device:TPU:40 now
where the time goes in v1:
time: 115 us
  starting transfers between devices  43 us (37%)
  blocking collectives  34.9 us (30%)
  waiting for transfers between devices  29.2 us (25%)
  matrix products  4.05 us (4%)
  other arithmetic  2.1 us (2%)
    all_to_all x1, blocking collectives, local(): lax.all_to_all(got, 'aux', 0, 0, axis_index_groups=over_z, tiled=True)  19.9 us
    ppermute x4, starting transfers between devices, local(): b = lax.ppermute(b, 'row', ring)  15.4 us
    all_to_all x1, blocking collectives, local(): lax.all_to_all(pieces, 'aux', 0, 0, axis_index_groups=over_x, tiled=True)  15 us
    ppermute x1, waiting for transfers between devices, local(): t = lax.ppermute(got, ('aux', 'row'), mirrored)  13.9 us
    ppermute x4, starting transfers between devices, local(): a = lax.ppermute(a, 'row', ring)  13.3 us
    ppermute x1, starting transfers between devices, local(): d1 = lax.ppermute(got, ('aux', 'row'), second)  7.63 us
    ppermute x4, waiting for transfers between devices, local(): a = lax.ppermute(a, 'row', ring)  7.61 us
    ppermute x4, waiting for transfers between devices, local(): b = lax.ppermute(b, 'row', ring)  6.88 us
  transfers between devices with their start and end apart: 12, of which 8 were waited for; matrix products, arithmetic and copies ran while one was open for 3% of the time, Pallas kernels for 0%

profile of v1, /device:TPU:40, one launch (start us, length us, event | category | flops | bytes accessed | tf_op | source)
XLA Modules:
  0.0 114.5 jit_solution(2823050322434714685)
XLA Ops:
  0.0 0.7 copy-done
  1.0 1.2 %broadcast_select_fusion = bf16[8,400,128]{2,1,0:T(8,128)(2,1)S(1)} fusion(bf16[8,400,128]{2,1,0:T(8,128)(2,1)} %param.2, pred[8,128]{1,0:T(8,128)(4,1)S(1)} %select_compare_fusion), kind=kLoop, calls=%fused_computation.12 | loop fusion | flops 409600 | bytes 1639424 | tf_op jit(solution)/shard_map/jit(_where)/select_n | solution.py:59
  2.3 1.9 %collective-permute-start = (bf16[1600,128]{1,0:T(8,128)(2,1)S(1)}, bf16[1600,128]{1,0:T(8,128)(2,1)S(1)}, u32[]{:S(2)}, u32[]{:S(2)}) collective-permute-start(bf16[1600,128]{1,0:T(8,128)(2,1)S(1)} %bitcast.45), channel_id=1, source_target_pairs={{0,1},{1,0},{2,3},{3,2},{4,5},{5,4},{6,7},{7,6},{8,9},{9,8},{10,11... | collective-permute-start | bytes 1228808 | tf_op jit(solution)/shard_map/ppermute | solution.py:69
  4.2 2.6 %collective-permute-start.1 = (bf16[1600,128]{1,0:T(8,128)(2,1)S(1)}, bf16[1600,128]{1,0:T(8,128)(2,1)S(1)}, u32[]{:S(2)}, u32[]{:S(2)}) collective-permute-start(bf16[1600,128]{1,0:T(8,128)(2,1)S(1)} %bitcast.28), channel_id=1, source_target_pairs={{0,2},{1,15},{2,4},{3,1},{4,6},{5,3},{6,8},{7,5},{8,10},{9,7},{10,... | collective-permute-start | bytes 1228808 | tf_op jit(solution)/shard_map/ppermute | solution.py:78
  6.9 2.6 %collective-permute-start.2 = (bf16[1600,128]{1,0:T(8,128)(2,1)S(1)}, bf16[1600,128]{1,0:T(8,128)(2,1)S(1)}, u32[]{:S(2)}, u32[]{:S(2)}) collective-permute-start(bf16[1600,128]{1,0:T(8,128)(2,1)S(1)} %collective-permute-done), channel_id=1, source_target_pairs={{0,2},{1,15},{2,4},{3,1},{4,6},{5,3},{6,8},{7,5},{8,10},{9,7},{10,... | collective-permute-start | bytes 1228808 | tf_op jit(solution)/shard_map/ppermute | solution.py:79
  9.9 4.2 %collective-permute-done.1 = bf16[1600,128]{1,0:T(8,128)(2,1)S(1)} collective-permute-done((bf16[1600,128]{1,0:T(8,128)(2,1)S(1)}, bf16[1600,128]{1,0:T(8,128)(2,1)S(1)}, u32[]{:S(2)}, u32[]{:S(2)}) %collective-permute-start.1) | collective-permute-done | bytes 409632 | tf_op jit(solution)/shard_map/ppermute | solution.py:78
  14.1 2.8 %collective-permute-start.3 = (bf16[1600,128]{1,0:T(8,128)(2,1)S(1)}, bf16[1600,128]{1,0:T(8,128)(2,1)S(1)}, u32[]{:S(2)}, u32[]{:S(2)}) collective-permute-start(bf16[1600,128]{1,0:T(8,128)(2,1)S(1)} %collective-permute-done.1), channel_id=1, source_target_pairs={{0,2},{1,15},{2,4},{3,1},{4,6},{5,3},{6,8},{7,5},{8,10},{9,7},{10,... | collective-permute-start | bytes 1228808 | tf_op jit(solution)/shard_map/ppermute | solution.py:78
  17.3 1.2 %collective-permute-done.2 = bf16[1600,128]{1,0:T(8,128)(2,1)S(1)} collective-permute-done((bf16[1600,128]{1,0:T(8,128)(2,1)S(1)}, bf16[1600,128]{1,0:T(8,128)(2,1)S(1)}, u32[]{:S(2)}, u32[]{:S(2)}) %collective-permute-start.2) | collective-permute-done | bytes 409632 | tf_op jit(solution)/shard_map/ppermute | solution.py:79
  18.5 3.8 %collective-permute-start.4 = (bf16[1600,128]{1,0:T(8,128)(2,1)S(1)}, bf16[1600,128]{1,0:T(8,128)(2,1)S(1)}, u32[]{:S(2)}, u32[]{:S(2)}) collective-permute-start(bf16[1600,128]{1,0:T(8,128)(2,1)S(1)} %collective-permute-done.2), channel_id=1, source_target_pairs={{0,2},{1,15},{2,4},{3,1},{4,6},{5,3},{6,8},{7,5},{8,10},{9,7},{10,... | collective-permute-start | bytes 1228808 | tf_op jit(solution)/shard_map/ppermute | solution.py:79
  22.7 1.8 %collective-permute-done.3 = bf16[1600,128]{1,0:T(8,128)(2,1)S(1)} collective-permute-done((bf16[1600,128]{1,0:T(8,128)(2,1)S(1)}, bf16[1600,128]{1,0:T(8,128)(2,1)S(1)}, u32[]{:S(2)}, u32[]{:S(2)}) %collective-permute-start.3) | collective-permute-done | bytes 409632 | tf_op jit(solution)/shard_map/ppermute | solution.py:78
  24.5 3.8 %collective-permute-start.5 = (bf16[1600,128]{1,0:T(8,128)(2,1)S(1)}, bf16[1600,128]{1,0:T(8,128)(2,1)S(1)}, u32[]{:S(2)}, u32[]{:S(2)}) collective-permute-start(bf16[1600,128]{1,0:T(8,128)(2,1)S(1)} %collective-permute-done.3), channel_id=1, source_target_pairs={{0,2},{1,15},{2,4},{3,1},{4,6},{5,3},{6,8},{7,5},{8,10},{9,7},{10,... | collective-permute-start | bytes 1228808 | tf_op jit(solution)/shard_map/ppermute | solution.py:78
  28.8 4.6 %collective-permute-start.6 = (bf16[1600,128]{1,0:T(8,128)(2,1)S(1)}, bf16[1600,128]{1,0:T(8,128)(2,1)S(1)}, u32[]{:S(2)}, u32[]{:S(2)}) collective-permute-start(bf16[1600,128]{1,0:T(8,128)(2,1)S(1)} %collective-permute-done.4), channel_id=1, source_target_pairs={{0,2},{1,15},{2,4},{3,1},{4,6},{5,3},{6,8},{7,5},{8,10},{9,7},{10,... | collective-permute-start | bytes 1228808 | tf_op jit(solution)/shard_map/ppermute | solution.py:79
  33.9 1.6 %collective-permute-done.5 = bf16[1600,128]{1,0:T(8,128)(2,1)S(1)} collective-permute-done((bf16[1600,128]{1,0:T(8,128)(2,1)S(1)}, bf16[1600,128]{1,0:T(8,128)(2,1)S(1)}, u32[]{:S(2)}, u32[]{:S(2)}) %collective-permute-start.5) | collective-permute-done | bytes 409632 | tf_op jit(solution)/shard_map/ppermute | solution.py:78
  35.5 4.0 %collective-permute-start.8 = (bf16[1600,128]{1,0:T(8,128)(2,1)S(1)}, bf16[1600,128]{1,0:T(8,128)(2,1)S(1)}, u32[]{:S(2)}, u32[]{:S(2)}) collective-permute-start(bf16[1600,128]{1,0:T(8,128)(2,1)S(1)} %collective-permute-done.5), channel_id=1, source_target_pairs={{0,2},{1,15},{2,4},{3,1},{4,6},{5,3},{6,8},{7,5},{8,10},{9,7},{10,... | collective-permute-start | bytes 1228808 | tf_op jit(solution)/shard_map/ppermute | solution.py:78
  39.9 4.5 %collective-permute-start.7 = (bf16[1600,128]{1,0:T(8,128)(2,1)S(1)}, bf16[1600,128]{1,0:T(8,128)(2,1)S(1)}, u32[]{:S(2)}, u32[]{:S(2)}) collective-permute-start(bf16[1600,128]{1,0:T(8,128)(2,1)S(1)} %collective-permute-done.6), channel_id=1, source_target_pairs={{0,2},{1,15},{2,4},{3,1},{4,6},{5,3},{6,8},{7,5},{8,10},{9,7},{10,... | collective-permute-start | bytes 1228808 | tf_op jit(solution)/shard_map/ppermute | solution.py:79
  45.4 5.6 %collective-permute-done.7 = bf16[1600,128]{1,0:T(8,128)(2,1)S(1)} collective-permute-done((bf16[1600,128]{1,0:T(8,128)(2,1)S(1)}, bf16[1600,128]{1,0:T(8,128)(2,1)S(1)}, u32[]{:S(2)}, u32[]{:S(2)}) %collective-permute-start.7) | collective-permute-done | bytes 409632 | tf_op jit(solution)/shard_map/ppermute | solution.py:79
  51.6 15.0 %all_to_all.10 = f32[4,8,64,128]{3,2,1,0:T(8,128)S(1)} all-to-all(f32[4,8,64,128]{3,2,1,0:T(8,128)S(1)} %bitcast.38), channel_id=1, replica_groups={{0,128,256,384},{16,144,272,400},{32,160,288,416},{48,176,304,432},{64,..., dimensions={0} | all-to-all | bytes 2097152 | tf_op jit(solution)/shard_map/all_to_all | solution.py:90
  66.7 19.9 %all_to_all.11 = f32[8,64,128]{2,1,0:T(8,128)S(1)} all-to-all(f32[8,64,128]{2,1,0:T(8,128)S(1)} %reduce_sum.18), channel_id=1, replica_groups={{0,16,32,48,64,80,96,112},{128,144,160,176,192,208,224,240},{256,272,28..., dimensions={0} | all-to-all | bytes 524288 | tf_op jit(solution)/shard_map/all_to_all | solution.py:91
  86.7 3.4 %collective-permute-start.10 = (f32[64,128]{0,1:T(8,128)S(1)}, f32[64,128]{0,1:T(8,128)S(1)}, u32[]{:S(2)}, u32[]{:S(2)}) collective-permute-start(f32[64,128]{0,1:T(8,128)S(1)} %copy.4), channel_id=1, source_target_pairs={{0,0},{33,1},{66,2},{98,3},{196,4},{228,5},{326,6},{358,7},{489,8}... | collective-permute-start | bytes 98312 | tf_op jit(solution)/shard_map/ppermute | solution.py:94
  90.1 7.6 %collective-permute-start.9 = (f32[64,128]{0,1:T(8,128)S(1)}, f32[64,128]{0,1:T(8,128)S(1)}, u32[]{:S(2)}, u32[]{:S(2)}) collective-permute-start(f32[64,128]{0,1:T(8,128)S(1)} %copy.4), channel_id=1, source_target_pairs={{16,0},{49,1},{82,2},{114,3},{212,4},{244,5},{342,6},{374,7},{505,... | collective-permute-start | bytes 98312 | tf_op jit(solution)/shard_map/ppermute | solution.py:95
  97.8 1.3 %collective-permute-start.11 = (f32[64,128]{1,0:T(8,128)S(1)}, f32[64,128]{1,0:T(8,128)S(1)}, u32[]{:S(2)}, u32[]{:S(2)}) collective-permute-start(f32[64,128]{1,0:T(8,128)S(1)} %reduce_sum.19), channel_id=1, source_target_pairs={{32,1},{161,2},{97,3},{289,4},{225,5},{417,6},{353,7},{480,8},{448... | collective-permute-start | bytes 98312 | tf_op jit(solution)/shard_map/ppermute | solution.py:96
  99.1 0.8 collective-permute-done.9
  99.9 13.9 %collective-permute-done.11 = f32[64,128]{1,0:T(8,128)S(1)} collective-permute-done((f32[64,128]{1,0:T(8,128)S(1)}, f32[64,128]{1,0:T(8,128)S(1)}, u32[]{:S(2)}, u32[]{:S(2)}) %collective-permute-start.11) | collective-permute-done | bytes 32800 | tf_op jit(solution)/shard_map/ppermute | solution.py:96
  113.8 0.7 fusion.7
  (26 shorter events, 4.7 us)
Async XLA Ops:
  0.0 0.7 copy-start
  2.3 4.5 %collective-permute-start = (bf16[1600,128]{1,0:T(8,128)(2,1)S(1)}, bf16[1600,128]{1,0:T(8,128)(2,1)S(1)}, u32[]{:S(2)}, u32[]{:S(2)}) collective-permute-start(bf16[1600,128]{1,0:T(8,128)(2,1)S(1)} %bitcast.45), channel_id=1, source_target_pairs={{0,1},{1,0},{2,3},{3,2},{4,5},{5,4},{6,7},{7,6},{8,9},{9,8},{10,11... | collective-permute-start | bytes 1228808 | tf_op jit(solution)/shard_map/ppermute | solution.py:69
  4.2 9.8 %collective-permute-start.1 = (bf16[1600,128]{1,0:T(8,128)(2,1)S(1)}, bf16[1600,128]{1,0:T(8,128)(2,1)S(1)}, u32[]{:S(2)}, u32[]{:S(2)}) collective-permute-start(bf16[1600,128]{1,0:T(8,128)(2,1)S(1)} %bitcast.28), channel_id=1, source_target_pairs={{0,2},{1,15},{2,4},{3,1},{4,6},{5,3},{6,8},{7,5},{8,10},{9,7},{10,... | collective-permute-start | bytes 1228808 | tf_op jit(solution)/shard_map/ppermute | solution.py:78
  6.9 11.6 %collective-permute-start.2 = (bf16[1600,128]{1,0:T(8,128)(2,1)S(1)}, bf16[1600,128]{1,0:T(8,128)(2,1)S(1)}, u32[]{:S(2)}, u32[]{:S(2)}) collective-permute-start(bf16[1600,128]{1,0:T(8,128)(2,1)S(1)} %collective-permute-done), channel_id=1, source_target_pairs={{0,2},{1,15},{2,4},{3,1},{4,6},{5,3},{6,8},{7,5},{8,10},{9,7},{10,... | collective-permute-start | bytes 1228808 | tf_op jit(solution)/shard_map/ppermute | solution.py:79
  14.1 10.4 %collective-permute-start.3 = (bf16[1600,128]{1,0:T(8,128)(2,1)S(1)}, bf16[1600,128]{1,0:T(8,128)(2,1)S(1)}, u32[]{:S(2)}, u32[]{:S(2)}) collective-permute-start(bf16[1600,128]{1,0:T(8,128)(2,1)S(1)} %collective-permute-done.1), channel_id=1, source_target_pairs={{0,2},{1,15},{2,4},{3,1},{4,6},{5,3},{6,8},{7,5},{8,10},{9,7},{10,... | collective-permute-start | bytes 1228808 | tf_op jit(solution)/shard_map/ppermute | solution.py:78
  18.5 10.4 %collective-permute-start.4 = (bf16[1600,128]{1,0:T(8,128)(2,1)S(1)}, bf16[1600,128]{1,0:T(8,128)(2,1)S(1)}, u32[]{:S(2)}, u32[]{:S(2)}) collective-permute-start(bf16[1600,128]{1,0:T(8,128)(2,1)S(1)} %collective-permute-done.2), channel_id=1, source_target_pairs={{0,2},{1,15},{2,4},{3,1},{4,6},{5,3},{6,8},{7,5},{8,10},{9,7},{10,... | collective-permute-start | bytes 1228808 | tf_op jit(solution)/shard_map/ppermute | solution.py:79
  24.5 11.0 %collective-permute-start.5 = (bf16[1600,128]{1,0:T(8,128)(2,1)S(1)}, bf16[1600,128]{1,0:T(8,128)(2,1)S(1)}, u32[]{:S(2)}, u32[]{:S(2)}) collective-permute-start(bf16[1600,128]{1,0:T(8,128)(2,1)S(1)} %collective-permute-done.3), channel_id=1, source_target_pairs={{0,2},{1,15},{2,4},{3,1},{4,6},{5,3},{6,8},{7,5},{8,10},{9,7},{10,... | collective-permute-start | bytes 1228808 | tf_op jit(solution)/shard_map/ppermute | solution.py:78
  28.8 11.1 %collective-permute-start.6 = (bf16[1600,128]{1,0:T(8,128)(2,1)S(1)}, bf16[1600,128]{1,0:T(8,128)(2,1)S(1)}, u32[]{:S(2)}, u32[]{:S(2)}) collective-permute-start(bf16[1600,128]{1,0:T(8,128)(2,1)S(1)} %collective-permute-done.4), channel_id=1, source_target_pairs={{0,2},{1,15},{2,4},{3,1},{4,6},{5,3},{6,8},{7,5},{8,10},{9,7},{10,... | collective-permute-start | bytes 1228808 | tf_op jit(solution)/shard_map/ppermute | solution.py:79
  35.5 15.8 %collective-permute-start.8 = (bf16[1600,128]{1,0:T(8,128)(2,1)S(1)}, bf16[1600,128]{1,0:T(8,128)(2,1)S(1)}, u32[]{:S(2)}, u32[]{:S(2)}) collective-permute-start(bf16[1600,128]{1,0:T(8,128)(2,1)S(1)} %collective-permute-done.5), channel_id=1, source_target_pairs={{0,2},{1,15},{2,4},{3,1},{4,6},{5,3},{6,8},{7,5},{8,10},{9,7},{10,... | collective-permute-start | bytes 1228808 | tf_op jit(solution)/shard_map/ppermute | solution.py:78
  39.9 11.0 %collective-permute-start.7 = (bf16[1600,128]{1,0:T(8,128)(2,1)S(1)}, bf16[1600,128]{1,0:T(8,128)(2,1)S(1)}, u32[]{:S(2)}, u32[]{:S(2)}) collective-permute-start(bf16[1600,128]{1,0:T(8,128)(2,1)S(1)} %collective-permute-done.6), channel_id=1, source_target_pairs={{0,2},{1,15},{2,4},{3,1},{4,6},{5,3},{6,8},{7,5},{8,10},{9,7},{10,... | collective-permute-start | bytes 1228808 | tf_op jit(solution)/shard_map/ppermute | solution.py:79
  86.7 12.4 %collective-permute-start.10 = (f32[64,128]{0,1:T(8,128)S(1)}, f32[64,128]{0,1:T(8,128)S(1)}, u32[]{:S(2)}, u32[]{:S(2)}) collective-permute-start(f32[64,128]{0,1:T(8,128)S(1)} %copy.4), channel_id=1, source_target_pairs={{0,0},{33,1},{66,2},{98,3},{196,4},{228,5},{326,6},{358,7},{489,8}... | collective-permute-start | bytes 98312 | tf_op jit(solution)/shard_map/ppermute | solution.py:94
  90.1 9.8 %collective-permute-start.9 = (f32[64,128]{0,1:T(8,128)S(1)}, f32[64,128]{0,1:T(8,128)S(1)}, u32[]{:S(2)}, u32[]{:S(2)}) collective-permute-start(f32[64,128]{0,1:T(8,128)S(1)} %copy.4), channel_id=1, source_target_pairs={{16,0},{49,1},{82,2},{114,3},{212,4},{244,5},{342,6},{374,7},{505,... | collective-permute-start | bytes 98312 | tf_op jit(solution)/shard_map/ppermute | solution.py:95
  97.8 16.0 %collective-permute-start.11 = (f32[64,128]{1,0:T(8,128)S(1)}, f32[64,128]{1,0:T(8,128)S(1)}, u32[]{:S(2)}, u32[]{:S(2)}) collective-permute-start(f32[64,128]{1,0:T(8,128)S(1)} %reduce_sum.19), channel_id=1, source_target_pairs={{32,1},{161,2},{97,3},{289,4},{225,5},{417,6},{353,7},{480,8},{448... | collective-permute-start | bytes 98312 | tf_op jit(solution)/shard_map/ppermute | solution.py:96

commit v2 on v1

--- a/solution.py
+++ b/solution.py
@@ -29,6 +29,19 @@
     return (up, block_at(up, s, i, j)), (1 - up, block_at(1 - up, s, j, i))
 
 
+PARTS = (10, 4, 2)
+
+
+def holder(place, g):
+    first, z = 0, 0
+    for count in PARTS:
+        each = 2 * count // AX
+        if place < first + count:
+            x, k = divmod(2 * (place - first) + g, each)
+            return x * AZ + z + k
+        first, z = first + count, z + each
+
+
 def deliveries():
     direct = ([], [])
     mirrored = []
@@ -38,9 +51,9 @@
             for i in range(2):
                 own, other = sources(X, j, Y, i)
                 for p in range(2):
-                    direct[p].append((dev(2 * own[1] + (h ^ p), Y, own[0]), dev(A, Y, i)))
+                    direct[p].append((dev(holder(own[1], h ^ p), Y, own[0]), dev(A, Y, i)))
                 if other is not None:
-                    mirrored.append((dev(2 * other[1] + h, X, other[0]), dev(A, Y, i)))
+                    mirrored.append((dev(holder(other[1], h), X, other[0]), dev(A, Y, i)))
     return direct[0], direct[1], mirrored
 
 
@@ -73,21 +86,29 @@
     def dot(x, y):
         return jnp.dot(x, y, preferred_element_type=jnp.float32)
 
+    over_x = [[x * AZ + z for x in range(AX)] for z in range(AZ)]
+
+    def sum_over_x(blocks):
+        parts = jnp.concatenate(blocks, axis=0).reshape(AX, -1, BS, cols)
+        return lax.all_to_all(parts, "aux", 0, 0, axis_index_groups=over_x, tiled=True).sum(axis=0)
+
     made = [dot(whole.T, whole), dot(own.T, b)]
-    for step in range(1, CHIPS // 2 + 1):
-        a = lax.ppermute(a, "row", ring)
-        b = lax.ppermute(b, "row", ring)
-        if step < CHIPS // 2:
-            made += [dot(left, a), dot(left, b)]
-        else:
-            low = chip < CHIPS // 2
-            made.append(dot(left[:cols], b))
-            made.append(dot(jnp.where(low, left[:cols], left[cols:]), jnp.where(low, a, b)))
-    pieces = jnp.concatenate(made, axis=0).reshape(AX, AZ, BS, cols)
+    for _ in range(2):
+        a, b = lax.ppermute(a, "row", ring), lax.ppermute(b, "row", ring)
+        made += [dot(left, a), dot(left, b)]
+    sums = [sum_over_x(made)]
+    a, b = lax.ppermute(a, "row", ring), lax.ppermute(b, "row", ring)
+    a, b, sums[0] = lax.optimization_barrier((a, b, sums[0]))
+    made = [dot(left, a), dot(left, b)]
+    a, b = lax.ppermute(a, "row", ring), lax.ppermute(b, "row", ring)
+    sums.append(sum_over_x(made))
+    a, b, sums[1] = lax.optimization_barrier((a, b, sums[1]))
+    low = chip < CHIPS // 2
+    near = jnp.where(low, left[:cols], left[cols:])
+    sums.append(sum_over_x([dot(left[:cols], b), dot(near, jnp.where(low, a, b))]))
 
-    over_x = [[x * AZ + z for x in range(AX)] for z in range(AZ)]
     over_z = [[x * AZ + z for z in range(AZ)] for x in range(AX)]
-    got = lax.all_to_all(pieces, "aux", 0, 0, axis_index_groups=over_x, tiled=True).sum(axis=0)
+    got = jnp.concatenate(sums, axis=0)
     got = lax.all_to_all(got, "aux", 0, 0, axis_index_groups=over_z, tiled=True).sum(axis=0)
 
     first, second, mirrored = deliveries()

time: 115 us -> 126 us (1.096)
  the two profiles are of different devices: /device:TPU:40 before, /device:TPU:158 now
where the time goes in v2:
time: 126 us; the launch traced here: 125 us
  starting transfers between devices  54.5 us (43%)
  waiting for transfers between devices  33.6 us (27%)
  blocking collectives  24.9 us (20%)
  matrix products  7.85 us (6%)
  other arithmetic  2.83 us (2%)
    ppermute x8, starting transfers between devices, local(): a, b = (lax.ppermute(a, 'row', ring), lax.ppermute(b, 'row', ring))  27.4 us
    all_to_all x1, blocking collectives, local(): lax.all_to_all(got, 'aux', 0, 0, axis_index_groups=over_z, tiled=True)  16.6 us
    ppermute x8, waiting for transfers between devices, local(): a, b = (lax.ppermute(a, 'row', ring), lax.ppermute(b, 'row', ring))  14.6 us
    ppermute x1, waiting for transfers between devices, local(): t = lax.ppermute(got, ('aux', 'row'), mirrored)  11.7 us
    all_to_all x2, starting transfers between devices, sum_over_x(): lax.all_to_all(parts, 'aux', 0, 0, axis_index_groups=over_x, tiled=True)  9.57 us
    ppermute x1, starting transfers between devices, local(): d1 = lax.ppermute(got, ('aux', 'row'), second)  8.77 us
    all_to_all x1, blocking collectives, sum_over_x(): lax.all_to_all(parts, 'aux', 0, 0, axis_index_groups=over_x, tiled=True)  8.33 us
    dot_general x10, matrix products, dot(): return jnp.dot(x, y, preferred_element_type=jnp.float32)  7.85 us
  transfers between devices with their start and end apart: 14, of which 8 were waited for; matrix products, arithmetic and copies ran while one was open for 5% of the time, Pallas kernels for 0%

profile of v2, /device:TPU:158, one launch (start us, length us, event | category | flops | bytes accessed | tf_op | source)
XLA Modules:
  0.0 125.0 jit_solution(9244765150343399883)
XLA Ops:
  2.3 1.9 %collective-permute-start.3 = (bf16[1600,128]{1,0:T(8,128)(2,1)S(1)}, bf16[1600,128]{1,0:T(8,128)(2,1)S(1)}, u32[]{:S(2)}, u32[]{:S(2)}) collective-permute-start(bf16[1600,128]{1,0:T(8,128)(2,1)S(1)} %bitcast.50), channel_id=1, source_target_pairs={{0,1},{1,0},{2,3},{3,2},{4,5},{5,4},{6,7},{7,6},{8,9},{9,8},{10,11... | collective-permute-start | bytes 1228808 | tf_op jit(solution)/shard_map/ppermute | solution.py:82
  4.2 4.7 %collective-permute-start = (bf16[1600,128]{1,0:T(8,128)(2,1)S(1)}, bf16[1600,128]{1,0:T(8,128)(2,1)S(1)}, u32[]{:S(2)}, u32[]{:S(2)}) collective-permute-start(bf16[1600,128]{1,0:T(8,128)(2,1)S(1)} %bitcast.33), channel_id=1, source_target_pairs={{0,2},{1,15},{2,4},{3,1},{4,6},{5,3},{6,8},{7,5},{8,10},{9,7},{10,... | collective-permute-start | bytes 1228808 | tf_op jit(solution)/shard_map/ppermute | solution.py:97
  10.0 2.6 %collective-permute-start.4 = (bf16[1600,128]{1,0:T(8,128)(2,1)S(1)}, bf16[1600,128]{1,0:T(8,128)(2,1)S(1)}, u32[]{:S(2)}, u32[]{:S(2)}) collective-permute-start(bf16[1600,128]{1,0:T(8,128)(2,1)S(1)} %collective-permute-done.3), channel_id=1, source_target_pairs={{0,2},{1,15},{2,4},{3,1},{4,6},{5,3},{6,8},{7,5},{8,10},{9,7},{10,... | collective-permute-start | bytes 1228808 | tf_op jit(solution)/shard_map/ppermute | solution.py:97
  12.6 1.8 %collective-permute-done = bf16[1600,128]{1,0:T(8,128)(2,1)S(1)} collective-permute-done((bf16[1600,128]{1,0:T(8,128)(2,1)S(1)}, bf16[1600,128]{1,0:T(8,128)(2,1)S(1)}, u32[]{:S(2)}, u32[]{:S(2)}) %collective-permute-start) | collective-permute-done | bytes 409632 | tf_op jit(solution)/shard_map/ppermute | solution.py:97
  14.4 5.6 %collective-permute-start.1 = (bf16[1600,128]{1,0:T(8,128)(2,1)S(1)}, bf16[1600,128]{1,0:T(8,128)(2,1)S(1)}, u32[]{:S(2)}, u32[]{:S(2)}) collective-permute-start(bf16[1600,128]{1,0:T(8,128)(2,1)S(1)} %collective-permute-done), channel_id=1, source_target_pairs={{0,2},{1,15},{2,4},{3,1},{4,6},{5,3},{6,8},{7,5},{8,10},{9,7},{10,... | collective-permute-start | bytes 1228808 | tf_op jit(solution)/shard_map/ppermute | solution.py:97
  22.0 2.4 %collective-permute-start.5 = (bf16[1600,128]{1,0:T(8,128)(2,1)S(1)}, bf16[1600,128]{1,0:T(8,128)(2,1)S(1)}, u32[]{:S(2)}, u32[]{:S(2)}) collective-permute-start(bf16[1600,128]{1,0:T(8,128)(2,1)S(1)} %collective-permute-done.4), channel_id=1, source_target_pairs={{0,2},{1,15},{2,4},{3,1},{4,6},{5,3},{6,8},{7,5},{8,10},{9,7},{10,... | collective-permute-start | bytes 1228808 | tf_op jit(solution)/shard_map/ppermute | solution.py:97
  26.6 5.3 %collective-permute-done.5 = bf16[1600,128]{1,0:T(8,128)(2,1)S(1)} collective-permute-done((bf16[1600,128]{1,0:T(8,128)(2,1)S(1)}, bf16[1600,128]{1,0:T(8,128)(2,1)S(1)}, u32[]{:S(2)}, u32[]{:S(2)}) %collective-permute-start.5) | collective-permute-done | bytes 409632 | tf_op jit(solution)/shard_map/ppermute | solution.py:97
  32.9 4.8 %all-to-all-start = ((f32[4,5,64,128]{3,2,1,0:T(8,128)}), f32[4,5,64,128]{3,2,1,0:T(8,128)S(1)}, u32[]{:S(2)}, u32[]{:S(2)}) async-start(f32[4,5,64,128]{3,2,1,0:T(8,128)} %bitcast.5), calls=%async_computation | async-start | bytes 1310720 | tf_op jit(solution)/shard_map/all_to_all | solution.py:93
  37.7 3.6 %collective-permute-start.2 = (bf16[1600,128]{1,0:T(8,128)(2,1)S(1)}, bf16[1600,128]{1,0:T(8,128)(2,1)S(1)}, u32[]{:S(2)}, u32[]{:S(2)}) collective-permute-start(bf16[1600,128]{1,0:T(8,128)(2,1)S(1)} %collective-permute-done.1), channel_id=1, source_target_pairs={{0,2},{1,15},{2,4},{3,1},{4,6},{5,3},{6,8},{7,5},{8,10},{9,7},{10,... | collective-permute-start | bytes 1228808 | tf_op jit(solution)/shard_map/ppermute | solution.py:100
  41.3 1.9 %collective-permute-start.6 = (bf16[1600,128]{1,0:T(8,128)(2,1)S(1)}, bf16[1600,128]{1,0:T(8,128)(2,1)S(1)}, u32[]{:S(2)}, u32[]{:S(2)}) collective-permute-start(bf16[1600,128]{1,0:T(8,128)(2,1)S(1)} %collective-permute-done.5), channel_id=1, source_target_pairs={{0,2},{1,15},{2,4},{3,1},{4,6},{5,3},{6,8},{7,5},{8,10},{9,7},{10,... | collective-permute-start | bytes 1228808 | tf_op jit(solution)/shard_map/ppermute | solution.py:100
  43.2 1.2 all-to-all-done
  44.4 3.1 %collective-permute-done.2 = bf16[1600,128]{1,0:T(8,128)(2,1)S(1)} collective-permute-done((bf16[1600,128]{1,0:T(8,128)(2,1)S(1)}, bf16[1600,128]{1,0:T(8,128)(2,1)S(1)}, u32[]{:S(2)}, u32[]{:S(2)}) %collective-permute-start.2) | collective-permute-done | bytes 409632 | tf_op jit(solution)/shard_map/ppermute | solution.py:100
  47.5 4.4 %collective-permute-done.6 = bf16[1600,128]{1,0:T(8,128)(2,1)S(1)} collective-permute-done((bf16[1600,128]{1,0:T(8,128)(2,1)S(1)}, bf16[1600,128]{1,0:T(8,128)(2,1)S(1)}, u32[]{:S(2)}, u32[]{:S(2)}) %collective-permute-start.6) | collective-permute-done | bytes 409632 | tf_op jit(solution)/shard_map/ppermute | solution.py:100
  52.4 4.8 %collective-permute-start.7 = (bf16[1600,128]{1,0:T(8,128)(2,1)S(1)}, bf16[1600,128]{1,0:T(8,128)(2,1)S(1)}, u32[]{:S(2)}, u32[]{:S(2)}) collective-permute-start(bf16[1600,128]{1,0:T(8,128)(2,1)S(1)} %collective-permute-done.2), channel_id=1, source_target_pairs={{0,2},{1,15},{2,4},{3,1},{4,6},{5,3},{6,8},{7,5},{8,10},{9,7},{10,... | collective-permute-start | bytes 1228808 | tf_op jit(solution)/shard_map/ppermute | solution.py:103
  57.2 1.9 %collective-permute-start.8 = (bf16[1600,128]{1,0:T(8,128)(2,1)S(1)}, bf16[1600,128]{1,0:T(8,128)(2,1)S(1)}, u32[]{:S(2)}, u32[]{:S(2)}) collective-permute-start(bf16[1600,128]{1,0:T(8,128)(2,1)S(1)} %collective-permute-done.6), channel_id=1, source_target_pairs={{0,2},{1,15},{2,4},{3,1},{4,6},{5,3},{6,8},{7,5},{8,10},{9,7},{10,... | collective-permute-start | bytes 1228808 | tf_op jit(solution)/shard_map/ppermute | solution.py:103
  60.2 4.8 %all-to-all-start.1 = ((f32[4,2,64,128]{3,2,1,0:T(8,128)}), f32[4,2,64,128]{3,2,1,0:T(8,128)S(1)}, u32[]{:S(2)}, u32[]{:S(2)}) async-start(f32[4,2,64,128]{3,2,1,0:T(8,128)} %bitcast.6), calls=%async_computation.1 | async-start | bytes 524288 | tf_op jit(solution)/shard_map/all_to_all | solution.py:93
  65.0 4.6 %all-to-all-done.1 = f32[4,2,64,128]{3,2,1,0:T(8,128)S(1)} async-done(((f32[4,2,64,128]{3,2,1,0:T(8,128)}), f32[4,2,64,128]{3,2,1,0:T(8,128)S(1)}, u32[]{:S(2)}, u32[]{:S(2)}) %all-to-all-start.1) | async-done | bytes 262176 | tf_op jit(solution)/shard_map/all_to_all | solution.py:93
  70.4 8.3 %all_to_all.20 = f32[4,1,64,128]{3,2,1,0:T(8,128)S(1)} all-to-all(f32[4,1,64,128]{3,2,1,0:T(8,128)S(1)} %bitcast.43), channel_id=1, replica_groups={{0,128,256,384},{16,144,272,400},{32,160,288,416},{48,176,304,432},{64,..., dimensions={0} | all-to-all | bytes 262144 | tf_op jit(solution)/shard_map/all_to_all | solution.py:93
  78.8 16.6 %all_to_all.21 = f32[8,64,128]{2,1,0:T(8,128)S(1)} all-to-all(f32[8,64,128]{2,1,0:T(8,128)S(1)} %pad_maximum_fusion.2), channel_id=1, replica_groups={{0,16,32,48,64,80,96,112},{128,144,160,176,192,208,224,240},{256,272,28..., dimensions={0} | all-to-all | bytes 524288 | tf_op jit(solution)/shard_map/all_to_all | solution.py:112
  95.5 4.9 %collective-permute-start.10 = (f32[64,128]{0,1:T(8,128)S(1)}, f32[64,128]{0,1:T(8,128)S(1)}, u32[]{:S(2)}, u32[]{:S(2)}) collective-permute-start(f32[64,128]{0,1:T(8,128)S(1)} %copy.7), channel_id=1, source_target_pairs={{0,0},{33,1},{66,2},{146,3},{292,4},{324,5},{86,6},{214,7},{377,8}... | collective-permute-start | bytes 98312 | tf_op jit(solution)/shard_map/ppermute | solution.py:115
  100.4 8.8 %collective-permute-start.9 = (f32[64,128]{0,1:T(8,128)S(1)}, f32[64,128]{0,1:T(8,128)S(1)}, u32[]{:S(2)}, u32[]{:S(2)}) collective-permute-start(f32[64,128]{0,1:T(8,128)S(1)} %copy.7), channel_id=1, source_target_pairs={{16,0},{49,1},{130,2},{162,3},{308,4},{388,5},{102,6},{230,7},{505... | collective-permute-start | bytes 98312 | tf_op jit(solution)/shard_map/ppermute | solution.py:116
  109.1 1.9 %collective-permute-start.11 = (f32[64,128]{1,0:T(8,128)S(1)}, f32[64,128]{1,0:T(8,128)S(1)}, u32[]{:S(2)}, u32[]{:S(2)}) collective-permute-start(f32[64,128]{1,0:T(8,128)S(1)} %reduce_sum.42), channel_id=1, source_target_pairs={{32,1},{257,2},{145,3},{433,4},{321,5},{465,6},{209,7},{368,8},{11... | collective-permute-start | bytes 98312 | tf_op jit(solution)/shard_map/ppermute | solution.py:117
  111.1 1.5 %collective-permute-done.9 = f32[64,128]{0,1:T(8,128)S(1)} collective-permute-done((f32[64,128]{0,1:T(8,128)S(1)}, f32[64,128]{0,1:T(8,128)S(1)}, u32[]{:S(2)}, u32[]{:S(2)}) %collective-permute-start.9) | collective-permute-done | bytes 32800 | tf_op jit(solution)/shard_map/ppermute | solution.py:116
  112.6 11.7 %collective-permute-done.11 = f32[64,128]{1,0:T(8,128)S(1)} collective-permute-done((f32[64,128]{1,0:T(8,128)S(1)}, f32[64,128]{1,0:T(8,128)S(1)}, u32[]{:S(2)}, u32[]{:S(2)}) %collective-permute-start.11) | collective-permute-done | bytes 32800 | tf_op jit(solution)/shard_map/ppermute | solution.py:117
  (35 shorter events, 11.8 us)
Async XLA Ops:
  0.0 0.7 copy-start
  2.3 7.7 %collective-permute-start.3 = (bf16[1600,128]{1,0:T(8,128)(2,1)S(1)}, bf16[1600,128]{1,0:T(8,128)(2,1)S(1)}, u32[]{:S(2)}, u32[]{:S(2)}) collective-permute-start(bf16[1600,128]{1,0:T(8,128)(2,1)S(1)} %bitcast.50), channel_id=1, source_target_pairs={{0,1},{1,0},{2,3},{3,2},{4,5},{5,4},{6,7},{7,6},{8,9},{9,8},{10,11... | collective-permute-start | bytes 1228808 | tf_op jit(solution)/shard_map/ppermute | solution.py:82
  4.2 10.2 %collective-permute-start = (bf16[1600,128]{1,0:T(8,128)(2,1)S(1)}, bf16[1600,128]{1,0:T(8,128)(2,1)S(1)}, u32[]{:S(2)}, u32[]{:S(2)}) collective-permute-start(bf16[1600,128]{1,0:T(8,128)(2,1)S(1)} %bitcast.33), channel_id=1, source_target_pairs={{0,2},{1,15},{2,4},{3,1},{4,6},{5,3},{6,8},{7,5},{8,10},{9,7},{10,... | collective-permute-start | bytes 1228808 | tf_op jit(solution)/shard_map/ppermute | solution.py:97
  10.0 12.0 %collective-permute-start.4 = (bf16[1600,128]{1,0:T(8,128)(2,1)S(1)}, bf16[1600,128]{1,0:T(8,128)(2,1)S(1)}, u32[]{:S(2)}, u32[]{:S(2)}) collective-permute-start(bf16[1600,128]{1,0:T(8,128)(2,1)S(1)} %collective-permute-done.3), channel_id=1, source_target_pairs={{0,2},{1,15},{2,4},{3,1},{4,6},{5,3},{6,8},{7,5},{8,10},{9,7},{10,... | collective-permute-start | bytes 1228808 | tf_op jit(solution)/shard_map/ppermute | solution.py:97
  14.4 11.1 %collective-permute-start.1 = (bf16[1600,128]{1,0:T(8,128)(2,1)S(1)}, bf16[1600,128]{1,0:T(8,128)(2,1)S(1)}, u32[]{:S(2)}, u32[]{:S(2)}) collective-permute-start(bf16[1600,128]{1,0:T(8,128)(2,1)S(1)} %collective-permute-done), channel_id=1, source_target_pairs={{0,2},{1,15},{2,4},{3,1},{4,6},{5,3},{6,8},{7,5},{8,10},{9,7},{10,... | collective-permute-start | bytes 1228808 | tf_op jit(solution)/shard_map/ppermute | solution.py:97
  22.0 9.8 %collective-permute-start.5 = (bf16[1600,128]{1,0:T(8,128)(2,1)S(1)}, bf16[1600,128]{1,0:T(8,128)(2,1)S(1)}, u32[]{:S(2)}, u32[]{:S(2)}) collective-permute-start(bf16[1600,128]{1,0:T(8,128)(2,1)S(1)} %collective-permute-done.4), channel_id=1, source_target_pairs={{0,2},{1,15},{2,4},{3,1},{4,6},{5,3},{6,8},{7,5},{8,10},{9,7},{10,... | collective-permute-start | bytes 1228808 | tf_op jit(solution)/shard_map/ppermute | solution.py:97
  32.9 11.5 %all-to-all-start = ((f32[4,5,64,128]{3,2,1,0:T(8,128)}), f32[4,5,64,128]{3,2,1,0:T(8,128)S(1)}, u32[]{:S(2)}, u32[]{:S(2)}) async-start(f32[4,5,64,128]{3,2,1,0:T(8,128)} %bitcast.5), calls=%async_computation | async-start | bytes 1310720 | tf_op jit(solution)/shard_map/all_to_all | solution.py:93
  37.7 9.8 %collective-permute-start.2 = (bf16[1600,128]{1,0:T(8,128)(2,1)S(1)}, bf16[1600,128]{1,0:T(8,128)(2,1)S(1)}, u32[]{:S(2)}, u32[]{:S(2)}) collective-permute-start(bf16[1600,128]{1,0:T(8,128)(2,1)S(1)} %collective-permute-done.1), channel_id=1, source_target_pairs={{0,2},{1,15},{2,4},{3,1},{4,6},{5,3},{6,8},{7,5},{8,10},{9,7},{10,... | collective-permute-start | bytes 1228808 | tf_op jit(solution)/shard_map/ppermute | solution.py:100
  41.3 10.6 %collective-permute-start.6 = (bf16[1600,128]{1,0:T(8,128)(2,1)S(1)}, bf16[1600,128]{1,0:T(8,128)(2,1)S(1)}, u32[]{:S(2)}, u32[]{:S(2)}) collective-permute-start(bf16[1600,128]{1,0:T(8,128)(2,1)S(1)} %collective-permute-done.5), channel_id=1, source_target_pairs={{0,2},{1,15},{2,4},{3,1},{4,6},{5,3},{6,8},{7,5},{8,10},{9,7},{10,... | collective-permute-start | bytes 1228808 | tf_op jit(solution)/shard_map/ppermute | solution.py:100
  52.4 17.4 %collective-permute-start.7 = (bf16[1600,128]{1,0:T(8,128)(2,1)S(1)}, bf16[1600,128]{1,0:T(8,128)(2,1)S(1)}, u32[]{:S(2)}, u32[]{:S(2)}) collective-permute-start(bf16[1600,128]{1,0:T(8,128)(2,1)S(1)} %collective-permute-done.2), channel_id=1, source_target_pairs={{0,2},{1,15},{2,4},{3,1},{4,6},{5,3},{6,8},{7,5},{8,10},{9,7},{10,... | collective-permute-start | bytes 1228808 | tf_op jit(solution)/shard_map/ppermute | solution.py:103
  57.2 12.6 %collective-permute-start.8 = (bf16[1600,128]{1,0:T(8,128)(2,1)S(1)}, bf16[1600,128]{1,0:T(8,128)(2,1)S(1)}, u32[]{:S(2)}, u32[]{:S(2)}) collective-permute-start(bf16[1600,128]{1,0:T(8,128)(2,1)S(1)} %collective-permute-done.6), channel_id=1, source_target_pairs={{0,2},{1,15},{2,4},{3,1},{4,6},{5,3},{6,8},{7,5},{8,10},{9,7},{10,... | collective-permute-start | bytes 1228808 | tf_op jit(solution)/shard_map/ppermute | solution.py:103
  60.2 9.4 %all-to-all-start.1 = ((f32[4,2,64,128]{3,2,1,0:T(8,128)}), f32[4,2,64,128]{3,2,1,0:T(8,128)S(1)}, u32[]{:S(2)}, u32[]{:S(2)}) async-start(f32[4,2,64,128]{3,2,1,0:T(8,128)} %bitcast.6), calls=%async_computation.1 | async-start | bytes 524288 | tf_op jit(solution)/shard_map/all_to_all | solution.py:93
  95.5 15.6 %collective-permute-start.10 = (f32[64,128]{0,1:T(8,128)S(1)}, f32[64,128]{0,1:T(8,128)S(1)}, u32[]{:S(2)}, u32[]{:S(2)}) collective-permute-start(f32[64,128]{0,1:T(8,128)S(1)} %copy.7), channel_id=1, source_target_pairs={{0,0},{33,1},{66,2},{146,3},{292,4},{324,5},{86,6},{214,7},{377,8}... | collective-permute-start | bytes 98312 | tf_op jit(solution)/shard_map/ppermute | solution.py:115
  100.4 12.2 %collective-permute-start.9 = (f32[64,128]{0,1:T(8,128)S(1)}, f32[64,128]{0,1:T(8,128)S(1)}, u32[]{:S(2)}, u32[]{:S(2)}) collective-permute-start(f32[64,128]{0,1:T(8,128)S(1)} %copy.7), channel_id=1, source_target_pairs={{16,0},{49,1},{130,2},{162,3},{308,4},{388,5},{102,6},{230,7},{505... | collective-permute-start | bytes 98312 | tf_op jit(solution)/shard_map/ppermute | solution.py:116
  109.1 15.1 %collective-permute-start.11 = (f32[64,128]{1,0:T(8,128)S(1)}, f32[64,128]{1,0:T(8,128)S(1)}, u32[]{:S(2)}, u32[]{:S(2)}) collective-permute-start(f32[64,128]{1,0:T(8,128)S(1)} %reduce_sum.42), channel_id=1, source_target_pairs={{32,1},{257,2},{145,3},{433,4},{321,5},{465,6},{209,7},{368,8},{11... | collective-permute-start | bytes 98312 | tf_op jit(solution)/shard_map/ppermute | solution.py:117

commit v3 on v1

--- a/solution.py
+++ b/solution.py
@@ -29,6 +29,11 @@
     return (up, block_at(up, s, i, j)), (1 - up, block_at(1 - up, s, j, i))
 
 
+def holder(place, g):
+    first, second = divmod(2 * place + g, AZ // 2)
+    return first // 2 * AZ + 2 * second + first % 2
+
+
 def deliveries():
     direct = ([], [])
     mirrored = []
@@ -38,9 +43,9 @@
             for i in range(2):
                 own, other = sources(X, j, Y, i)
                 for p in range(2):
-                    direct[p].append((dev(2 * own[1] + (h ^ p), Y, own[0]), dev(A, Y, i)))
+                    direct[p].append((dev(holder(own[1], h ^ p), Y, own[0]), dev(A, Y, i)))
                 if other is not None:
-                    mirrored.append((dev(2 * other[1] + h, X, other[0]), dev(A, Y, i)))
+                    mirrored.append((dev(holder(other[1], h), X, other[0]), dev(A, Y, i)))
     return direct[0], direct[1], mirrored
 
 
@@ -53,11 +58,18 @@
     chip, core = row // 2, row % 2
 
     blocks = cols // BS
-    mine = lax.dynamic_slice_in_dim(significant, row * blocks, blocks, 1)
-    lane = lax.broadcasted_iota(jnp.int32, (aux_here, cols), 1) // BS
-    keep = jnp.where(lane == 0, mine[:, :1], mine[:, 1:2]) != 0
-    masked = jnp.where(keep[:, None, :], slabs, jnp.zeros_like(slabs))
+    lane = lax.broadcasted_iota(jnp.int32, (1, cols), 1) // BS
 
+    def mask_of(first, count, block_row):
+        mine = lax.dynamic_slice(significant, (first, block_row * blocks), (count, blocks))
+        return (jnp.where(lane == 0, mine[:, :1], mine[:, 1:2]) != 0)[:, None, :]
+
+    def masked_half(x, block_row):
+        x = x.reshape(half, occupied, cols)
+        return jnp.where(mask_of(core * half, half, block_row), x, jnp.zeros_like(x)).reshape(depth, cols)
+
+    masked = jnp.where(mask_of(0, aux_here, row), slabs, jnp.zeros_like(slabs))
+    raw = lax.dynamic_slice_in_dim(slabs, core * half, half, 0).reshape(depth, cols)
     own = lax.dynamic_slice_in_dim(masked, core * half, half, 0).reshape(depth, cols)
     give = lax.dynamic_slice_in_dim(masked, (1 - core) * half, half, 0).reshape(depth, cols)
     swap = [(r, r ^ 1) for r in range(2 * CHIPS)]
@@ -66,7 +78,7 @@
         for y in range(CHIPS)
         for c in range(2)
     ]
-    a, b = own, lax.ppermute(give, "row", swap)
+    a, b = raw, lax.ppermute(give, "row", swap)
     left = jnp.concatenate([own.T, b.T], axis=0)
     whole = masked.reshape(2 * depth, cols)
 
@@ -77,18 +89,20 @@
     for step in range(1, CHIPS // 2 + 1):
         a = lax.ppermute(a, "row", ring)
         b = lax.ppermute(b, "row", ring)
+        there = (chip + jnp.where(core == 0, CHIPS - step, step)) % CHIPS
+        near = masked_half(a, 2 * there + core)
         if step < CHIPS // 2:
-            made += [dot(left, a), dot(left, b)]
+            made += [dot(left, near), dot(left, b)]
         else:
             low = chip < CHIPS // 2
             made.append(dot(left[:cols], b))
-            made.append(dot(jnp.where(low, left[:cols], left[cols:]), jnp.where(low, a, b)))
-    pieces = jnp.concatenate(made, axis=0).reshape(AX, AZ, BS, cols)
+            made.append(dot(jnp.where(low, left[:cols], left[cols:]), jnp.where(low, near, b)))
+    pieces = jnp.concatenate(made, axis=0).reshape(2 * AX, AZ // 2, BS, cols)
 
-    over_x = [[x * AZ + z for x in range(AX)] for z in range(AZ)]
-    over_z = [[x * AZ + z for z in range(AZ)] for x in range(AX)]
-    got = lax.all_to_all(pieces, "aux", 0, 0, axis_index_groups=over_x, tiled=True).sum(axis=0)
-    got = lax.all_to_all(got, "aux", 0, 0, axis_index_groups=over_z, tiled=True).sum(axis=0)
+    eights = [[x * AZ + 2 * k + m for x in range(AX) for m in range(2)] for k in range(AZ // 2)]
+    fours = [[x * AZ + 2 * k + m for k in range(AZ // 2)] for x in range(AX) for m in range(2)]
+    got = lax.all_to_all(pieces, "aux", 0, 0, axis_index_groups=eights, tiled=True).sum(axis=0)
+    got = lax.all_to_all(got, "aux", 0, 0, axis_index_groups=fours, tiled=True).sum(axis=0)
 
     first, second, mirrored = deliveries()
     d0 = lax.ppermute(got, ("aux", "row"), first)

time: 115 us -> 115 us (level)
  the two profiles are of different devices: /device:TPU:40 before, /device:TPU:7 now
where the time goes in v3:
time: 115 us; the launch traced here: 114 us
  starting transfers between devices  56.1 us (49%)
  blocking collectives  30.3 us (26%)
  waiting for transfers between devices  18.6 us (16%)
  matrix products  4.05 us (4%)
  local copies, waits for them, and re-layouts  3.46 us (3%)
  other arithmetic  1.17 us (1%)
    ppermute x4, starting transfers between devices, local(): b = lax.ppermute(b, 'row', ring)  16.6 us
    ppermute x1, starting transfers between devices, local(): d1 = lax.ppermute(got, ('aux', 'row'), second)  16.1 us
    ppermute x4, starting transfers between devices, local(): a = lax.ppermute(a, 'row', ring)  15.9 us
    all_to_all x1, blocking collectives, local(): lax.all_to_all(pieces, 'aux', 0, 0, axis_index_groups=eights, tiled=True)  15.5 us
    all_to_all x1, blocking collectives, local(): lax.all_to_all(got, 'aux', 0, 0, axis_index_groups=fours, tiled=True)  14.7 us
    ppermute x1, waiting for transfers between devices, local(): t = lax.ppermute(got, ('aux', 'row'), mirrored)  11.1 us
    ppermute x4, waiting for transfers between devices, local(): b = lax.ppermute(b, 'row', ring)  6.75 us
    dot_general x10, matrix products, dot(): return jnp.dot(x, y, preferred_element_type=jnp.float32)  4.05 us
  transfers between devices with their start and end apart: 12, of which 5 were waited for; matrix products, arithmetic and copies ran while one was open for 5% of the time, Pallas kernels for 0%

profile of v3, /device:TPU:7, one launch (start us, length us, event | category | flops | bytes accessed | tf_op | source)
XLA Modules:
  0.0 114.1 jit_solution(2362517660251563616)
XLA Ops:
  0.0 1.8 %constant_dynamic-slice_fusion = bf16[4,400,128]{2,1,0:T(8,128)(2,1)} fusion(bf16[8,400,128]{2,1,0:T(8,128)(2,1)} %param.2, s32[]{:T(128)S(6)} %select_n.188), kind=kLoop, calls=%fused_computation.47 | loop fusion | bytes 819204 | tf_op jit(solution)/shard_map/dynamic_slice | solution.py:72
  1.8 5.1 %collective-permute-start.1 = (bf16[1600,128]{1,0:T(8,128)(2,1)}, bf16[1600,128]{1,0:T(8,128)(2,1)S(1)}, u32[]{:S(2)}, u32[]{:S(2)}) collective-permute-start(bf16[1600,128]{1,0:T(8,128)(2,1)} %bitcast.6), channel_id=1, source_target_pairs={{0,2},{1,15},{2,4},{3,1},{4,6},{5,3},{6,8},{7,5},{8,10},{9,7},{10,... | collective-permute-start | bytes 1228808 | tf_op jit(solution)/shard_map/ppermute | solution.py:90
  7.0 0.8 constant_dynamic-slice_fusion.3
  8.1 1.9 %collective-permute-start = (bf16[1600,128]{1,0:T(8,128)(2,1)S(1)}, bf16[1600,128]{1,0:T(8,128)(2,1)S(1)}, u32[]{:S(2)}, u32[]{:S(2)}) collective-permute-start(bf16[1600,128]{1,0:T(8,128)(2,1)S(1)} %bitcast.56), channel_id=1, source_target_pairs={{0,1},{1,0},{2,3},{3,2},{4,5},{5,4},{6,7},{7,6},{8,9},{9,8},{10,11... | collective-permute-start | bytes 1228808 | tf_op jit(solution)/shard_map/ppermute | solution.py:81
  11.1 0.6 collective-permute-done
  11.8 3.0 %collective-permute-start.2 = (bf16[1600,128]{1,0:T(8,128)(2,1)S(1)}, bf16[1600,128]{1,0:T(8,128)(2,1)S(1)}, u32[]{:S(2)}, u32[]{:S(2)}) collective-permute-start(bf16[1600,128]{1,0:T(8,128)(2,1)S(1)} %collective-permute-done), channel_id=1, source_target_pairs={{0,2},{1,15},{2,4},{3,1},{4,6},{5,3},{6,8},{7,5},{8,10},{9,7},{10,... | collective-permute-start | bytes 1228808 | tf_op jit(solution)/shard_map/ppermute | solution.py:91
  14.8 3.0 %collective-permute-start.3 = (bf16[1600,128]{1,0:T(8,128)(2,1)S(1)}, bf16[1600,128]{1,0:T(8,128)(2,1)S(1)}, u32[]{:S(2)}, u32[]{:S(2)}) collective-permute-start(bf16[1600,128]{1,0:T(8,128)(2,1)S(1)} %collective-permute-done.1), channel_id=1, source_target_pairs={{0,2},{1,15},{2,4},{3,1},{4,6},{5,3},{6,8},{7,5},{8,10},{9,7},{10,... | collective-permute-start | bytes 1228808 | tf_op jit(solution)/shard_map/ppermute | solution.py:90
  18.2 2.6 %collective-permute-done.2 = bf16[1600,128]{1,0:T(8,128)(2,1)S(1)} collective-permute-done((bf16[1600,128]{1,0:T(8,128)(2,1)S(1)}, bf16[1600,128]{1,0:T(8,128)(2,1)S(1)}, u32[]{:S(2)}, u32[]{:S(2)}) %collective-permute-start.2) | collective-permute-done | bytes 409632 | tf_op jit(solution)/shard_map/ppermute | solution.py:91
  20.8 3.9 %collective-permute-start.4 = (bf16[1600,128]{1,0:T(8,128)(2,1)S(1)}, bf16[1600,128]{1,0:T(8,128)(2,1)S(1)}, u32[]{:S(2)}, u32[]{:S(2)}) collective-permute-start(bf16[1600,128]{1,0:T(8,128)(2,1)S(1)} %collective-permute-done.2), channel_id=1, source_target_pairs={{0,2},{1,15},{2,4},{3,1},{4,6},{5,3},{6,8},{7,5},{8,10},{9,7},{10,... | collective-permute-start | bytes 1228808 | tf_op jit(solution)/shard_map/ppermute | solution.py:91
  25.2 3.9 %collective-permute-start.5 = (bf16[1600,128]{1,0:T(8,128)(2,1)S(1)}, bf16[1600,128]{1,0:T(8,128)(2,1)S(1)}, u32[]{:S(2)}, u32[]{:S(2)}) collective-permute-start(bf16[1600,128]{1,0:T(8,128)(2,1)S(1)} %collective-permute-done.3), channel_id=1, source_target_pairs={{0,2},{1,15},{2,4},{3,1},{4,6},{5,3},{6,8},{7,5},{8,10},{9,7},{10,... | collective-permute-start | bytes 1228808 | tf_op jit(solution)/shard_map/ppermute | solution.py:90
  29.1 0.4 convolution_dynamic-update-slice_fusion.4
  29.7 4.8 %collective-permute-start.6 = (bf16[1600,128]{1,0:T(8,128)(2,1)S(1)}, bf16[1600,128]{1,0:T(8,128)(2,1)S(1)}, u32[]{:S(2)}, u32[]{:S(2)}) collective-permute-start(bf16[1600,128]{1,0:T(8,128)(2,1)S(1)} %collective-permute-done.4), channel_id=1, source_target_pairs={{0,2},{1,15},{2,4},{3,1},{4,6},{5,3},{6,8},{7,5},{8,10},{9,7},{10,... | collective-permute-start | bytes 1228808 | tf_op jit(solution)/shard_map/ppermute | solution.py:91
  34.5 0.4 convolution_dynamic-update-slice_fusion.3
  35.0 3.9 %collective-permute-start.8 = (bf16[1600,128]{1,0:T(8,128)(2,1)S(1)}, bf16[1600,128]{1,0:T(8,128)(2,1)S(1)}, u32[]{:S(2)}, u32[]{:S(2)}) collective-permute-start(bf16[1600,128]{1,0:T(8,128)(2,1)S(1)} %collective-permute-done.5), channel_id=1, source_target_pairs={{0,2},{1,15},{2,4},{3,1},{4,6},{5,3},{6,8},{7,5},{8,10},{9,7},{10,... | collective-permute-start | bytes 1228808 | tf_op jit(solution)/shard_map/ppermute | solution.py:90
  39.0 0.4 convolution_dynamic-update-slice_fusion.2
  39.4 5.0 %collective-permute-start.7 = (bf16[1600,128]{1,0:T(8,128)(2,1)S(1)}, bf16[1600,128]{1,0:T(8,128)(2,1)S(1)}, u32[]{:S(2)}, u32[]{:S(2)}) collective-permute-start(bf16[1600,128]{1,0:T(8,128)(2,1)S(1)} %collective-permute-done.6), channel_id=1, source_target_pairs={{0,2},{1,15},{2,4},{3,1},{4,6},{5,3},{6,8},{7,5},{8,10},{9,7},{10,... | collective-permute-start | bytes 1228808 | tf_op jit(solution)/shard_map/ppermute | solution.py:91
  45.3 4.0 %collective-permute-done.7 = bf16[1600,128]{1,0:T(8,128)(2,1)S(1)} collective-permute-done((bf16[1600,128]{1,0:T(8,128)(2,1)S(1)}, bf16[1600,128]{1,0:T(8,128)(2,1)S(1)}, u32[]{:S(2)}, u32[]{:S(2)}) %collective-permute-start.7) | collective-permute-done | bytes 409632 | tf_op jit(solution)/shard_map/ppermute | solution.py:91
  50.0 15.5 %all_to_all.10 = f32[8,4,64,128]{3,2,1,0:T(8,128)S(1)} all-to-all(f32[8,4,64,128]{3,2,1,0:T(8,128)S(1)} %bitcast.55), channel_id=1, replica_groups={{0,16,128,144,256,272,384,400},{32,48,160,176,288,304,416,432},{64,80,1..., dimensions={0} | all-to-all | bytes 2097152 | tf_op jit(solution)/shard_map/all_to_all | solution.py:104
  65.6 14.7 %all_to_all.11 = f32[4,64,128]{2,1,0:T(8,128)S(1)} all-to-all(f32[4,64,128]{2,1,0:T(8,128)S(1)} %reduce_sum.18), channel_id=1, replica_groups={{0,32,64,96},{16,48,80,112},{128,160,192,224},{144,176,208,240},{256,28..., dimensions={0} | all-to-all | bytes 262144 | tf_op jit(solution)/shard_map/all_to_all | solution.py:105
  80.5 3.7 %collective-permute-start.10 = (f32[64,128]{0,1:T(8,128)S(1)}, f32[64,128]{0,1:T(8,128)S(1)}, u32[]{:S(2)}, u32[]{:S(2)}) collective-permute-start(f32[64,128]{0,1:T(8,128)S(1)} %copy.4), channel_id=1, source_target_pairs={{0,0},{65,1},{18,2},{82,3},{148,4},{212,5},{278,6},{342,7},{473,8}... | collective-permute-start | bytes 98312 | tf_op jit(solution)/shard_map/ppermute | solution.py:108
  84.2 16.1 %collective-permute-start.9 = (f32[64,128]{0,1:T(8,128)S(1)}, f32[64,128]{0,1:T(8,128)S(1)}, u32[]{:S(2)}, u32[]{:S(2)}) collective-permute-start(f32[64,128]{0,1:T(8,128)S(1)} %copy.4), channel_id=1, source_target_pairs={{32,0},{97,1},{50,2},{114,3},{180,4},{244,5},{310,6},{374,7},{505,... | collective-permute-start | bytes 98312 | tf_op jit(solution)/shard_map/ppermute | solution.py:109
  100.3 1.9 %collective-permute-start.11 = (f32[64,128]{1,0:T(8,128)S(1)}, f32[64,128]{1,0:T(8,128)S(1)}, u32[]{:S(2)}, u32[]{:S(2)}) collective-permute-start(f32[64,128]{1,0:T(8,128)S(1)} %reduce_sum.19), channel_id=1, source_target_pairs={{64,1},{193,2},{81,3},{321,4},{209,5},{449,6},{337,7},{464,8},{400... | collective-permute-start | bytes 98312 | tf_op jit(solution)/shard_map/ppermute | solution.py:110
  102.3 11.1 %collective-permute-done.11 = f32[64,128]{1,0:T(8,128)S(1)} collective-permute-done((f32[64,128]{1,0:T(8,128)S(1)}, f32[64,128]{1,0:T(8,128)S(1)}, u32[]{:S(2)}, u32[]{:S(2)}) %collective-permute-start.11) | collective-permute-done | bytes 32800 | tf_op jit(solution)/shard_map/ppermute | solution.py:110
  113.4 0.7 fusion.6
  (36 shorter events, 4.3 us)
Async XLA Ops:
  0.0 8.0 %copy-start = (bf16[8,400,128]{2,1,0:T(8,128)(2,1)S(1)}, bf16[8,400,128]{2,1,0:T(8,128)(2,1)}, u32[]{:S(2)}) copy-start(bf16[8,400,128]{2,1,0:T(8,128)(2,1)} %param.2) | copy-start | bytes 2457604
  1.8 13.0 %collective-permute-start.1 = (bf16[1600,128]{1,0:T(8,128)(2,1)}, bf16[1600,128]{1,0:T(8,128)(2,1)S(1)}, u32[]{:S(2)}, u32[]{:S(2)}) collective-permute-start(bf16[1600,128]{1,0:T(8,128)(2,1)} %bitcast.6), channel_id=1, source_target_pairs={{0,2},{1,15},{2,4},{3,1},{4,6},{5,3},{6,8},{7,5},{8,10},{9,7},{10,... | collective-permute-start | bytes 1228808 | tf_op jit(solution)/shard_map/ppermute | solution.py:90
  8.1 2.5 %copy-start.1 = (s32[8,32]{1,0:T(8,128)S(1)}, s32[8,32]{1,0:T(8,128)}, u32[]{:S(2)}) copy-start(s32[8,32]{1,0:T(8,128)} %param.3) | copy-start | bytes 3076
  8.1 3.6 %collective-permute-start = (bf16[1600,128]{1,0:T(8,128)(2,1)S(1)}, bf16[1600,128]{1,0:T(8,128)(2,1)S(1)}, u32[]{:S(2)}, u32[]{:S(2)}) collective-permute-start(bf16[1600,128]{1,0:T(8,128)(2,1)S(1)} %bitcast.56), channel_id=1, source_target_pairs={{0,1},{1,0},{2,3},{3,2},{4,5},{5,4},{6,7},{7,6},{8,9},{9,8},{10,11... | collective-permute-start | bytes 1228808 | tf_op jit(solution)/shard_map/ppermute | solution.py:81
  11.8 9.0 %collective-permute-start.2 = (bf16[1600,128]{1,0:T(8,128)(2,1)S(1)}, bf16[1600,128]{1,0:T(8,128)(2,1)S(1)}, u32[]{:S(2)}, u32[]{:S(2)}) collective-permute-start(bf16[1600,128]{1,0:T(8,128)(2,1)S(1)} %collective-permute-done), channel_id=1, source_target_pairs={{0,2},{1,15},{2,4},{3,1},{4,6},{5,3},{6,8},{7,5},{8,10},{9,7},{10,... | collective-permute-start | bytes 1228808 | tf_op jit(solution)/shard_map/ppermute | solution.py:91
  14.8 10.3 %collective-permute-start.3 = (bf16[1600,128]{1,0:T(8,128)(2,1)S(1)}, bf16[1600,128]{1,0:T(8,128)(2,1)S(1)}, u32[]{:S(2)}, u32[]{:S(2)}) collective-permute-start(bf16[1600,128]{1,0:T(8,128)(2,1)S(1)} %collective-permute-done.1), channel_id=1, source_target_pairs={{0,2},{1,15},{2,4},{3,1},{4,6},{5,3},{6,8},{7,5},{8,10},{9,7},{10,... | collective-permute-start | bytes 1228808 | tf_op jit(solution)/shard_map/ppermute | solution.py:90
  20.8 9.0 %collective-permute-start.4 = (bf16[1600,128]{1,0:T(8,128)(2,1)S(1)}, bf16[1600,128]{1,0:T(8,128)(2,1)S(1)}, u32[]{:S(2)}, u32[]{:S(2)}) collective-permute-start(bf16[1600,128]{1,0:T(8,128)(2,1)S(1)} %collective-permute-done.2), channel_id=1, source_target_pairs={{0,2},{1,15},{2,4},{3,1},{4,6},{5,3},{6,8},{7,5},{8,10},{9,7},{10,... | collective-permute-start | bytes 1228808 | tf_op jit(solution)/shard_map/ppermute | solution.py:91
  25.2 9.9 %collective-permute-start.5 = (bf16[1600,128]{1,0:T(8,128)(2,1)S(1)}, bf16[1600,128]{1,0:T(8,128)(2,1)S(1)}, u32[]{:S(2)}, u32[]{:S(2)}) collective-permute-start(bf16[1600,128]{1,0:T(8,128)(2,1)S(1)} %collective-permute-done.3), channel_id=1, source_target_pairs={{0,2},{1,15},{2,4},{3,1},{4,6},{5,3},{6,8},{7,5},{8,10},{9,7},{10,... | collective-permute-start | bytes 1228808 | tf_op jit(solution)/shard_map/ppermute | solution.py:90
  29.7 9.7 %collective-permute-start.6 = (bf16[1600,128]{1,0:T(8,128)(2,1)S(1)}, bf16[1600,128]{1,0:T(8,128)(2,1)S(1)}, u32[]{:S(2)}, u32[]{:S(2)}) collective-permute-start(bf16[1600,128]{1,0:T(8,128)(2,1)S(1)} %collective-permute-done.4), channel_id=1, source_target_pairs={{0,2},{1,15},{2,4},{3,1},{4,6},{5,3},{6,8},{7,5},{8,10},{9,7},{10,... | collective-permute-start | bytes 1228808 | tf_op jit(solution)/shard_map/ppermute | solution.py:91
  35.0 14.6 %collective-permute-start.8 = (bf16[1600,128]{1,0:T(8,128)(2,1)S(1)}, bf16[1600,128]{1,0:T(8,128)(2,1)S(1)}, u32[]{:S(2)}, u32[]{:S(2)}) collective-permute-start(bf16[1600,128]{1,0:T(8,128)(2,1)S(1)} %collective-permute-done.5), channel_id=1, source_target_pairs={{0,2},{1,15},{2,4},{3,1},{4,6},{5,3},{6,8},{7,5},{8,10},{9,7},{10,... | collective-permute-start | bytes 1228808 | tf_op jit(solution)/shard_map/ppermute | solution.py:90
  39.4 9.9 %collective-permute-start.7 = (bf16[1600,128]{1,0:T(8,128)(2,1)S(1)}, bf16[1600,128]{1,0:T(8,128)(2,1)S(1)}, u32[]{:S(2)}, u32[]{:S(2)}) collective-permute-start(bf16[1600,128]{1,0:T(8,128)(2,1)S(1)} %collective-permute-done.6), channel_id=1, source_target_pairs={{0,2},{1,15},{2,4},{3,1},{4,6},{5,3},{6,8},{7,5},{8,10},{9,7},{10,... | collective-permute-start | bytes 1228808 | tf_op jit(solution)/shard_map/ppermute | solution.py:91
  80.5 21.7 %collective-permute-start.10 = (f32[64,128]{0,1:T(8,128)S(1)}, f32[64,128]{0,1:T(8,128)S(1)}, u32[]{:S(2)}, u32[]{:S(2)}) collective-permute-start(f32[64,128]{0,1:T(8,128)S(1)} %copy.4), channel_id=1, source_target_pairs={{0,0},{65,1},{18,2},{82,3},{148,4},{212,5},{278,6},{342,7},{473,8}... | collective-permute-start | bytes 98312 | tf_op jit(solution)/shard_map/ppermute | solution.py:108
  84.2 18.0 %collective-permute-start.9 = (f32[64,128]{0,1:T(8,128)S(1)}, f32[64,128]{0,1:T(8,128)S(1)}, u32[]{:S(2)}, u32[]{:S(2)}) collective-permute-start(f32[64,128]{0,1:T(8,128)S(1)} %copy.4), channel_id=1, source_target_pairs={{32,0},{97,1},{50,2},{114,3},{180,4},{244,5},{310,6},{374,7},{505,... | collective-permute-start | bytes 98312 | tf_op jit(solution)/shard_map/ppermute | solution.py:109
  100.3 13.1 %collective-permute-start.11 = (f32[64,128]{1,0:T(8,128)S(1)}, f32[64,128]{1,0:T(8,128)S(1)}, u32[]{:S(2)}, u32[]{:S(2)}) collective-permute-start(f32[64,128]{1,0:T(8,128)S(1)} %reduce_sum.19), channel_id=1, source_target_pairs={{64,1},{193,2},{81,3},{321,4},{209,5},{449,6},{337,7},{464,8},{400... | collective-permute-start | bytes 98312 | tf_op jit(solution)/shard_map/ppermute | solution.py:110

commit v4 on v3

--- a/solution.py
+++ b/solution.py
@@ -64,39 +64,43 @@
         mine = lax.dynamic_slice(significant, (first, block_row * blocks), (count, blocks))
         return (jnp.where(lane == 0, mine[:, :1], mine[:, 1:2]) != 0)[:, None, :]
 
-    def masked_half(x, block_row):
+    def masked_half(x, block_row, which=core):
         x = x.reshape(half, occupied, cols)
-        return jnp.where(mask_of(core * half, half, block_row), x, jnp.zeros_like(x)).reshape(depth, cols)
+        return jnp.where(mask_of(which * half, half, block_row), x, jnp.zeros_like(x)).reshape(depth, cols)
 
-    masked = jnp.where(mask_of(0, aux_here, row), slabs, jnp.zeros_like(slabs))
-    raw = lax.dynamic_slice_in_dim(slabs, core * half, half, 0).reshape(depth, cols)
-    own = lax.dynamic_slice_in_dim(masked, core * half, half, 0).reshape(depth, cols)
-    give = lax.dynamic_slice_in_dim(masked, (1 - core) * half, half, 0).reshape(depth, cols)
+    def raw_half(which):
+        return lax.dynamic_slice_in_dim(slabs, which * half, half, 0).reshape(depth, cols)
+
     swap = [(r, r ^ 1) for r in range(2 * CHIPS)]
     ring = [
         (2 * y + c, 2 * ((y + (1 if c == 0 else -1)) % CHIPS) + c)
         for y in range(CHIPS)
         for c in range(2)
     ]
-    a, b = raw, lax.ppermute(give, "row", swap)
-    left = jnp.concatenate([own.T, b.T], axis=0)
+    cross = [(2 * y + 1 - c, 2 * ((y + (1 if c == 0 else -1)) % CHIPS) + c) for y in range(CHIPS) for c in range(2)]
+    a, b = lax.optimization_barrier((raw_half(core), raw_half(1 - core)))
+    far_a, far_b = lax.ppermute(a, "row", ring), lax.ppermute(b, "row", cross)
+    masked = jnp.where(mask_of(0, aux_here, row), slabs, jnp.zeros_like(slabs))
+    own = masked_half(a, row)
+    other = lax.ppermute(masked_half(b, row, 1 - core), "row", swap)
+    left = jnp.concatenate([own.T, other.T], axis=0)
     whole = masked.reshape(2 * depth, cols)
 
     def dot(x, y):
         return jnp.dot(x, y, preferred_element_type=jnp.float32)
 
-    made = [dot(whole.T, whole), dot(own.T, b)]
+    made = [dot(whole.T, whole), dot(own.T, other)]
     for step in range(1, CHIPS // 2 + 1):
-        a = lax.ppermute(a, "row", ring)
-        b = lax.ppermute(b, "row", ring)
         there = (chip + jnp.where(core == 0, CHIPS - step, step)) % CHIPS
-        near = masked_half(a, 2 * there + core)
+        near_a = masked_half(far_a, 2 * there + core)
+        near_b = masked_half(far_b, 2 * there + 1 - core)
         if step < CHIPS // 2:
-            made += [dot(left, near), dot(left, b)]
+            far_a, far_b = lax.ppermute(far_a, "row", ring), lax.ppermute(far_b, "row", ring)
+            made += [dot(left, near_a), dot(left, near_b)]
         else:
             low = chip < CHIPS // 2
-            made.append(dot(left[:cols], b))
-            made.append(dot(jnp.where(low, left[:cols], left[cols:]), jnp.where(low, near, b)))
+            made.append(dot(left[:cols], near_b))
+            made.append(dot(jnp.where(low, left[:cols], left[cols:]), jnp.where(low, near_a, near_b)))
     pieces = jnp.concatenate(made, axis=0).reshape(2 * AX, AZ // 2, BS, cols)
 
     eights = [[x * AZ + 2 * k + m for x in range(AX) for m in range(2)] for k in range(AZ // 2)]

time: 115 us -> 114 us (level)
  the two profiles are of different devices: /device:TPU:7 before, /device:TPU:32 now
where the time goes in v4:
time: 114 us; the launch traced here: 113 us
  waiting for transfers between devices  38.9 us (34%)
  blocking collectives  36.7 us (32%)
  starting transfers between devices  29.2 us (26%)
  matrix products  4.04 us (4%)
  local copies, waits for them, and re-layouts  2.74 us (2%)
  other arithmetic  1.37 us (1%)
    all_to_all x1, blocking collectives, local(): lax.all_to_all(got, 'aux', 0, 0, axis_index_groups=fours, tiled=True)  19.3 us
    all_to_all x1, blocking collectives, local(): lax.all_to_all(pieces, 'aux', 0, 0, axis_index_groups=eights, tiled=True)  17.4 us
    ppermute x3, waiting for transfers between devices, local(): lax.ppermute(far_b, 'row', ring)  13.1 us
    ppermute x1, waiting for transfers between devices, local(): t = lax.ppermute(got, ('aux', 'row'), mirrored)  10.8 us
    ppermute x3, starting transfers between devices, local(): lax.ppermute(far_b, 'row', ring)  7.72 us
    ppermute x3, waiting for transfers between devices, local(): lax.ppermute(far_a, 'row', ring)  7.58 us
    ppermute x3, starting transfers between devices, local(): lax.ppermute(far_a, 'row', ring)  5.73 us
    ppermute x2, starting transfers between devices, local(): far_a, far_b = (lax.ppermute(a, 'row', ring), lax.ppermute(b, 'row', cross))  4.64 us
  transfers between devices with their start and end apart: 12, of which 10 were waited for; matrix products, arithmetic and copies ran while one was open for 5% of the time, Pallas kernels for 0%

profile of v4, /device:TPU:32, one launch (start us, length us, event | category | flops | bytes accessed | tf_op | source)
XLA Modules:
  0.0 113.5 jit_solution(9794899047476857766)
XLA Ops:
  0.0 1.2 %constant_dynamic-slice_fusion = (bf16[4,400,128]{2,1,0:T(8,128)(2,1)S(1)}, bf16[4,400,128]{2,1,0:T(8,128)(2,1)S(1)}) fusion(bf16[8,400,128]{2,1,0:T(8,128)(2,1)} %param.2, s32[]{:T(128)S(6)} %select_n.289, s32[]{:T(128)S(6)} %select_n.287), kind=kLoop, calls=%fused_computation.73 | loop fusion | bytes 1638408 | tf_op jit(solution)/shard_map/dynamic_slice | solution.py:72
  1.2 2.7 %collective-permute-start.1 = (bf16[1600,128]{1,0:T(8,128)(2,1)S(1)}, bf16[1600,128]{1,0:T(8,128)(2,1)S(1)}, u32[]{:S(2)}, u32[]{:S(2)}) collective-permute-start(bf16[1600,128]{1,0:T(8,128)(2,1)S(1)} %bitcast.67), channel_id=1, source_target_pairs={{0,2},{1,15},{2,4},{3,1},{4,6},{5,3},{6,8},{7,5},{8,10},{9,7},{10,... | collective-permute-start | bytes 1228808 | tf_op jit(solution)/shard_map/ppermute | solution.py:82
  3.9 1.9 %collective-permute-start.2 = (bf16[1600,128]{1,0:T(8,128)(2,1)S(1)}, bf16[1600,128]{1,0:T(8,128)(2,1)S(1)}, u32[]{:S(2)}, u32[]{:S(2)}) collective-permute-start(bf16[1600,128]{1,0:T(8,128)(2,1)S(1)} %bitcast.65), channel_id=1, source_target_pairs={{1,2},{0,15},{3,4},{2,1},{5,6},{4,3},{7,8},{6,5},{9,10},{8,7},{11,... | collective-permute-start | bytes 1228808 | tf_op jit(solution)/shard_map/ppermute | solution.py:82
  7.4 2.7 %collective-permute-start = (bf16[1600,128]{1,0:T(8,128)(2,1)S(1)}, bf16[1600,128]{1,0:T(8,128)(2,1)S(1)}, u32[]{:S(2)}, u32[]{:S(2)}) collective-permute-start(bf16[1600,128]{1,0:T(8,128)(2,1)S(1)} %bitcast_select_fusion.8), channel_id=1, source_target_pairs={{0,1},{1,0},{2,3},{3,2},{4,5},{5,4},{6,7},{7,6},{8,9},{9,8},{10,11... | collective-permute-start | bytes 1228808 | tf_op jit(solution)/shard_map/ppermute | solution.py:85
  11.0 3.7 %collective-permute-done.1 = bf16[1600,128]{1,0:T(8,128)(2,1)S(1)} collective-permute-done((bf16[1600,128]{1,0:T(8,128)(2,1)S(1)}, bf16[1600,128]{1,0:T(8,128)(2,1)S(1)}, u32[]{:S(2)}, u32[]{:S(2)}) %collective-permute-start.1) | collective-permute-done | bytes 409632 | tf_op jit(solution)/shard_map/ppermute | solution.py:82
  14.7 1.9 %collective-permute-start.3 = (bf16[1600,128]{1,0:T(8,128)(2,1)S(1)}, bf16[1600,128]{1,0:T(8,128)(2,1)S(1)}, u32[]{:S(2)}, u32[]{:S(2)}) collective-permute-start(bf16[1600,128]{1,0:T(8,128)(2,1)S(1)} %collective-permute-done.1), channel_id=1, source_target_pairs={{0,2},{1,15},{2,4},{3,1},{4,6},{5,3},{6,8},{7,5},{8,10},{9,7},{10,... | collective-permute-start | bytes 1228808 | tf_op jit(solution)/shard_map/ppermute | solution.py:98
  16.8 3.9 %collective-permute-start.4 = (bf16[1600,128]{1,0:T(8,128)(2,1)S(1)}, bf16[1600,128]{1,0:T(8,128)(2,1)S(1)}, u32[]{:S(2)}, u32[]{:S(2)}) collective-permute-start(bf16[1600,128]{1,0:T(8,128)(2,1)S(1)} %collective-permute-done.2), channel_id=1, source_target_pairs={{0,2},{1,15},{2,4},{3,1},{4,6},{5,3},{6,8},{7,5},{8,10},{9,7},{10,... | collective-permute-start | bytes 1228808 | tf_op jit(solution)/shard_map/ppermute | solution.py:98
  22.0 3.8 %collective-permute-done.3 = bf16[1600,128]{1,0:T(8,128)(2,1)S(1)} collective-permute-done((bf16[1600,128]{1,0:T(8,128)(2,1)S(1)}, bf16[1600,128]{1,0:T(8,128)(2,1)S(1)}, u32[]{:S(2)}, u32[]{:S(2)}) %collective-permute-start.3) | collective-permute-done | bytes 409632 | tf_op jit(solution)/shard_map/ppermute | solution.py:98
  25.7 1.9 %collective-permute-start.5 = (bf16[1600,128]{1,0:T(8,128)(2,1)S(1)}, bf16[1600,128]{1,0:T(8,128)(2,1)S(1)}, u32[]{:S(2)}, u32[]{:S(2)}) collective-permute-start(bf16[1600,128]{1,0:T(8,128)(2,1)S(1)} %collective-permute-done.3), channel_id=1, source_target_pairs={{0,2},{1,15},{2,4},{3,1},{4,6},{5,3},{6,8},{7,5},{8,10},{9,7},{10,... | collective-permute-start | bytes 1228808 | tf_op jit(solution)/shard_map/ppermute | solution.py:98
  27.7 2.4 %collective-permute-done.4 = bf16[1600,128]{1,0:T(8,128)(2,1)S(1)} collective-permute-done((bf16[1600,128]{1,0:T(8,128)(2,1)S(1)}, bf16[1600,128]{1,0:T(8,128)(2,1)S(1)}, u32[]{:S(2)}, u32[]{:S(2)}) %collective-permute-start.4) | collective-permute-done | bytes 409632 | tf_op jit(solution)/shard_map/ppermute | solution.py:98
  30.1 1.9 %collective-permute-start.6 = (bf16[1600,128]{1,0:T(8,128)(2,1)S(1)}, bf16[1600,128]{1,0:T(8,128)(2,1)S(1)}, u32[]{:S(2)}, u32[]{:S(2)}) collective-permute-start(bf16[1600,128]{1,0:T(8,128)(2,1)S(1)} %collective-permute-done.4), channel_id=1, source_target_pairs={{0,2},{1,15},{2,4},{3,1},{4,6},{5,3},{6,8},{7,5},{8,10},{9,7},{10,... | collective-permute-start | bytes 1228808 | tf_op jit(solution)/shard_map/ppermute | solution.py:98
  33.0 3.8 %collective-permute-done.5 = bf16[1600,128]{1,0:T(8,128)(2,1)S(1)} collective-permute-done((bf16[1600,128]{1,0:T(8,128)(2,1)S(1)}, bf16[1600,128]{1,0:T(8,128)(2,1)S(1)}, u32[]{:S(2)}, u32[]{:S(2)}) %collective-permute-start.5) | collective-permute-done | bytes 409632 | tf_op jit(solution)/shard_map/ppermute | solution.py:98
  36.8 1.9 %collective-permute-start.8 = (bf16[1600,128]{1,0:T(8,128)(2,1)S(1)}, bf16[1600,128]{1,0:T(8,128)(2,1)S(1)}, u32[]{:S(2)}, u32[]{:S(2)}) collective-permute-start(bf16[1600,128]{1,0:T(8,128)(2,1)S(1)} %collective-permute-done.5), channel_id=1, source_target_pairs={{0,2},{1,15},{2,4},{3,1},{4,6},{5,3},{6,8},{7,5},{8,10},{9,7},{10,... | collective-permute-start | bytes 1228808 | tf_op jit(solution)/shard_map/ppermute | solution.py:98
  38.7 2.4 %collective-permute-done.6 = bf16[1600,128]{1,0:T(8,128)(2,1)S(1)} collective-permute-done((bf16[1600,128]{1,0:T(8,128)(2,1)S(1)}, bf16[1600,128]{1,0:T(8,128)(2,1)S(1)}, u32[]{:S(2)}, u32[]{:S(2)}) %collective-permute-start.6) | collective-permute-done | bytes 409632 | tf_op jit(solution)/shard_map/ppermute | solution.py:98
  41.2 1.9 %collective-permute-start.7 = (bf16[1600,128]{1,0:T(8,128)(2,1)S(1)}, bf16[1600,128]{1,0:T(8,128)(2,1)S(1)}, u32[]{:S(2)}, u32[]{:S(2)}) collective-permute-start(bf16[1600,128]{1,0:T(8,128)(2,1)S(1)} %collective-permute-done.6), channel_id=1, source_target_pairs={{0,2},{1,15},{2,4},{3,1},{4,6},{5,3},{6,8},{7,5},{8,10},{9,7},{10,... | collective-permute-start | bytes 1228808 | tf_op jit(solution)/shard_map/ppermute | solution.py:98
  44.0 8.2 %collective-permute-done.7 = bf16[1600,128]{1,0:T(8,128)(2,1)S(1)} collective-permute-done((bf16[1600,128]{1,0:T(8,128)(2,1)S(1)}, bf16[1600,128]{1,0:T(8,128)(2,1)S(1)}, u32[]{:S(2)}, u32[]{:S(2)}) %collective-permute-start.7) | collective-permute-done | bytes 409632 | tf_op jit(solution)/shard_map/ppermute | solution.py:98
  53.0 17.4 %all_to_all.10 = f32[8,4,64,128]{3,2,1,0:T(8,128)S(1)} all-to-all(f32[8,4,64,128]{3,2,1,0:T(8,128)S(1)} %bitcast.69), channel_id=1, replica_groups={{0,16,128,144,256,272,384,400},{32,48,160,176,288,304,416,432},{64,80,1..., dimensions={0} | all-to-all | bytes 2097152 | tf_op jit(solution)/shard_map/all_to_all | solution.py:108
  70.4 19.3 %all_to_all.11 = f32[4,64,128]{2,1,0:T(8,128)S(1)} all-to-all(f32[4,64,128]{2,1,0:T(8,128)S(1)} %reduce_sum.18), channel_id=1, replica_groups={{0,32,64,96},{16,48,80,112},{128,160,192,224},{144,176,208,240},{256,28..., dimensions={0} | all-to-all | bytes 262144 | tf_op jit(solution)/shard_map/all_to_all | solution.py:109
  89.9 3.0 %collective-permute-start.10 = (f32[64,128]{0,1:T(8,128)S(1)}, f32[64,128]{0,1:T(8,128)S(1)}, u32[]{:S(2)}, u32[]{:S(2)}) collective-permute-start(f32[64,128]{0,1:T(8,128)S(1)} %copy.4), channel_id=1, source_target_pairs={{0,0},{65,1},{18,2},{82,3},{148,4},{212,5},{278,6},{342,7},{473,8}... | collective-permute-start | bytes 98312 | tf_op jit(solution)/shard_map/ppermute | solution.py:112
  92.9 4.1 %collective-permute-start.9 = (f32[64,128]{0,1:T(8,128)S(1)}, f32[64,128]{0,1:T(8,128)S(1)}, u32[]{:S(2)}, u32[]{:S(2)}) collective-permute-start(f32[64,128]{0,1:T(8,128)S(1)} %copy.4), channel_id=1, source_target_pairs={{32,0},{97,1},{50,2},{114,3},{180,4},{244,5},{310,6},{374,7},{505,... | collective-permute-start | bytes 98312 | tf_op jit(solution)/shard_map/ppermute | solution.py:113
  97.1 1.3 %collective-permute-start.11 = (f32[64,128]{1,0:T(8,128)S(1)}, f32[64,128]{1,0:T(8,128)S(1)}, u32[]{:S(2)}, u32[]{:S(2)}) collective-permute-start(f32[64,128]{1,0:T(8,128)S(1)} %reduce_sum.19), channel_id=1, source_target_pairs={{64,1},{193,2},{81,3},{321,4},{209,5},{449,6},{337,7},{464,8},{400... | collective-permute-start | bytes 98312 | tf_op jit(solution)/shard_map/ppermute | solution.py:114
  98.4 2.9 %collective-permute-done.10 = f32[64,128]{0,1:T(8,128)S(1)} collective-permute-done((f32[64,128]{0,1:T(8,128)S(1)}, f32[64,128]{0,1:T(8,128)S(1)}, u32[]{:S(2)}, u32[]{:S(2)}) %collective-permute-start.10) | collective-permute-done | bytes 32800 | tf_op jit(solution)/shard_map/ppermute | solution.py:112
  102.0 10.8 %collective-permute-done.11 = f32[64,128]{1,0:T(8,128)S(1)} collective-permute-done((f32[64,128]{1,0:T(8,128)S(1)}, f32[64,128]{1,0:T(8,128)S(1)}, u32[]{:S(2)}, u32[]{:S(2)}) %collective-permute-start.11) | collective-permute-done | bytes 32800 | tf_op jit(solution)/shard_map/ppermute | solution.py:114
  112.8 0.7 fusion.9
  (43 shorter events, 7.1 us)
Async XLA Ops:
  0.0 6.0 %copy-start.1 = (s32[8,32]{1,0:T(8,128)S(1)}, s32[8,32]{1,0:T(8,128)}, u32[]{:S(2)}) copy-start(s32[8,32]{1,0:T(8,128)} %param.3) | copy-start | bytes 3076
  1.2 9.3 %copy-start = (bf16[8,400,128]{2,1,0:T(8,128)(2,1)S(1)}, bf16[8,400,128]{2,1,0:T(8,128)(2,1)}, u32[]{:S(2)}) copy-start(bf16[8,400,128]{2,1,0:T(8,128)(2,1)} %param.2) | copy-start | bytes 2457604
  1.2 13.5 %collective-permute-start.1 = (bf16[1600,128]{1,0:T(8,128)(2,1)S(1)}, bf16[1600,128]{1,0:T(8,128)(2,1)S(1)}, u32[]{:S(2)}, u32[]{:S(2)}) collective-permute-start(bf16[1600,128]{1,0:T(8,128)(2,1)S(1)} %bitcast.67), channel_id=1, source_target_pairs={{0,2},{1,15},{2,4},{3,1},{4,6},{5,3},{6,8},{7,5},{8,10},{9,7},{10,... | collective-permute-start | bytes 1228808 | tf_op jit(solution)/shard_map/ppermute | solution.py:82
  3.9 12.9 %collective-permute-start.2 = (bf16[1600,128]{1,0:T(8,128)(2,1)S(1)}, bf16[1600,128]{1,0:T(8,128)(2,1)S(1)}, u32[]{:S(2)}, u32[]{:S(2)}) collective-permute-start(bf16[1600,128]{1,0:T(8,128)(2,1)S(1)} %bitcast.65), channel_id=1, source_target_pairs={{1,2},{0,15},{3,4},{2,1},{5,6},{4,3},{7,8},{6,5},{9,10},{8,7},{11,... | collective-permute-start | bytes 1228808 | tf_op jit(solution)/shard_map/ppermute | solution.py:82
  7.4 13.3 %collective-permute-start = (bf16[1600,128]{1,0:T(8,128)(2,1)S(1)}, bf16[1600,128]{1,0:T(8,128)(2,1)S(1)}, u32[]{:S(2)}, u32[]{:S(2)}) collective-permute-start(bf16[1600,128]{1,0:T(8,128)(2,1)S(1)} %bitcast_select_fusion.8), channel_id=1, source_target_pairs={{0,1},{1,0},{2,3},{3,2},{4,5},{5,4},{6,7},{7,6},{8,9},{9,8},{10,11... | collective-permute-start | bytes 1228808 | tf_op jit(solution)/shard_map/ppermute | solution.py:85
  14.7 11.0 %collective-permute-start.3 = (bf16[1600,128]{1,0:T(8,128)(2,1)S(1)}, bf16[1600,128]{1,0:T(8,128)(2,1)S(1)}, u32[]{:S(2)}, u32[]{:S(2)}) collective-permute-start(bf16[1600,128]{1,0:T(8,128)(2,1)S(1)} %collective-permute-done.1), channel_id=1, source_target_pairs={{0,2},{1,15},{2,4},{3,1},{4,6},{5,3},{6,8},{7,5},{8,10},{9,7},{10,... | collective-permute-start | bytes 1228808 | tf_op jit(solution)/shard_map/ppermute | solution.py:98
  16.8 13.3 %collective-permute-start.4 = (bf16[1600,128]{1,0:T(8,128)(2,1)S(1)}, bf16[1600,128]{1,0:T(8,128)(2,1)S(1)}, u32[]{:S(2)}, u32[]{:S(2)}) collective-permute-start(bf16[1600,128]{1,0:T(8,128)(2,1)S(1)} %collective-permute-done.2), channel_id=1, source_target_pairs={{0,2},{1,15},{2,4},{3,1},{4,6},{5,3},{6,8},{7,5},{8,10},{9,7},{10,... | collective-permute-start | bytes 1228808 | tf_op jit(solution)/shard_map/ppermute | solution.py:98
  25.7 11.0 %collective-permute-start.5 = (bf16[1600,128]{1,0:T(8,128)(2,1)S(1)}, bf16[1600,128]{1,0:T(8,128)(2,1)S(1)}, u32[]{:S(2)}, u32[]{:S(2)}) collective-permute-start(bf16[1600,128]{1,0:T(8,128)(2,1)S(1)} %collective-permute-done.3), channel_id=1, source_target_pairs={{0,2},{1,15},{2,4},{3,1},{4,6},{5,3},{6,8},{7,5},{8,10},{9,7},{10,... | collective-permute-start | bytes 1228808 | tf_op jit(solution)/shard_map/ppermute | solution.py:98
  30.1 11.0 %collective-permute-start.6 = (bf16[1600,128]{1,0:T(8,128)(2,1)S(1)}, bf16[1600,128]{1,0:T(8,128)(2,1)S(1)}, u32[]{:S(2)}, u32[]{:S(2)}) collective-permute-start(bf16[1600,128]{1,0:T(8,128)(2,1)S(1)} %collective-permute-done.4), channel_id=1, source_target_pairs={{0,2},{1,15},{2,4},{3,1},{4,6},{5,3},{6,8},{7,5},{8,10},{9,7},{10,... | collective-permute-start | bytes 1228808 | tf_op jit(solution)/shard_map/ppermute | solution.py:98
  36.8 15.4 %collective-permute-start.8 = (bf16[1600,128]{1,0:T(8,128)(2,1)S(1)}, bf16[1600,128]{1,0:T(8,128)(2,1)S(1)}, u32[]{:S(2)}, u32[]{:S(2)}) collective-permute-start(bf16[1600,128]{1,0:T(8,128)(2,1)S(1)} %collective-permute-done.5), channel_id=1, source_target_pairs={{0,2},{1,15},{2,4},{3,1},{4,6},{5,3},{6,8},{7,5},{8,10},{9,7},{10,... | collective-permute-start | bytes 1228808 | tf_op jit(solution)/shard_map/ppermute | solution.py:98
  41.2 11.0 %collective-permute-start.7 = (bf16[1600,128]{1,0:T(8,128)(2,1)S(1)}, bf16[1600,128]{1,0:T(8,128)(2,1)S(1)}, u32[]{:S(2)}, u32[]{:S(2)}) collective-permute-start(bf16[1600,128]{1,0:T(8,128)(2,1)S(1)} %collective-permute-done.6), channel_id=1, source_target_pairs={{0,2},{1,15},{2,4},{3,1},{4,6},{5,3},{6,8},{7,5},{8,10},{9,7},{10,... | collective-permute-start | bytes 1228808 | tf_op jit(solution)/shard_map/ppermute | solution.py:98
  89.9 11.4 %collective-permute-start.10 = (f32[64,128]{0,1:T(8,128)S(1)}, f32[64,128]{0,1:T(8,128)S(1)}, u32[]{:S(2)}, u32[]{:S(2)}) collective-permute-start(f32[64,128]{0,1:T(8,128)S(1)} %copy.4), channel_id=1, source_target_pairs={{0,0},{65,1},{18,2},{82,3},{148,4},{212,5},{278,6},{342,7},{473,8}... | collective-permute-start | bytes 98312 | tf_op jit(solution)/shard_map/ppermute | solution.py:112
  92.9 9.1 %collective-permute-start.9 = (f32[64,128]{0,1:T(8,128)S(1)}, f32[64,128]{0,1:T(8,128)S(1)}, u32[]{:S(2)}, u32[]{:S(2)}) collective-permute-start(f32[64,128]{0,1:T(8,128)S(1)} %copy.4), channel_id=1, source_target_pairs={{32,0},{97,1},{50,2},{114,3},{180,4},{244,5},{310,6},{374,7},{505,... | collective-permute-start | bytes 98312 | tf_op jit(solution)/shard_map/ppermute | solution.py:113
  97.1 15.7 %collective-permute-start.11 = (f32[64,128]{1,0:T(8,128)S(1)}, f32[64,128]{1,0:T(8,128)S(1)}, u32[]{:S(2)}, u32[]{:S(2)}) collective-permute-start(f32[64,128]{1,0:T(8,128)S(1)} %reduce_sum.19), channel_id=1, source_target_pairs={{64,1},{193,2},{81,3},{321,4},{209,5},{449,6},{337,7},{464,8},{400... | collective-permute-start | bytes 98312 | tf_op jit(solution)/shard_map/ppermute | solution.py:114

commit v5 on v4

v5 whole, which is shorter than its diff:
```python
import jax
import jax.numpy as jnp
from jax import lax
from jax.sharding import PartitionSpec as P

BS = 64
AX, AZ = 4, 8
CHIPS = 8
BOTH = ("aux", "row")


def dev(aux, chip, core):
    return aux * 2 * CHIPS + (chip % CHIPS) * 2 + core


PLACES = {(s, e, f): (s - 1, f, e) for s in range(1, CHIPS // 2) for f in range(2) for e in range(2)}
PLACES |= {(s, 0, f): (3, s // 4, f) for s in (0, 4) for f in range(2)}


ORDER = [(3, 0)] + [(pair, m) for pair in range(3) for m in range(2)] + [(3, 1)]


def first_holder(Y, core, pair):
    if core:
        return (Y + 1 + 2 * pair) % CHIPS // 2
    return (Y - 1 - 2 * pair) % CHIPS // 2


def second_holder(Y, q, g):
    return 2 * ((Y + q) % 2) + g


def holder(Y, core, tile, g):
    pair, m, q = PLACES[tile]
    return dev(first_holder(Y, core, pair) * AZ + 2 * second_holder(Y, q, g) + (core ^ m), Y, core)


def summing_groups():
    rows = [(Y, c) for Y in range(CHIPS) for c in range(2)]
    first = [
        [dev(first_holder(Y, c, pair) * AZ + 2 * k + (c ^ m), Y, c) for pair, m in ORDER]
        for k in range(AZ // 2)
        for Y, c in rows
    ]
    second = [
        [dev(x * AZ + 2 * second_holder(Y, q, g) + m, Y, c) for q in range(2) for g in range(2)]
        for x in range(AX)
        for m in range(2)
        for Y, c in rows
    ]
    return first, second


def sources(X, j, Y, i):
    d = (X - Y) % CHIPS
    if d == 0:
        return ((i, (0, 0, 0)), None) if i == j else ((i, (0, 0, 1)), (j, (0, 0, 1)))
    if d == CHIPS // 2:
        if i != j:
            return (i, (4, 0, 1)), (j, (4, 0, 1))
        low = Y < CHIPS // 2
        return (i if low else 1 - i, (4, 0, 0)), (1 - i if low else i, (4, 0, 0))
    s, here = (d, 1) if d < CHIPS // 2 else (CHIPS - d, 0)
    there = 1 - here
    return (here, (s, int(i != here), int(j != here))), (there, (s, int(j != there), int(i != there)))


def deliveries():
    direct = ([], [])
    mirrored = []
    for A in range(AX * AZ):
        X, j, h = A // 4, A // 2 % 2, A % 2
        for Y in range(CHIPS):
            for i in range(2):
                own, other = sources(X, j, Y, i)
                for p in range(2):
                    direct[p].append((holder(Y, *own, h ^ p), dev(A, Y, i)))
                if other is not None:
                    mirrored.append((holder(X, *other, h), dev(A, Y, i)))
    return direct[0], direct[1], mirrored


def local(slabs, significant):
    aux_here, occupied, cols = slabs.shape
    half = aux_here // 2
    depth = half * occupied
    row = lax.axis_index("row")
    aux = lax.axis_index("aux")
    chip, core = row // 2, row % 2

    blocks = cols // BS
    lane = lax.broadcasted_iota(jnp.int32, (1, cols), 1) // BS

    def mask_of(first, count, block_row):
        mine = lax.dynamic_slice(significant, (first, block_row * blocks), (count, blocks))
        return (jnp.where(lane == 0, mine[:, :1], mine[:, 1:2]) != 0)[:, None, :]

    def masked_half(x, block_row, which=core):
        x = x.reshape(half, occupied, cols)
        return jnp.where(mask_of(which * half, half, block_row), x, jnp.zeros_like(x)).reshape(depth, cols)

    def raw_half(which):
        return lax.dynamic_slice_in_dim(slabs, which * half, half, 0).reshape(depth, cols)

    swap = [(r, r ^ 1) for r in range(2 * CHIPS)]
    ring = [
        (2 * y + c, 2 * ((y + (1 if c == 0 else -1)) % CHIPS) + c)
        for y in range(CHIPS)
        for c in range(2)
    ]
    cross = [(2 * y + 1 - c, 2 * ((y + (1 if c == 0 else -1)) % CHIPS) + c) for y in range(CHIPS) for c in range(2)]
    a, b = lax.optimization_barrier((raw_half(core), raw_half(1 - core)))
    far_a, far_b = lax.ppermute(a, "row", ring), lax.ppermute(b, "row", cross)
    masked = jnp.where(mask_of(0, aux_here, row), slabs, jnp.zeros_like(slabs))
    own = masked_half(a, row)
    other = lax.ppermute(masked_half(b, row, 1 - core), "row", swap)
    left = jnp.concatenate([own.T, other.T], axis=0)
    whole = masked.reshape(2 * depth, cols)

    def dot(x, y):
        return jnp.dot(x, y, preferred_element_type=jnp.float32)

    tiles = [dot(whole.T, whole), dot(own.T, other)]
    for step in range(1, CHIPS // 2 + 1):
        there = (chip + jnp.where(core == 0, CHIPS - step, step)) % CHIPS
        near_a = masked_half(far_a, 2 * there + core)
        near_b = masked_half(far_b, 2 * there + 1 - core)
        if step < CHIPS // 2:
            far_a, far_b = lax.ppermute(far_a, "row", ring), lax.ppermute(far_b, "row", ring)
            tiles += [dot(left, near_a), dot(left, near_b)]
        else:
            low = chip < CHIPS // 2
            tiles.append(dot(jnp.where(low, left[:cols], left[cols:]), jnp.where(low, near_a, near_b)))
            tiles.append(dot(left[:cols], near_b))
    pieces = jnp.concatenate(tiles, axis=0).reshape(2 * AX, AZ // 2, BS, cols)

    first, second = summing_groups()
    got = lax.all_to_all(pieces, BOTH, 0, 0, axis_index_groups=first, tiled=True).sum(axis=0)
    got = lax.all_to_all(got, BOTH, 0, 0, axis_index_groups=second, tiled=True).sum(axis=0)

    near, next_to, mirrored = deliveries()
    t = lax.optimization_barrier(lax.ppermute(got, BOTH, mirrored).T)
    d0 = lax.ppermute(got, BOTH, near)
    d1 = lax.ppermute(got, BOTH, next_to)
    odd = aux % 2 == 1
    top = jnp.where(odd, d1[:, BS:], d0[:, :BS])
    bottom = jnp.where(odd, d0[:, BS:], d1[:, :BS])
    return jnp.concatenate([top, bottom], axis=0) + t


def solution(mesh):
    return jax.shard_map(
        local,
        mesh=mesh,
        in_specs=(P("aux", None, "row"), P("aux", None)),
        out_specs=P("row", "aux"),
        check_vma=False,
    )
```

time: 114 us -> 111 us (0.974)
  the two profiles are of different devices: /device:TPU:32 before, /device:TPU:23 now
where the time goes in v5:
time: 111 us
  starting transfers between devices  46.6 us (42%)
  blocking collectives  31.3 us (28%)
  waiting for transfers between devices  24.3 us (22%)
  matrix products  4.05 us (4%)
  local copies, waits for them, and re-layouts  2.74 us (2%)
  other arithmetic  1.35 us (1%)
    all_to_all x1, blocking collectives, local(): lax.all_to_all(got, BOTH, 0, 0, axis_index_groups=second, tiled=True)  16.2 us
    all_to_all x1, blocking collectives, local(): lax.all_to_all(pieces, BOTH, 0, 0, axis_index_groups=first, tiled=True)  15.1 us
    ppermute x1, starting transfers between devices, local(): t = lax.optimization_barrier(lax.ppermute(got, BOTH, mirrored).T)  13.6 us
    ppermute x3, waiting for transfers between devices, local(): lax.ppermute(far_b, 'row', ring)  9.25 us
    ppermute x1, starting transfers between devices, local(): d0 = lax.ppermute(got, BOTH, near)  8.83 us
    ppermute x2, starting transfers between devices, local(): far_a, far_b = (lax.ppermute(a, 'row', ring), lax.ppermute(b, 'row', cross))  8.59 us
    ppermute x3, waiting for transfers between devices, local(): lax.ppermute(far_a, 'row', ring)  7.74 us
    ppermute x1, waiting for transfers between devices, local(): d1 = lax.ppermute(got, BOTH, next_to)  6.87 us
  transfers between devices with their start and end apart: 12, of which 8 were waited for; matrix products, arithmetic and copies ran while one was open for 5% of the time, Pallas kernels for 0%

profile of v5, /device:TPU:23, one launch (start us, length us, event | category | flops | bytes accessed | tf_op | source)
XLA Modules:
  0.0 110.8 jit_solution(14557875823145274881)
XLA Ops:
  0.0 1.2 %constant_dynamic-slice_fusion = (bf16[4,400,128]{2,1,0:T(8,128)(2,1)S(1)}, bf16[4,400,128]{2,1,0:T(8,128)(2,1)S(1)}) fusion(bf16[8,400,128]{2,1,0:T(8,128)(2,1)} %param.2, s32[]{:T(128)S(6)} %select_n.280, s32[]{:T(128)S(6)} %select_n.278), kind=kLoop, calls=%fused_computation.68 | loop fusion | bytes 1638408 | tf_op jit(solution)/shard_map/dynamic_slice | solution.py:103
  1.2 2.2 %collective-permute-start.1 = (bf16[1600,128]{1,0:T(8,128)(2,1)S(1)}, bf16[1600,128]{1,0:T(8,128)(2,1)S(1)}, u32[]{:S(2)}, u32[]{:S(2)}) collective-permute-start(bf16[1600,128]{1,0:T(8,128)(2,1)S(1)} %bitcast.66), channel_id=1, source_target_pairs={{0,2},{1,15},{2,4},{3,1},{4,6},{5,3},{6,8},{7,5},{8,10},{9,7},{10,... | collective-permute-start | bytes 1228808 | tf_op jit(solution)/shard_map/ppermute | solution.py:113
  3.4 6.4 %collective-permute-start.2 = (bf16[1600,128]{1,0:T(8,128)(2,1)S(1)}, bf16[1600,128]{1,0:T(8,128)(2,1)S(1)}, u32[]{:S(2)}, u32[]{:S(2)}) collective-permute-start(bf16[1600,128]{1,0:T(8,128)(2,1)S(1)} %bitcast.64), channel_id=1, source_target_pairs={{1,2},{0,15},{3,4},{2,1},{5,6},{4,3},{7,8},{6,5},{9,10},{8,7},{11,... | collective-permute-start | bytes 1228808 | tf_op jit(solution)/shard_map/ppermute | solution.py:113
  11.4 1.9 %collective-permute-start = (bf16[1600,128]{1,0:T(8,128)(2,1)S(1)}, bf16[1600,128]{1,0:T(8,128)(2,1)S(1)}, u32[]{:S(2)}, u32[]{:S(2)}) collective-permute-start(bf16[1600,128]{1,0:T(8,128)(2,1)S(1)} %bitcast_select_fusion.8), channel_id=1, source_target_pairs={{0,1},{1,0},{2,3},{3,2},{4,5},{5,4},{6,7},{7,6},{8,9},{9,8},{10,11... | collective-permute-start | bytes 1228808 | tf_op jit(solution)/shard_map/ppermute | solution.py:116
  14.2 1.9 %collective-permute-start.3 = (bf16[1600,128]{1,0:T(8,128)(2,1)S(1)}, bf16[1600,128]{1,0:T(8,128)(2,1)S(1)}, u32[]{:S(2)}, u32[]{:S(2)}) collective-permute-start(bf16[1600,128]{1,0:T(8,128)(2,1)S(1)} %collective-permute-done.1), channel_id=1, source_target_pairs={{0,2},{1,15},{2,4},{3,1},{4,6},{5,3},{6,8},{7,5},{8,10},{9,7},{10,... | collective-permute-start | bytes 1228808 | tf_op jit(solution)/shard_map/ppermute | solution.py:129
  16.2 2.2 %collective-permute-start.4 = (bf16[1600,128]{1,0:T(8,128)(2,1)S(1)}, bf16[1600,128]{1,0:T(8,128)(2,1)S(1)}, u32[]{:S(2)}, u32[]{:S(2)}) collective-permute-start(bf16[1600,128]{1,0:T(8,128)(2,1)S(1)} %collective-permute-done.2), channel_id=1, source_target_pairs={{0,2},{1,15},{2,4},{3,1},{4,6},{5,3},{6,8},{7,5},{8,10},{9,7},{10,... | collective-permute-start | bytes 1228808 | tf_op jit(solution)/shard_map/ppermute | solution.py:129
  19.7 3.5 %collective-permute-done.3 = bf16[1600,128]{1,0:T(8,128)(2,1)S(1)} collective-permute-done((bf16[1600,128]{1,0:T(8,128)(2,1)S(1)}, bf16[1600,128]{1,0:T(8,128)(2,1)S(1)}, u32[]{:S(2)}, u32[]{:S(2)}) %collective-permute-start.3) | collective-permute-done | bytes 409632 | tf_op jit(solution)/shard_map/ppermute | solution.py:129
  23.2 1.9 %collective-permute-start.5 = (bf16[1600,128]{1,0:T(8,128)(2,1)S(1)}, bf16[1600,128]{1,0:T(8,128)(2,1)S(1)}, u32[]{:S(2)}, u32[]{:S(2)}) collective-permute-start(bf16[1600,128]{1,0:T(8,128)(2,1)S(1)} %collective-permute-done.3), channel_id=1, source_target_pairs={{0,2},{1,15},{2,4},{3,1},{4,6},{5,3},{6,8},{7,5},{8,10},{9,7},{10,... | collective-permute-start | bytes 1228808 | tf_op jit(solution)/shard_map/ppermute | solution.py:129
  25.1 2.4 %collective-permute-done.4 = bf16[1600,128]{1,0:T(8,128)(2,1)S(1)} collective-permute-done((bf16[1600,128]{1,0:T(8,128)(2,1)S(1)}, bf16[1600,128]{1,0:T(8,128)(2,1)S(1)}, u32[]{:S(2)}, u32[]{:S(2)}) %collective-permute-start.4) | collective-permute-done | bytes 409632 | tf_op jit(solution)/shard_map/ppermute | solution.py:129
  27.6 1.9 %collective-permute-start.6 = (bf16[1600,128]{1,0:T(8,128)(2,1)S(1)}, bf16[1600,128]{1,0:T(8,128)(2,1)S(1)}, u32[]{:S(2)}, u32[]{:S(2)}) collective-permute-start(bf16[1600,128]{1,0:T(8,128)(2,1)S(1)} %collective-permute-done.4), channel_id=1, source_target_pairs={{0,2},{1,15},{2,4},{3,1},{4,6},{5,3},{6,8},{7,5},{8,10},{9,7},{10,... | collective-permute-start | bytes 1228808 | tf_op jit(solution)/shard_map/ppermute | solution.py:129
  29.5 0.4 convolution_dynamic-update-slice_fusion.3
  30.4 1.7 %collective-permute-done.5 = bf16[1600,128]{1,0:T(8,128)(2,1)S(1)} collective-permute-done((bf16[1600,128]{1,0:T(8,128)(2,1)S(1)}, bf16[1600,128]{1,0:T(8,128)(2,1)S(1)}, u32[]{:S(2)}, u32[]{:S(2)}) %collective-permute-start.5) | collective-permute-done | bytes 409632 | tf_op jit(solution)/shard_map/ppermute | solution.py:129
  32.1 1.9 %collective-permute-start.7 = (bf16[1600,128]{1,0:T(8,128)(2,1)S(1)}, bf16[1600,128]{1,0:T(8,128)(2,1)S(1)}, u32[]{:S(2)}, u32[]{:S(2)}) collective-permute-start(bf16[1600,128]{1,0:T(8,128)(2,1)S(1)} %collective-permute-done.5), channel_id=1, source_target_pairs={{0,2},{1,15},{2,4},{3,1},{4,6},{5,3},{6,8},{7,5},{8,10},{9,7},{10,... | collective-permute-start | bytes 1228808 | tf_op jit(solution)/shard_map/ppermute | solution.py:129
  34.1 2.4 %collective-permute-done.6 = bf16[1600,128]{1,0:T(8,128)(2,1)S(1)} collective-permute-done((bf16[1600,128]{1,0:T(8,128)(2,1)S(1)}, bf16[1600,128]{1,0:T(8,128)(2,1)S(1)}, u32[]{:S(2)}, u32[]{:S(2)}) %collective-permute-start.6) | collective-permute-done | bytes 409632 | tf_op jit(solution)/shard_map/ppermute | solution.py:129
  36.5 1.9 %collective-permute-start.8 = (bf16[1600,128]{1,0:T(8,128)(2,1)S(1)}, bf16[1600,128]{1,0:T(8,128)(2,1)S(1)}, u32[]{:S(2)}, u32[]{:S(2)}) collective-permute-start(bf16[1600,128]{1,0:T(8,128)(2,1)S(1)} %collective-permute-done.6), channel_id=1, source_target_pairs={{0,2},{1,15},{2,4},{3,1},{4,6},{5,3},{6,8},{7,5},{8,10},{9,7},{10,... | collective-permute-start | bytes 1228808 | tf_op jit(solution)/shard_map/ppermute | solution.py:129
  39.4 2.5 %collective-permute-done.7 = bf16[1600,128]{1,0:T(8,128)(2,1)S(1)} collective-permute-done((bf16[1600,128]{1,0:T(8,128)(2,1)S(1)}, bf16[1600,128]{1,0:T(8,128)(2,1)S(1)}, u32[]{:S(2)}, u32[]{:S(2)}) %collective-permute-start.7) | collective-permute-done | bytes 409632 | tf_op jit(solution)/shard_map/ppermute | solution.py:129
  41.9 4.4 %collective-permute-done.8 = bf16[1600,128]{1,0:T(8,128)(2,1)S(1)} collective-permute-done((bf16[1600,128]{1,0:T(8,128)(2,1)S(1)}, bf16[1600,128]{1,0:T(8,128)(2,1)S(1)}, u32[]{:S(2)}, u32[]{:S(2)}) %collective-permute-start.8) | collective-permute-done | bytes 409632 | tf_op jit(solution)/shard_map/ppermute | solution.py:129
  47.0 15.1 %all_to_all.10 = f32[8,4,64,128]{3,2,1,0:T(8,128)S(1)} all-to-all(f32[8,4,64,128]{3,2,1,0:T(8,128)S(1)} %bitcast.68), channel_id=1, replica_groups={{0,384,400,256,272,128,144,16},{401,17,1,145,129,273,257,385},{130,2,18..., dimensions={0} | all-to-all | bytes 2097152 | tf_op jit(solution)/shard_map/all_to_all | solution.py:138
  62.2 16.2 %all_to_all.11 = f32[4,64,128]{2,1,0:T(8,128)S(1)} all-to-all(f32[4,64,128]{2,1,0:T(8,128)S(1)} %reduce_sum.18), channel_id=1, replica_groups={{0,32,64,96},{1,33,65,97},{66,98,2,34},{67,99,3,35},{4,36,68,100},{5,37..., dimensions={0} | all-to-all | bytes 262144 | tf_op jit(solution)/shard_map/all_to_all | solution.py:139
  78.4 13.6 %collective-permute-start.11 = (f32[64,128]{1,0:T(8,128)S(1)}, f32[64,128]{1,0:T(8,128)S(1)}, u32[]{:S(2)}, u32[]{:S(2)}) collective-permute-start(f32[64,128]{1,0:T(8,128)S(1)} %reduce_sum.19), channel_id=1, source_target_pairs={{64,1},{65,2},{81,3},{193,4},{209,5},{321,6},{337,7},{16,8},{80,9}... | collective-permute-start | bytes 98312 | tf_op jit(solution)/shard_map/ppermute | solution.py:142
  92.1 8.8 %collective-permute-start.10 = (f32[64,128]{0,1:T(8,128)S(1)}, f32[64,128]{0,1:T(8,128)S(1)}, u32[]{:S(2)}, u32[]{:S(2)}) collective-permute-start(f32[64,128]{0,1:T(8,128)S(1)} %copy.4), channel_id=1, source_target_pairs={{0,0},{465,1},{66,2},{2,3},{388,4},{452,5},{454,6},{390,7},{137,8}... | collective-permute-start | bytes 98312 | tf_op jit(solution)/shard_map/ppermute | solution.py:143
  100.9 1.9 %collective-permute-start.9 = (f32[64,128]{0,1:T(8,128)S(1)}, f32[64,128]{0,1:T(8,128)S(1)}, u32[]{:S(2)}, u32[]{:S(2)}) collective-permute-start(f32[64,128]{0,1:T(8,128)S(1)} %copy.4), channel_id=1, source_target_pairs={{32,0},{497,1},{98,2},{34,3},{420,4},{484,5},{486,6},{422,7},{169,... | collective-permute-start | bytes 98312 | tf_op jit(solution)/shard_map/ppermute | solution.py:144
  103.2 6.9 %collective-permute-done.9 = f32[64,128]{0,1:T(8,128)S(1)} collective-permute-done((f32[64,128]{0,1:T(8,128)S(1)}, f32[64,128]{0,1:T(8,128)S(1)}, u32[]{:S(2)}, u32[]{:S(2)}) %collective-permute-start.9) | collective-permute-done | bytes 32800 | tf_op jit(solution)/shard_map/ppermute | solution.py:144
  110.1 0.7 maximum_add_fusion
  (43 shorter events, 6.2 us)
Async XLA Ops:
  0.0 10.0 %copy-start.1 = (s32[8,32]{1,0:T(8,128)S(1)}, s32[8,32]{1,0:T(8,128)}, u32[]{:S(2)}) copy-start(s32[8,32]{1,0:T(8,128)} %param.3) | copy-start | bytes 3076
  1.2 12.5 %copy-start = (bf16[8,400,128]{2,1,0:T(8,128)(2,1)S(1)}, bf16[8,400,128]{2,1,0:T(8,128)(2,1)}, u32[]{:S(2)}) copy-start(bf16[8,400,128]{2,1,0:T(8,128)(2,1)} %param.2) | copy-start | bytes 2457604
  1.2 13.0 %collective-permute-start.1 = (bf16[1600,128]{1,0:T(8,128)(2,1)S(1)}, bf16[1600,128]{1,0:T(8,128)(2,1)S(1)}, u32[]{:S(2)}, u32[]{:S(2)}) collective-permute-start(bf16[1600,128]{1,0:T(8,128)(2,1)S(1)} %bitcast.66), channel_id=1, source_target_pairs={{0,2},{1,15},{2,4},{3,1},{4,6},{5,3},{6,8},{7,5},{8,10},{9,7},{10,... | collective-permute-start | bytes 1228808 | tf_op jit(solution)/shard_map/ppermute | solution.py:113
  3.4 12.7 %collective-permute-start.2 = (bf16[1600,128]{1,0:T(8,128)(2,1)S(1)}, bf16[1600,128]{1,0:T(8,128)(2,1)S(1)}, u32[]{:S(2)}, u32[]{:S(2)}) collective-permute-start(bf16[1600,128]{1,0:T(8,128)(2,1)S(1)} %bitcast.64), channel_id=1, source_target_pairs={{1,2},{0,15},{3,4},{2,1},{5,6},{4,3},{7,8},{6,5},{9,10},{8,7},{11,... | collective-permute-start | bytes 1228808 | tf_op jit(solution)/shard_map/ppermute | solution.py:113
  11.4 7.1 %collective-permute-start = (bf16[1600,128]{1,0:T(8,128)(2,1)S(1)}, bf16[1600,128]{1,0:T(8,128)(2,1)S(1)}, u32[]{:S(2)}, u32[]{:S(2)}) collective-permute-start(bf16[1600,128]{1,0:T(8,128)(2,1)S(1)} %bitcast_select_fusion.8), channel_id=1, source_target_pairs={{0,1},{1,0},{2,3},{3,2},{4,5},{5,4},{6,7},{7,6},{8,9},{9,8},{10,11... | collective-permute-start | bytes 1228808 | tf_op jit(solution)/shard_map/ppermute | solution.py:116
  14.2 9.0 %collective-permute-start.3 = (bf16[1600,128]{1,0:T(8,128)(2,1)S(1)}, bf16[1600,128]{1,0:T(8,128)(2,1)S(1)}, u32[]{:S(2)}, u32[]{:S(2)}) collective-permute-start(bf16[1600,128]{1,0:T(8,128)(2,1)S(1)} %collective-permute-done.1), channel_id=1, source_target_pairs={{0,2},{1,15},{2,4},{3,1},{4,6},{5,3},{6,8},{7,5},{8,10},{9,7},{10,... | collective-permute-start | bytes 1228808 | tf_op jit(solution)/shard_map/ppermute | solution.py:129
  16.2 11.4 %collective-permute-start.4 = (bf16[1600,128]{1,0:T(8,128)(2,1)S(1)}, bf16[1600,128]{1,0:T(8,128)(2,1)S(1)}, u32[]{:S(2)}, u32[]{:S(2)}) collective-permute-start(bf16[1600,128]{1,0:T(8,128)(2,1)S(1)} %collective-permute-done.2), channel_id=1, source_target_pairs={{0,2},{1,15},{2,4},{3,1},{4,6},{5,3},{6,8},{7,5},{8,10},{9,7},{10,... | collective-permute-start | bytes 1228808 | tf_op jit(solution)/shard_map/ppermute | solution.py:129
  23.2 9.0 %collective-permute-start.5 = (bf16[1600,128]{1,0:T(8,128)(2,1)S(1)}, bf16[1600,128]{1,0:T(8,128)(2,1)S(1)}, u32[]{:S(2)}, u32[]{:S(2)}) collective-permute-start(bf16[1600,128]{1,0:T(8,128)(2,1)S(1)} %collective-permute-done.3), channel_id=1, source_target_pairs={{0,2},{1,15},{2,4},{3,1},{4,6},{5,3},{6,8},{7,5},{8,10},{9,7},{10,... | collective-permute-start | bytes 1228808 | tf_op jit(solution)/shard_map/ppermute | solution.py:129
  27.6 9.0 %collective-permute-start.6 = (bf16[1600,128]{1,0:T(8,128)(2,1)S(1)}, bf16[1600,128]{1,0:T(8,128)(2,1)S(1)}, u32[]{:S(2)}, u32[]{:S(2)}) collective-permute-start(bf16[1600,128]{1,0:T(8,128)(2,1)S(1)} %collective-permute-done.4), channel_id=1, source_target_pairs={{0,2},{1,15},{2,4},{3,1},{4,6},{5,3},{6,8},{7,5},{8,10},{9,7},{10,... | collective-permute-start | bytes 1228808 | tf_op jit(solution)/shard_map/ppermute | solution.py:129
  32.1 9.8 %collective-permute-start.7 = (bf16[1600,128]{1,0:T(8,128)(2,1)S(1)}, bf16[1600,128]{1,0:T(8,128)(2,1)S(1)}, u32[]{:S(2)}, u32[]{:S(2)}) collective-permute-start(bf16[1600,128]{1,0:T(8,128)(2,1)S(1)} %collective-permute-done.5), channel_id=1, source_target_pairs={{0,2},{1,15},{2,4},{3,1},{4,6},{5,3},{6,8},{7,5},{8,10},{9,7},{10,... | collective-permute-start | bytes 1228808 | tf_op jit(solution)/shard_map/ppermute | solution.py:129
  36.5 9.8 %collective-permute-start.8 = (bf16[1600,128]{1,0:T(8,128)(2,1)S(1)}, bf16[1600,128]{1,0:T(8,128)(2,1)S(1)}, u32[]{:S(2)}, u32[]{:S(2)}) collective-permute-start(bf16[1600,128]{1,0:T(8,128)(2,1)S(1)} %collective-permute-done.6), channel_id=1, source_target_pairs={{0,2},{1,15},{2,4},{3,1},{4,6},{5,3},{6,8},{7,5},{8,10},{9,7},{10,... | collective-permute-start | bytes 1228808 | tf_op jit(solution)/shard_map/ppermute | solution.py:129
  78.4 24.5 %collective-permute-start.11 = (f32[64,128]{1,0:T(8,128)S(1)}, f32[64,128]{1,0:T(8,128)S(1)}, u32[]{:S(2)}, u32[]{:S(2)}) collective-permute-start(f32[64,128]{1,0:T(8,128)S(1)} %reduce_sum.19), channel_id=1, source_target_pairs={{64,1},{65,2},{81,3},{193,4},{209,5},{321,6},{337,7},{16,8},{80,9}... | collective-permute-start | bytes 98312 | tf_op jit(solution)/shard_map/ppermute | solution.py:142
  92.1 11.2 %collective-permute-start.10 = (f32[64,128]{0,1:T(8,128)S(1)}, f32[64,128]{0,1:T(8,128)S(1)}, u32[]{:S(2)}, u32[]{:S(2)}) collective-permute-start(f32[64,128]{0,1:T(8,128)S(1)} %copy.4), channel_id=1, source_target_pairs={{0,0},{465,1},{66,2},{2,3},{388,4},{452,5},{454,6},{390,7},{137,8}... | collective-permute-start | bytes 98312 | tf_op jit(solution)/shard_map/ppermute | solution.py:143
  100.9 9.2 %collective-permute-start.9 = (f32[64,128]{0,1:T(8,128)S(1)}, f32[64,128]{0,1:T(8,128)S(1)}, u32[]{:S(2)}, u32[]{:S(2)}) collective-permute-start(f32[64,128]{0,1:T(8,128)S(1)} %copy.4), channel_id=1, source_target_pairs={{32,0},{497,1},{98,2},{34,3},{420,4},{484,5},{486,6},{422,7},{169,... | collective-permute-start | bytes 98312 | tf_op jit(solution)/shard_map/ppermute | solution.py:144

commit v6 on v5

--- a/solution.py
+++ b/solution.py
@@ -13,17 +13,13 @@
     return aux * 2 * CHIPS + (chip % CHIPS) * 2 + core
 
 
-PLACES = {(s, e, f): (s - 1, f, e) for s in range(1, CHIPS // 2) for f in range(2) for e in range(2)}
-PLACES |= {(s, 0, f): (3, s // 4, f) for s in (0, 4) for f in range(2)}
-
-
-ORDER = [(3, 0)] + [(pair, m) for pair in range(3) for m in range(2)] + [(3, 1)]
+PLACES = {(0, 0): (0, 0), (1, 1): (0, 1), (2, 1): (1, 0), (3, 1): (1, 1)}
+PLACES |= {(4, 0): (2, 0), (3, 0): (2, 1), (2, 0): (3, 0), (1, 0): (3, 1)}
+PAIRS = [0, 3, 1, 2]
 
 
 def first_holder(Y, core, pair):
-    if core:
-        return (Y + 1 + 2 * pair) % CHIPS // 2
-    return (Y - 1 - 2 * pair) % CHIPS // 2
+    return (Y + (-2 * pair if core else 2 * pair)) % CHIPS // 2
 
 
 def second_holder(Y, q, g):
@@ -31,23 +27,24 @@
 
 
 def holder(Y, core, tile, g):
-    pair, m, q = PLACES[tile]
-    return dev(first_holder(Y, core, pair) * AZ + 2 * second_holder(Y, q, g) + (core ^ m), Y, core)
+    pair, q = PLACES[tile[:2]]
+    return dev(first_holder(Y, core, pair) * AZ + 2 * second_holder(Y, q, g) + (core ^ tile[2]), Y, core)
 
 
 def summing_groups():
     rows = [(Y, c) for Y in range(CHIPS) for c in range(2)]
     first = [
-        [dev(first_holder(Y, c, pair) * AZ + 2 * k + (c ^ m), Y, c) for pair, m in ORDER]
+        [dev(first_holder(Y, c, pair) * AZ + 2 * k + (c ^ m), Y, c) for pair in PAIRS for m in range(2)]
         for k in range(AZ // 2)
         for Y, c in rows
     ]
-    second = [
-        [dev(x * AZ + 2 * second_holder(Y, q, g) + m, Y, c) for q in range(2) for g in range(2)]
-        for x in range(AX)
-        for m in range(2)
-        for Y, c in rows
-    ]
+    second = []
+    for x in range(AX):
+        for m in range(2):
+            for Y, c in rows:
+                pair = next(p for p in PAIRS if first_holder(Y, c, p) == x)
+                qs = (1, 0) if pair > 1 else (0, 1)
+                second.append([dev(x * AZ + 2 * second_holder(Y, q, g) + m, Y, c) for q in qs for g in range(2)])
     return first, second
 
 
@@ -114,25 +111,30 @@
     masked = jnp.where(mask_of(0, aux_here, row), slabs, jnp.zeros_like(slabs))
     own = masked_half(a, row)
     other = lax.ppermute(masked_half(b, row, 1 - core), "row", swap)
-    left = jnp.concatenate([own.T, other.T], axis=0)
+    left = (own.T, other.T)
     whole = masked.reshape(2 * depth, cols)
 
     def dot(x, y):
         return jnp.dot(x, y, preferred_element_type=jnp.float32)
 
-    tiles = [dot(whole.T, whole), dot(own.T, other)]
+    tiles = {(0, 0, 0): dot(whole.T, whole), (0, 0, 1): dot(left[0], other)}
     for step in range(1, CHIPS // 2 + 1):
         there = (chip + jnp.where(core == 0, CHIPS - step, step)) % CHIPS
         near_a = masked_half(far_a, 2 * there + core)
         near_b = masked_half(far_b, 2 * there + 1 - core)
         if step < CHIPS // 2:
             far_a, far_b = lax.ppermute(far_a, "row", ring), lax.ppermute(far_b, "row", ring)
-            tiles += [dot(left, near_a), dot(left, near_b)]
+            for e in range(2):
+                tiles[step, e, 0], tiles[step, e, 1] = dot(left[e], near_a), dot(left[e], near_b)
         else:
             low = chip < CHIPS // 2
-            tiles.append(dot(jnp.where(low, left[:cols], left[cols:]), jnp.where(low, near_a, near_b)))
-            tiles.append(dot(left[:cols], near_b))
-    pieces = jnp.concatenate(tiles, axis=0).reshape(2 * AX, AZ // 2, BS, cols)
+            tiles[4, 0, 0] = dot(jnp.where(low, left[0], left[1]), jnp.where(low, near_a, near_b))
+            tiles[4, 0, 1] = dot(left[0], near_b)
+    at = {place: tile for tile, place in PLACES.items()}
+    pieces = [
+        tiles[(*at[pair, q], m)] for pair in PAIRS for m in range(2) for q in ((1, 0) if pair > 1 else (0, 1))
+    ]
+    pieces = jnp.concatenate(pieces, axis=0).reshape(2 * AX, AZ // 2, BS, cols)
 
     first, second = summing_groups()
     got = lax.all_to_all(pieces, BOTH, 0, 0, axis_index_groups=first, tiled=True).sum(axis=0)

time: 111 us -> 108 us (0.973)
  the two profiles are of different devices: /device:TPU:23 before, /device:TPU:10 now
where the time goes in v6:
time: 108 us
  starting transfers between devices  52.8 us (49%)
  blocking collectives  32.2 us (30%)
  waiting for transfers between devices  12.4 us (11%)
  matrix products  5.23 us (5%)
  local copies, waits for them, and re-layouts  3.38 us (3%)
  other arithmetic  1.36 us (1%)
    all_to_all x1, blocking collectives, local(): lax.all_to_all(pieces, BOTH, 0, 0, axis_index_groups=first, tiled=True)  19.4 us
    ppermute x3, starting transfers between devices, local(): lax.ppermute(far_a, 'row', ring)  14.3 us
    all_to_all x1, blocking collectives, local(): lax.all_to_all(got, BOTH, 0, 0, axis_index_groups=second, tiled=True)  12.8 us
    ppermute x3, starting transfers between devices, local(): lax.ppermute(far_b, 'row', ring)  10.3 us
    ppermute x1, starting transfers between devices, local(): d0 = lax.ppermute(got, BOTH, near)  9.53 us
    ppermute x1, starting transfers between devices, local(): t = lax.optimization_barrier(lax.ppermute(got, BOTH, mirrored).T)  7.65 us
    ppermute x2, starting transfers between devices, local(): far_a, far_b = (lax.ppermute(a, 'row', ring), lax.ppermute(b, 'row', cross))  6.89 us
    ppermute x1, waiting for transfers between devices, local(): d1 = lax.ppermute(got, BOTH, next_to)  5.42 us
  transfers between devices with their start and end apart: 12, of which 5 were waited for; matrix products, arithmetic and copies ran while one was open for 6% of the time, Pallas kernels for 0%

profile of v6, /device:TPU:10, one launch (start us, length us, event | category | flops | bytes accessed | tf_op | source)
XLA Modules:
  0.0 107.9 jit_solution(4827336856362413025)
XLA Ops:
  0.0 1.2 %constant_dynamic-slice_fusion = (bf16[4,400,128]{2,1,0:T(8,128)(2,1)S(1)}, bf16[4,400,128]{2,1,0:T(8,128)(2,1)S(1)}) fusion(bf16[8,400,128]{2,1,0:T(8,128)(2,1)} %param.2, s32[]{:T(128)S(6)} %select_n.289, s32[]{:T(128)S(6)} %select_n.291), kind=kLoop, calls=%fused_computation.73 | loop fusion | bytes 1638408 | tf_op jit(solution)/shard_map/dynamic_slice | solution.py:100
  1.2 3.5 %collective-permute-start.1 = (bf16[1600,128]{1,0:T(8,128)(2,1)S(1)}, bf16[1600,128]{1,0:T(8,128)(2,1)S(1)}, u32[]{:S(2)}, u32[]{:S(2)}) collective-permute-start(bf16[1600,128]{1,0:T(8,128)(2,1)S(1)} %bitcast.62), channel_id=1, source_target_pairs={{0,2},{1,15},{2,4},{3,1},{4,6},{5,3},{6,8},{7,5},{8,10},{9,7},{10,... | collective-permute-start | bytes 1228808 | tf_op jit(solution)/shard_map/ppermute | solution.py:110
  4.7 3.4 %collective-permute-start.2 = (bf16[1600,128]{1,0:T(8,128)(2,1)S(1)}, bf16[1600,128]{1,0:T(8,128)(2,1)S(1)}, u32[]{:S(2)}, u32[]{:S(2)}) collective-permute-start(bf16[1600,128]{1,0:T(8,128)(2,1)S(1)} %bitcast.60), channel_id=1, source_target_pairs={{1,2},{0,15},{3,4},{2,1},{5,6},{4,3},{7,8},{6,5},{9,10},{8,7},{11,... | collective-permute-start | bytes 1228808 | tf_op jit(solution)/shard_map/ppermute | solution.py:110
  8.3 0.7 copy-done.1
  9.4 2.2 %collective-permute-start = (bf16[1600,128]{1,0:T(8,128)(2,1)S(1)}, bf16[1600,128]{1,0:T(8,128)(2,1)S(1)}, u32[]{:S(2)}, u32[]{:S(2)}) collective-permute-start(bf16[1600,128]{1,0:T(8,128)(2,1)S(1)} %bitcast_select_fusion.9), channel_id=1, source_target_pairs={{0,1},{1,0},{2,3},{3,2},{4,5},{5,4},{6,7},{7,6},{8,9},{9,8},{10,11... | collective-permute-start | bytes 1228808 | tf_op jit(solution)/shard_map/ppermute | solution.py:113
  13.0 0.4 fusion
  13.4 4.7 %collective-permute-start.3 = (bf16[1600,128]{1,0:T(8,128)(2,1)S(1)}, bf16[1600,128]{1,0:T(8,128)(2,1)S(1)}, u32[]{:S(2)}, u32[]{:S(2)}) collective-permute-start(bf16[1600,128]{1,0:T(8,128)(2,1)S(1)} %collective-permute-done.1), channel_id=1, source_target_pairs={{0,2},{1,15},{2,4},{3,1},{4,6},{5,3},{6,8},{7,5},{8,10},{9,7},{10,... | collective-permute-start | bytes 1228808 | tf_op jit(solution)/shard_map/ppermute | solution.py:126
  18.2 2.6 %collective-permute-start.4 = (bf16[1600,128]{1,0:T(8,128)(2,1)S(1)}, bf16[1600,128]{1,0:T(8,128)(2,1)S(1)}, u32[]{:S(2)}, u32[]{:S(2)}) collective-permute-start(bf16[1600,128]{1,0:T(8,128)(2,1)S(1)} %collective-permute-done.2), channel_id=1, source_target_pairs={{0,2},{1,15},{2,4},{3,1},{4,6},{5,3},{6,8},{7,5},{8,10},{9,7},{10,... | collective-permute-start | bytes 1228808 | tf_op jit(solution)/shard_map/ppermute | solution.py:126
  22.1 1.4 %collective-permute-done.3 = bf16[1600,128]{1,0:T(8,128)(2,1)S(1)} collective-permute-done((bf16[1600,128]{1,0:T(8,128)(2,1)S(1)}, bf16[1600,128]{1,0:T(8,128)(2,1)S(1)}, u32[]{:S(2)}, u32[]{:S(2)}) %collective-permute-start.3) | collective-permute-done | bytes 409632 | tf_op jit(solution)/shard_map/ppermute | solution.py:126
  23.6 4.4 %collective-permute-start.5 = (bf16[1600,128]{1,0:T(8,128)(2,1)S(1)}, bf16[1600,128]{1,0:T(8,128)(2,1)S(1)}, u32[]{:S(2)}, u32[]{:S(2)}) collective-permute-start(bf16[1600,128]{1,0:T(8,128)(2,1)S(1)} %collective-permute-done.3), channel_id=1, source_target_pairs={{0,2},{1,15},{2,4},{3,1},{4,6},{5,3},{6,8},{7,5},{8,10},{9,7},{10,... | collective-permute-start | bytes 1228808 | tf_op jit(solution)/shard_map/ppermute | solution.py:126
  28.7 3.7 %collective-permute-start.6 = (bf16[1600,128]{1,0:T(8,128)(2,1)S(1)}, bf16[1600,128]{1,0:T(8,128)(2,1)S(1)}, u32[]{:S(2)}, u32[]{:S(2)}) collective-permute-start(bf16[1600,128]{1,0:T(8,128)(2,1)S(1)} %collective-permute-done.4), channel_id=1, source_target_pairs={{0,2},{1,15},{2,4},{3,1},{4,6},{5,3},{6,8},{7,5},{8,10},{9,7},{10,... | collective-permute-start | bytes 1228808 | tf_op jit(solution)/shard_map/ppermute | solution.py:126
  33.1 0.4 collective-permute-done.5
  33.5 5.2 %collective-permute-start.7 = (bf16[1600,128]{1,0:T(8,128)(2,1)S(1)}, bf16[1600,128]{1,0:T(8,128)(2,1)S(1)}, u32[]{:S(2)}, u32[]{:S(2)}) collective-permute-start(bf16[1600,128]{1,0:T(8,128)(2,1)S(1)} %collective-permute-done.5), channel_id=1, source_target_pairs={{0,2},{1,15},{2,4},{3,1},{4,6},{5,3},{6,8},{7,5},{8,10},{9,7},{10,... | collective-permute-start | bytes 1228808 | tf_op jit(solution)/shard_map/ppermute | solution.py:126
  39.4 4.0 %collective-permute-start.8 = (bf16[1600,128]{1,0:T(8,128)(2,1)S(1)}, bf16[1600,128]{1,0:T(8,128)(2,1)S(1)}, u32[]{:S(2)}, u32[]{:S(2)}) collective-permute-start(bf16[1600,128]{1,0:T(8,128)(2,1)S(1)} %collective-permute-done.6), channel_id=1, source_target_pairs={{0,2},{1,15},{2,4},{3,1},{4,6},{5,3},{6,8},{7,5},{8,10},{9,7},{10,... | collective-permute-start | bytes 1228808 | tf_op jit(solution)/shard_map/ppermute | solution.py:126
  44.1 0.4 collective-permute-done.7
  44.5 4.7 %collective-permute-done.8 = bf16[1600,128]{1,0:T(8,128)(2,1)S(1)} collective-permute-done((bf16[1600,128]{1,0:T(8,128)(2,1)S(1)}, bf16[1600,128]{1,0:T(8,128)(2,1)S(1)}, u32[]{:S(2)}, u32[]{:S(2)}) %collective-permute-start.8) | collective-permute-done | bytes 409632 | tf_op jit(solution)/shard_map/ppermute | solution.py:126
  49.3 0.3 convolution_dynamic-update-slice_fusion.2
  50.3 19.4 %all_to_all.10 = f32[8,4,64,128]{3,2,1,0:T(8,128)S(1)} all-to-all(f32[8,4,64,128]{3,2,1,0:T(8,128)S(1)} %bitcast.64), channel_id=1, replica_groups={{0,16,384,400,128,144,256,272},{17,1,145,129,401,385,273,257},{2,18,386..., dimensions={0} | all-to-all | bytes 2097152 | tf_op jit(solution)/shard_map/all_to_all | solution.py:140
  69.7 12.8 %all_to_all.11 = f32[4,64,128]{2,1,0:T(8,128)S(1)} all-to-all(f32[4,64,128]{2,1,0:T(8,128)S(1)} %reduce_sum.18), channel_id=1, replica_groups={{0,32,64,96},{1,33,65,97},{66,98,2,34},{67,99,3,35},{68,100,4,36},{5,37..., dimensions={0} | all-to-all | bytes 262144 | tf_op jit(solution)/shard_map/all_to_all | solution.py:141
  82.5 7.6 %collective-permute-start.11 = (f32[64,128]{1,0:T(8,128)S(1)}, f32[64,128]{1,0:T(8,128)S(1)}, u32[]{:S(2)}, u32[]{:S(2)}) collective-permute-start(f32[64,128]{1,0:T(8,128)S(1)} %reduce_sum.19), channel_id=1, source_target_pairs={{16,1},{65,2},{81,3},{385,4},{401,5},{449,6},{465,7},{256,8},{272,... | collective-permute-start | bytes 98312 | tf_op jit(solution)/shard_map/ppermute | solution.py:144
  90.3 9.5 %collective-permute-start.10 = (f32[64,128]{0,1:T(8,128)S(1)}, f32[64,128]{0,1:T(8,128)S(1)}, u32[]{:S(2)}, u32[]{:S(2)}) collective-permute-start(f32[64,128]{0,1:T(8,128)S(1)} %copy.4), channel_id=1, source_target_pairs={{0,0},{1,1},{386,2},{2,3},{4,4},{260,5},{390,6},{262,7},{25,8},{9,... | collective-permute-start | bytes 98312 | tf_op jit(solution)/shard_map/ppermute | solution.py:145
  99.8 1.9 %collective-permute-start.9 = (f32[64,128]{0,1:T(8,128)S(1)}, f32[64,128]{0,1:T(8,128)S(1)}, u32[]{:S(2)}, u32[]{:S(2)}) collective-permute-start(f32[64,128]{0,1:T(8,128)S(1)} %copy.4), channel_id=1, source_target_pairs={{32,0},{33,1},{418,2},{34,3},{36,4},{292,5},{422,6},{294,7},{57,8}... | collective-permute-start | bytes 98312 | tf_op jit(solution)/shard_map/ppermute | solution.py:146
  101.8 5.4 %collective-permute-done.9 = f32[64,128]{0,1:T(8,128)S(1)} collective-permute-done((f32[64,128]{0,1:T(8,128)S(1)}, f32[64,128]{0,1:T(8,128)S(1)}, u32[]{:S(2)}, u32[]{:S(2)}) %collective-permute-start.9) | collective-permute-done | bytes 32800 | tf_op jit(solution)/shard_map/ppermute | solution.py:146
  107.2 0.7 maximum_add_fusion
  (49 shorter events, 6.7 us)
Async XLA Ops:
  1.2 12.2 %collective-permute-start.1 = (bf16[1600,128]{1,0:T(8,128)(2,1)S(1)}, bf16[1600,128]{1,0:T(8,128)(2,1)S(1)}, u32[]{:S(2)}, u32[]{:S(2)}) collective-permute-start(bf16[1600,128]{1,0:T(8,128)(2,1)S(1)} %bitcast.62), channel_id=1, source_target_pairs={{0,2},{1,15},{2,4},{3,1},{4,6},{5,3},{6,8},{7,5},{8,10},{9,7},{10,... | collective-permute-start | bytes 1228808 | tf_op jit(solution)/shard_map/ppermute | solution.py:110
  4.7 13.5 %collective-permute-start.2 = (bf16[1600,128]{1,0:T(8,128)(2,1)S(1)}, bf16[1600,128]{1,0:T(8,128)(2,1)S(1)}, u32[]{:S(2)}, u32[]{:S(2)}) collective-permute-start(bf16[1600,128]{1,0:T(8,128)(2,1)S(1)} %bitcast.60), channel_id=1, source_target_pairs={{1,2},{0,15},{3,4},{2,1},{5,6},{4,3},{7,8},{6,5},{9,10},{8,7},{11,... | collective-permute-start | bytes 1228808 | tf_op jit(solution)/shard_map/ppermute | solution.py:110
  8.3 0.7 copy-start.1
  9.3 3.6 %copy-start = (bf16[8,400,128]{2,1,0:T(8,128)(2,1)S(1)}, bf16[8,400,128]{2,1,0:T(8,128)(2,1)}, u32[]{:S(2)}) copy-start(bf16[8,400,128]{2,1,0:T(8,128)(2,1)} %param.2) | copy-start | bytes 2457604
  9.4 11.4 %collective-permute-start = (bf16[1600,128]{1,0:T(8,128)(2,1)S(1)}, bf16[1600,128]{1,0:T(8,128)(2,1)S(1)}, u32[]{:S(2)}, u32[]{:S(2)}) collective-permute-start(bf16[1600,128]{1,0:T(8,128)(2,1)S(1)} %bitcast_select_fusion.9), channel_id=1, source_target_pairs={{0,1},{1,0},{2,3},{3,2},{4,5},{5,4},{6,7},{7,6},{8,9},{9,8},{10,11... | collective-permute-start | bytes 1228808 | tf_op jit(solution)/shard_map/ppermute | solution.py:113
  13.4 10.2 %collective-permute-start.3 = (bf16[1600,128]{1,0:T(8,128)(2,1)S(1)}, bf16[1600,128]{1,0:T(8,128)(2,1)S(1)}, u32[]{:S(2)}, u32[]{:S(2)}) collective-permute-start(bf16[1600,128]{1,0:T(8,128)(2,1)S(1)} %collective-permute-done.1), channel_id=1, source_target_pairs={{0,2},{1,15},{2,4},{3,1},{4,6},{5,3},{6,8},{7,5},{8,10},{9,7},{10,... | collective-permute-start | bytes 1228808 | tf_op jit(solution)/shard_map/ppermute | solution.py:126
  18.2 10.5 %collective-permute-start.4 = (bf16[1600,128]{1,0:T(8,128)(2,1)S(1)}, bf16[1600,128]{1,0:T(8,128)(2,1)S(1)}, u32[]{:S(2)}, u32[]{:S(2)}) collective-permute-start(bf16[1600,128]{1,0:T(8,128)(2,1)S(1)} %collective-permute-done.2), channel_id=1, source_target_pairs={{0,2},{1,15},{2,4},{3,1},{4,6},{5,3},{6,8},{7,5},{8,10},{9,7},{10,... | collective-permute-start | bytes 1228808 | tf_op jit(solution)/shard_map/ppermute | solution.py:126
  23.6 9.9 %collective-permute-start.5 = (bf16[1600,128]{1,0:T(8,128)(2,1)S(1)}, bf16[1600,128]{1,0:T(8,128)(2,1)S(1)}, u32[]{:S(2)}, u32[]{:S(2)}) collective-permute-start(bf16[1600,128]{1,0:T(8,128)(2,1)S(1)} %collective-permute-done.3), channel_id=1, source_target_pairs={{0,2},{1,15},{2,4},{3,1},{4,6},{5,3},{6,8},{7,5},{8,10},{9,7},{10,... | collective-permute-start | bytes 1228808 | tf_op jit(solution)/shard_map/ppermute | solution.py:126
  28.7 10.7 %collective-permute-start.6 = (bf16[1600,128]{1,0:T(8,128)(2,1)S(1)}, bf16[1600,128]{1,0:T(8,128)(2,1)S(1)}, u32[]{:S(2)}, u32[]{:S(2)}) collective-permute-start(bf16[1600,128]{1,0:T(8,128)(2,1)S(1)} %collective-permute-done.4), channel_id=1, source_target_pairs={{0,2},{1,15},{2,4},{3,1},{4,6},{5,3},{6,8},{7,5},{8,10},{9,7},{10,... | collective-permute-start | bytes 1228808 | tf_op jit(solution)/shard_map/ppermute | solution.py:126
  33.5 11.0 %collective-permute-start.7 = (bf16[1600,128]{1,0:T(8,128)(2,1)S(1)}, bf16[1600,128]{1,0:T(8,128)(2,1)S(1)}, u32[]{:S(2)}, u32[]{:S(2)}) collective-permute-start(bf16[1600,128]{1,0:T(8,128)(2,1)S(1)} %collective-permute-done.5), channel_id=1, source_target_pairs={{0,2},{1,15},{2,4},{3,1},{4,6},{5,3},{6,8},{7,5},{8,10},{9,7},{10,... | collective-permute-start | bytes 1228808 | tf_op jit(solution)/shard_map/ppermute | solution.py:126
  39.4 9.8 %collective-permute-start.8 = (bf16[1600,128]{1,0:T(8,128)(2,1)S(1)}, bf16[1600,128]{1,0:T(8,128)(2,1)S(1)}, u32[]{:S(2)}, u32[]{:S(2)}) collective-permute-start(bf16[1600,128]{1,0:T(8,128)(2,1)S(1)} %collective-permute-done.6), channel_id=1, source_target_pairs={{0,2},{1,15},{2,4},{3,1},{4,6},{5,3},{6,8},{7,5},{8,10},{9,7},{10,... | collective-permute-start | bytes 1228808 | tf_op jit(solution)/shard_map/ppermute | solution.py:126
  82.5 19.2 %collective-permute-start.11 = (f32[64,128]{1,0:T(8,128)S(1)}, f32[64,128]{1,0:T(8,128)S(1)}, u32[]{:S(2)}, u32[]{:S(2)}) collective-permute-start(f32[64,128]{1,0:T(8,128)S(1)} %reduce_sum.19), channel_id=1, source_target_pairs={{16,1},{65,2},{81,3},{385,4},{401,5},{449,6},{465,7},{256,8},{272,... | collective-permute-start | bytes 98312 | tf_op jit(solution)/shard_map/ppermute | solution.py:144
  90.3 11.5 %collective-permute-start.10 = (f32[64,128]{0,1:T(8,128)S(1)}, f32[64,128]{0,1:T(8,128)S(1)}, u32[]{:S(2)}, u32[]{:S(2)}) collective-permute-start(f32[64,128]{0,1:T(8,128)S(1)} %copy.4), channel_id=1, source_target_pairs={{0,0},{1,1},{386,2},{2,3},{4,4},{260,5},{390,6},{262,7},{25,8},{9,... | collective-permute-start | bytes 98312 | tf_op jit(solution)/shard_map/ppermute | solution.py:145
  99.8 7.4 %collective-permute-start.9 = (f32[64,128]{0,1:T(8,128)S(1)}, f32[64,128]{0,1:T(8,128)S(1)}, u32[]{:S(2)}, u32[]{:S(2)}) collective-permute-start(f32[64,128]{0,1:T(8,128)S(1)} %copy.4), channel_id=1, source_target_pairs={{32,0},{33,1},{418,2},{34,3},{36,4},{292,5},{422,6},{294,7},{57,8}... | collective-permute-start | bytes 98312 | tf_op jit(solution)/shard_map/ppermute | solution.py:146

commit v7 on v6

--- a/solution.py
+++ b/solution.py
@@ -1,3 +1,6 @@
+import functools
+import itertools
+
 import jax
 import jax.numpy as jnp
 from jax import lax
@@ -16,36 +19,7 @@
 PLACES = {(0, 0): (0, 0), (1, 1): (0, 1), (2, 1): (1, 0), (3, 1): (1, 1)}
 PLACES |= {(4, 0): (2, 0), (3, 0): (2, 1), (2, 0): (3, 0), (1, 0): (3, 1)}
 PAIRS = [0, 3, 1, 2]
-
-
-def first_holder(Y, core, pair):
-    return (Y + (-2 * pair if core else 2 * pair)) % CHIPS // 2
-
-
-def second_holder(Y, q, g):
-    return 2 * ((Y + q) % 2) + g
-
-
-def holder(Y, core, tile, g):
-    pair, q = PLACES[tile[:2]]
-    return dev(first_holder(Y, core, pair) * AZ + 2 * second_holder(Y, q, g) + (core ^ tile[2]), Y, core)
-
-
-def summing_groups():
-    rows = [(Y, c) for Y in range(CHIPS) for c in range(2)]
-    first = [
-        [dev(first_holder(Y, c, pair) * AZ + 2 * k + (c ^ m), Y, c) for pair in PAIRS for m in range(2)]
-        for k in range(AZ // 2)
-        for Y, c in rows
-    ]
-    second = []
-    for x in range(AX):
-        for m in range(2):
-            for Y, c in rows:
-                pair = next(p for p in PAIRS if first_holder(Y, c, p) == x)
-                qs = (1, 0) if pair > 1 else (0, 1)
-                second.append([dev(x * AZ + 2 * second_holder(Y, q, g) + m, Y, c) for q in qs for g in range(2)])
-    return first, second
+POWER, MIRRORED = 2, 1.0
 
 
 def sources(X, j, Y, i):
@@ -60,6 +34,76 @@
     s, here = (d, 1) if d < CHIPS // 2 else (CHIPS - d, 0)
     there = 1 - here
     return (here, (s, int(i != here), int(j != here))), (there, (s, int(j != there), int(i != there)))
+
+
+def chunks():
+    at = {place: tile for tile, place in PLACES.items()}
+    return [
+        [((*at[pair, q], m), g) for q in ((1, 0) if pair > 1 else (0, 1)) for g in range(2)]
+        for pair in PAIRS
+        for m in range(2)
+    ]
+
+
+def hops(a, b):
+    ends = [(aux // AZ, aux % AZ, row // 2) for aux, row in (a, b)]
+    far = [min((u - v) % n, (v - u) % n) for u, v, n in zip(*ends, (AX, AZ, CHIPS))]
+    return sum(far) + 0.5 * (a[1] % 2 != b[1] % 2)
+
+
+@functools.cache
+def owners():
+    to = {}
+    for A in range(AX * AZ):
+        X, j, h = A // 4, A // 2 % 2, A % 2
+        for Y in range(CHIPS):
+            for i in range(2):
+                (core, tile), other = sources(X, j, Y, i)
+                for g in range(2):
+                    to.setdefault((Y, core, tile, g), []).append((1.0, (A, 2 * Y + i)))
+                if other is not None:
+                    to.setdefault((X, *other, h), []).append((MIRRORED, (A, 2 * Y + i)))
+    return to
+
+
+@functools.cache
+def layout(Y, core):
+    spots = [(x, m) for x in range(AX) for m in range(2)]
+
+    def cost(piece, x, m, k):
+        tile, g = piece
+        at = (x * AZ + 2 * k + m, 2 * Y + core)
+        return sum(w * hops(at, to) ** POWER for w, to in owners()[Y, core, tile, g])
+
+    best = {0: (0.0, [])}
+    for chunk in chunks():
+        options = []
+        for x, m in spots:
+            table = [[cost(piece, x, m, k) for k in range(AZ // 2)] for piece in chunk]
+            options.append(min((sum(table[p][k] for p, k in enumerate(order)), order) for order in itertools.permutations(range(AZ // 2))))
+        after = {}
+        for used, (total, chosen) in best.items():
+            for n, (more, order) in enumerate(options):
+                if not used >> n & 1:
+                    found = (total + more, [*chosen, (*spots[n], order)])
+                    now = used | 1 << n
+                    if now not in after or found < after[now]:
+                        after[now] = found
+        best = after
+    return best[2 ** len(spots) - 1][1]
+
+
+def holder(Y, core, tile, g):
+    for chunk, (x, m, order) in zip(chunks(), layout(Y, core)):
+        if (tile, g) in chunk:
+            return dev(x * AZ + 2 * order[chunk.index((tile, g))] + m, Y, core)
+
+
+def summing_groups():
+    rows = [(Y, c) for Y in range(CHIPS) for c in range(2)]
+    first = [[dev(x * AZ + 2 * k + m, Y, c) for x, m, _ in layout(Y, c)] for k in range(AZ // 2) for Y, c in rows]
+    second = [[dev(x * AZ + 2 * k + m, Y, c) for k in order] for Y, c in rows for x, m, order in layout(Y, c)]
+    return first, second
 
 
 def deliveries():
@@ -130,10 +174,7 @@
             low = chip < CHIPS // 2
             tiles[4, 0, 0] = dot(jnp.where(low, left[0], left[1]), jnp.where(low, near_a, near_b))
             tiles[4, 0, 1] = dot(left[0], near_b)
-    at = {place: tile for tile, place in PLACES.items()}
-    pieces = [
-        tiles[(*at[pair, q], m)] for pair in PAIRS for m in range(2) for q in ((1, 0) if pair > 1 else (0, 1))
-    ]
+    pieces = [tiles[tile] for chunk in chunks() for tile, g in chunk if g == 0]
     pieces = jnp.concatenate(pieces, axis=0).reshape(2 * AX, AZ // 2, BS, cols)
 
     first, second = summing_groups()

time: 108 us -> 107 us (level)
  the two profiles are of different devices: /device:TPU:10 before, /device:TPU:14 now
where the time goes in v7:
time: 107 us; the launch traced here: 106 us
  starting transfers between devices  51.5 us (48%)
  blocking collectives  30.9 us (29%)
  waiting for transfers between devices  13.3 us (12%)
  matrix products  5.23 us (5%)
  local copies, waits for them, and re-layouts  3.38 us (3%)
  other arithmetic  1.36 us (1%)
    all_to_all x1, blocking collectives, local(): lax.all_to_all(pieces, BOTH, 0, 0, axis_index_groups=first, tiled=True)  17.9 us
    ppermute x3, starting transfers between devices, local(): lax.ppermute(far_a, 'row', ring)  14.3 us
    all_to_all x1, blocking collectives, local(): lax.all_to_all(got, BOTH, 0, 0, axis_index_groups=second, tiled=True)  12.9 us
    ppermute x3, starting transfers between devices, local(): lax.ppermute(far_b, 'row', ring)  10.3 us
    ppermute x1, starting transfers between devices, local(): t = lax.optimization_barrier(lax.ppermute(got, BOTH, mirrored).T)  8.15 us
    ppermute x1, starting transfers between devices, local(): d0 = lax.ppermute(got, BOTH, near)  7.72 us
    ppermute x2, starting transfers between devices, local(): far_a, far_b = (lax.ppermute(a, 'row', ring), lax.ppermute(b, 'row', cross))  6.89 us
    ppermute x1, waiting for transfers between devices, local(): d1 = lax.ppermute(got, BOTH, next_to)  6.31 us
  transfers between devices with their start and end apart: 12, of which 5 were waited for; matrix products, arithmetic and copies ran while one was open for 6% of the time, Pallas kernels for 0%

profile of v7, /device:TPU:14, one launch (start us, length us, event | category | flops | bytes accessed | tf_op | source)
XLA Modules:
  0.0 106.2 jit_solution(3663658839230509635)
XLA Ops:
  0.0 1.2 %constant_dynamic-slice_fusion = (bf16[4,400,128]{2,1,0:T(8,128)(2,1)S(1)}, bf16[4,400,128]{2,1,0:T(8,128)(2,1)S(1)}) fusion(bf16[8,400,128]{2,1,0:T(8,128)(2,1)} %param.2, s32[]{:T(128)S(6)} %select_n.289, s32[]{:T(128)S(6)} %select_n.291), kind=kLoop, calls=%fused_computation.73 | loop fusion | bytes 1638408 | tf_op jit(solution)/shard_map/dynamic_slice | solution.py:144
  1.2 3.5 %collective-permute-start.1 = (bf16[1600,128]{1,0:T(8,128)(2,1)S(1)}, bf16[1600,128]{1,0:T(8,128)(2,1)S(1)}, u32[]{:S(2)}, u32[]{:S(2)}) collective-permute-start(bf16[1600,128]{1,0:T(8,128)(2,1)S(1)} %bitcast.62), channel_id=1, source_target_pairs={{0,2},{1,15},{2,4},{3,1},{4,6},{5,3},{6,8},{7,5},{8,10},{9,7},{10,... | collective-permute-start | bytes 1228808 | tf_op jit(solution)/shard_map/ppermute | solution.py:154
  4.7 3.4 %collective-permute-start.2 = (bf16[1600,128]{1,0:T(8,128)(2,1)S(1)}, bf16[1600,128]{1,0:T(8,128)(2,1)S(1)}, u32[]{:S(2)}, u32[]{:S(2)}) collective-permute-start(bf16[1600,128]{1,0:T(8,128)(2,1)S(1)} %bitcast.60), channel_id=1, source_target_pairs={{1,2},{0,15},{3,4},{2,1},{5,6},{4,3},{7,8},{6,5},{9,10},{8,7},{11,... | collective-permute-start | bytes 1228808 | tf_op jit(solution)/shard_map/ppermute | solution.py:154
  8.3 0.7 copy-done.1
  9.4 2.2 %collective-permute-start = (bf16[1600,128]{1,0:T(8,128)(2,1)S(1)}, bf16[1600,128]{1,0:T(8,128)(2,1)S(1)}, u32[]{:S(2)}, u32[]{:S(2)}) collective-permute-start(bf16[1600,128]{1,0:T(8,128)(2,1)S(1)} %bitcast_select_fusion.9), channel_id=1, source_target_pairs={{0,1},{1,0},{2,3},{3,2},{4,5},{5,4},{6,7},{7,6},{8,9},{9,8},{10,11... | collective-permute-start | bytes 1228808 | tf_op jit(solution)/shard_map/ppermute | solution.py:157
  13.0 0.4 fusion
  13.4 4.7 %collective-permute-start.3 = (bf16[1600,128]{1,0:T(8,128)(2,1)S(1)}, bf16[1600,128]{1,0:T(8,128)(2,1)S(1)}, u32[]{:S(2)}, u32[]{:S(2)}) collective-permute-start(bf16[1600,128]{1,0:T(8,128)(2,1)S(1)} %collective-permute-done.1), channel_id=1, source_target_pairs={{0,2},{1,15},{2,4},{3,1},{4,6},{5,3},{6,8},{7,5},{8,10},{9,7},{10,... | collective-permute-start | bytes 1228808 | tf_op jit(solution)/shard_map/ppermute | solution.py:170
  18.2 2.6 %collective-permute-start.4 = (bf16[1600,128]{1,0:T(8,128)(2,1)S(1)}, bf16[1600,128]{1,0:T(8,128)(2,1)S(1)}, u32[]{:S(2)}, u32[]{:S(2)}) collective-permute-start(bf16[1600,128]{1,0:T(8,128)(2,1)S(1)} %collective-permute-done.2), channel_id=1, source_target_pairs={{0,2},{1,15},{2,4},{3,1},{4,6},{5,3},{6,8},{7,5},{8,10},{9,7},{10,... | collective-permute-start | bytes 1228808 | tf_op jit(solution)/shard_map/ppermute | solution.py:170
  22.1 1.4 %collective-permute-done.3 = bf16[1600,128]{1,0:T(8,128)(2,1)S(1)} collective-permute-done((bf16[1600,128]{1,0:T(8,128)(2,1)S(1)}, bf16[1600,128]{1,0:T(8,128)(2,1)S(1)}, u32[]{:S(2)}, u32[]{:S(2)}) %collective-permute-start.3) | collective-permute-done | bytes 409632 | tf_op jit(solution)/shard_map/ppermute | solution.py:170
  23.6 4.4 %collective-permute-start.5 = (bf16[1600,128]{1,0:T(8,128)(2,1)S(1)}, bf16[1600,128]{1,0:T(8,128)(2,1)S(1)}, u32[]{:S(2)}, u32[]{:S(2)}) collective-permute-start(bf16[1600,128]{1,0:T(8,128)(2,1)S(1)} %collective-permute-done.3), channel_id=1, source_target_pairs={{0,2},{1,15},{2,4},{3,1},{4,6},{5,3},{6,8},{7,5},{8,10},{9,7},{10,... | collective-permute-start | bytes 1228808 | tf_op jit(solution)/shard_map/ppermute | solution.py:170
  28.7 3.7 %collective-permute-start.6 = (bf16[1600,128]{1,0:T(8,128)(2,1)S(1)}, bf16[1600,128]{1,0:T(8,128)(2,1)S(1)}, u32[]{:S(2)}, u32[]{:S(2)}) collective-permute-start(bf16[1600,128]{1,0:T(8,128)(2,1)S(1)} %collective-permute-done.4), channel_id=1, source_target_pairs={{0,2},{1,15},{2,4},{3,1},{4,6},{5,3},{6,8},{7,5},{8,10},{9,7},{10,... | collective-permute-start | bytes 1228808 | tf_op jit(solution)/shard_map/ppermute | solution.py:170
  33.1 0.4 collective-permute-done.5
  33.5 5.2 %collective-permute-start.7 = (bf16[1600,128]{1,0:T(8,128)(2,1)S(1)}, bf16[1600,128]{1,0:T(8,128)(2,1)S(1)}, u32[]{:S(2)}, u32[]{:S(2)}) collective-permute-start(bf16[1600,128]{1,0:T(8,128)(2,1)S(1)} %collective-permute-done.5), channel_id=1, source_target_pairs={{0,2},{1,15},{2,4},{3,1},{4,6},{5,3},{6,8},{7,5},{8,10},{9,7},{10,... | collective-permute-start | bytes 1228808 | tf_op jit(solution)/shard_map/ppermute | solution.py:170
  39.4 4.0 %collective-permute-start.8 = (bf16[1600,128]{1,0:T(8,128)(2,1)S(1)}, bf16[1600,128]{1,0:T(8,128)(2,1)S(1)}, u32[]{:S(2)}, u32[]{:S(2)}) collective-permute-start(bf16[1600,128]{1,0:T(8,128)(2,1)S(1)} %collective-permute-done.6), channel_id=1, source_target_pairs={{0,2},{1,15},{2,4},{3,1},{4,6},{5,3},{6,8},{7,5},{8,10},{9,7},{10,... | collective-permute-start | bytes 1228808 | tf_op jit(solution)/shard_map/ppermute | solution.py:170
  44.1 0.4 collective-permute-done.7
  44.5 4.7 %collective-permute-done.8 = bf16[1600,128]{1,0:T(8,128)(2,1)S(1)} collective-permute-done((bf16[1600,128]{1,0:T(8,128)(2,1)S(1)}, bf16[1600,128]{1,0:T(8,128)(2,1)S(1)}, u32[]{:S(2)}, u32[]{:S(2)}) %collective-permute-start.8) | collective-permute-done | bytes 409632 | tf_op jit(solution)/shard_map/ppermute | solution.py:170
  49.3 0.3 convolution_dynamic-update-slice_fusion.2
  50.3 17.9 %all_to_all.10 = f32[8,4,64,128]{3,2,1,0:T(8,128)S(1)} all-to-all(f32[8,4,64,128]{3,2,1,0:T(8,128)S(1)} %bitcast.64), channel_id=1, replica_groups={{400,16,384,0,256,272,144,128},{385,1,401,17,129,145,257,273},{146,18,1..., dimensions={0} | all-to-all | bytes 2097152 | tf_op jit(solution)/shard_map/all_to_all | solution.py:181
  68.3 12.9 %all_to_all.11 = f32[4,64,128]{2,1,0:T(8,128)S(1)} all-to-all(f32[4,64,128]{2,1,0:T(8,128)S(1)} %reduce_sum.18), channel_id=1, replica_groups={{400,496,432,464},{16,48,112,80},{480,448,384,416},{96,0,32,64},{256,35..., dimensions={0} | all-to-all | bytes 262144 | tf_op jit(solution)/shard_map/all_to_all | solution.py:182
  81.3 8.2 %collective-permute-start.11 = (f32[64,128]{1,0:T(8,128)S(1)}, f32[64,128]{1,0:T(8,128)S(1)}, u32[]{:S(2)}, u32[]{:S(2)}) collective-permute-start(f32[64,128]{1,0:T(8,128)S(1)} %reduce_sum.19), channel_id=1, source_target_pairs={{16,1},{97,2},{481,3},{241,4},{161,5},{209,6},{225,7},{240,8},{128... | collective-permute-start | bytes 98312 | tf_op jit(solution)/shard_map/ppermute | solution.py:185
  89.5 7.7 %collective-permute-start.10 = (f32[64,128]{0,1:T(8,128)S(1)}, f32[64,128]{0,1:T(8,128)S(1)}, u32[]{:S(2)}, u32[]{:S(2)}) collective-permute-start(f32[64,128]{0,1:T(8,128)S(1)} %copy.4), channel_id=1, source_target_pairs={{400,0},{1,1},{162,2},{242,3},{4,4},{388,5},{406,6},{102,7},{9,8},... | collective-permute-start | bytes 98312 | tf_op jit(solution)/shard_map/ppermute | solution.py:186
  97.2 1.9 %collective-permute-start.9 = (f32[64,128]{0,1:T(8,128)S(1)}, f32[64,128]{0,1:T(8,128)S(1)}, u32[]{:S(2)}, u32[]{:S(2)}) collective-permute-start(f32[64,128]{0,1:T(8,128)S(1)} %copy.4), channel_id=1, source_target_pairs={{496,0},{33,1},{130,2},{146,3},{36,4},{484,5},{502,6},{6,7},{41,8}... | collective-permute-start | bytes 98312 | tf_op jit(solution)/shard_map/ppermute | solution.py:187
  99.2 6.3 %collective-permute-done.9 = f32[64,128]{0,1:T(8,128)S(1)} collective-permute-done((f32[64,128]{0,1:T(8,128)S(1)}, f32[64,128]{0,1:T(8,128)S(1)}, u32[]{:S(2)}, u32[]{:S(2)}) %collective-permute-start.9) | collective-permute-done | bytes 32800 | tf_op jit(solution)/shard_map/ppermute | solution.py:187
  105.5 0.7 maximum_add_fusion
  (49 shorter events, 6.7 us)
Async XLA Ops:
  1.2 12.2 %collective-permute-start.1 = (bf16[1600,128]{1,0:T(8,128)(2,1)S(1)}, bf16[1600,128]{1,0:T(8,128)(2,1)S(1)}, u32[]{:S(2)}, u32[]{:S(2)}) collective-permute-start(bf16[1600,128]{1,0:T(8,128)(2,1)S(1)} %bitcast.62), channel_id=1, source_target_pairs={{0,2},{1,15},{2,4},{3,1},{4,6},{5,3},{6,8},{7,5},{8,10},{9,7},{10,... | collective-permute-start | bytes 1228808 | tf_op jit(solution)/shard_map/ppermute | solution.py:154
  4.7 13.5 %collective-permute-start.2 = (bf16[1600,128]{1,0:T(8,128)(2,1)S(1)}, bf16[1600,128]{1,0:T(8,128)(2,1)S(1)}, u32[]{:S(2)}, u32[]{:S(2)}) collective-permute-start(bf16[1600,128]{1,0:T(8,128)(2,1)S(1)} %bitcast.60), channel_id=1, source_target_pairs={{1,2},{0,15},{3,4},{2,1},{5,6},{4,3},{7,8},{6,5},{9,10},{8,7},{11,... | collective-permute-start | bytes 1228808 | tf_op jit(solution)/shard_map/ppermute | solution.py:154
  8.3 0.7 copy-start.1
  9.3 3.6 %copy-start = (bf16[8,400,128]{2,1,0:T(8,128)(2,1)S(1)}, bf16[8,400,128]{2,1,0:T(8,128)(2,1)}, u32[]{:S(2)}) copy-start(bf16[8,400,128]{2,1,0:T(8,128)(2,1)} %param.2) | copy-start | bytes 2457604
  9.4 11.4 %collective-permute-start = (bf16[1600,128]{1,0:T(8,128)(2,1)S(1)}, bf16[1600,128]{1,0:T(8,128)(2,1)S(1)}, u32[]{:S(2)}, u32[]{:S(2)}) collective-permute-start(bf16[1600,128]{1,0:T(8,128)(2,1)S(1)} %bitcast_select_fusion.9), channel_id=1, source_target_pairs={{0,1},{1,0},{2,3},{3,2},{4,5},{5,4},{6,7},{7,6},{8,9},{9,8},{10,11... | collective-permute-start | bytes 1228808 | tf_op jit(solution)/shard_map/ppermute | solution.py:157
  13.4 10.2 %collective-permute-start.3 = (bf16[1600,128]{1,0:T(8,128)(2,1)S(1)}, bf16[1600,128]{1,0:T(8,128)(2,1)S(1)}, u32[]{:S(2)}, u32[]{:S(2)}) collective-permute-start(bf16[1600,128]{1,0:T(8,128)(2,1)S(1)} %collective-permute-done.1), channel_id=1, source_target_pairs={{0,2},{1,15},{2,4},{3,1},{4,6},{5,3},{6,8},{7,5},{8,10},{9,7},{10,... | collective-permute-start | bytes 1228808 | tf_op jit(solution)/shard_map/ppermute | solution.py:170
  18.2 10.5 %collective-permute-start.4 = (bf16[1600,128]{1,0:T(8,128)(2,1)S(1)}, bf16[1600,128]{1,0:T(8,128)(2,1)S(1)}, u32[]{:S(2)}, u32[]{:S(2)}) collective-permute-start(bf16[1600,128]{1,0:T(8,128)(2,1)S(1)} %collective-permute-done.2), channel_id=1, source_target_pairs={{0,2},{1,15},{2,4},{3,1},{4,6},{5,3},{6,8},{7,5},{8,10},{9,7},{10,... | collective-permute-start | bytes 1228808 | tf_op jit(solution)/shard_map/ppermute | solution.py:170
  23.6 9.9 %collective-permute-start.5 = (bf16[1600,128]{1,0:T(8,128)(2,1)S(1)}, bf16[1600,128]{1,0:T(8,128)(2,1)S(1)}, u32[]{:S(2)}, u32[]{:S(2)}) collective-permute-start(bf16[1600,128]{1,0:T(8,128)(2,1)S(1)} %collective-permute-done.3), channel_id=1, source_target_pairs={{0,2},{1,15},{2,4},{3,1},{4,6},{5,3},{6,8},{7,5},{8,10},{9,7},{10,... | collective-permute-start | bytes 1228808 | tf_op jit(solution)/shard_map/ppermute | solution.py:170
  28.7 10.7 %collective-permute-start.6 = (bf16[1600,128]{1,0:T(8,128)(2,1)S(1)}, bf16[1600,128]{1,0:T(8,128)(2,1)S(1)}, u32[]{:S(2)}, u32[]{:S(2)}) collective-permute-start(bf16[1600,128]{1,0:T(8,128)(2,1)S(1)} %collective-permute-done.4), channel_id=1, source_target_pairs={{0,2},{1,15},{2,4},{3,1},{4,6},{5,3},{6,8},{7,5},{8,10},{9,7},{10,... | collective-permute-start | bytes 1228808 | tf_op jit(solution)/shard_map/ppermute | solution.py:170
  33.5 11.0 %collective-permute-start.7 = (bf16[1600,128]{1,0:T(8,128)(2,1)S(1)}, bf16[1600,128]{1,0:T(8,128)(2,1)S(1)}, u32[]{:S(2)}, u32[]{:S(2)}) collective-permute-start(bf16[1600,128]{1,0:T(8,128)(2,1)S(1)} %collective-permute-done.5), channel_id=1, source_target_pairs={{0,2},{1,15},{2,4},{3,1},{4,6},{5,3},{6,8},{7,5},{8,10},{9,7},{10,... | collective-permute-start | bytes 1228808 | tf_op jit(solution)/shard_map/ppermute | solution.py:170
  39.4 9.8 %collective-permute-start.8 = (bf16[1600,128]{1,0:T(8,128)(2,1)S(1)}, bf16[1600,128]{1,0:T(8,128)(2,1)S(1)}, u32[]{:S(2)}, u32[]{:S(2)}) collective-permute-start(bf16[1600,128]{1,0:T(8,128)(2,1)S(1)} %collective-permute-done.6), channel_id=1, source_target_pairs={{0,2},{1,15},{2,4},{3,1},{4,6},{5,3},{6,8},{7,5},{8,10},{9,7},{10,... | collective-permute-start | bytes 1228808 | tf_op jit(solution)/shard_map/ppermute | solution.py:170
  81.3 17.9 %collective-permute-start.11 = (f32[64,128]{1,0:T(8,128)S(1)}, f32[64,128]{1,0:T(8,128)S(1)}, u32[]{:S(2)}, u32[]{:S(2)}) collective-permute-start(f32[64,128]{1,0:T(8,128)S(1)} %reduce_sum.19), channel_id=1, source_target_pairs={{16,1},{97,2},{481,3},{241,4},{161,5},{209,6},{225,7},{240,8},{128... | collective-permute-start | bytes 98312 | tf_op jit(solution)/shard_map/ppermute | solution.py:185
  89.5 9.7 %collective-permute-start.10 = (f32[64,128]{0,1:T(8,128)S(1)}, f32[64,128]{0,1:T(8,128)S(1)}, u32[]{:S(2)}, u32[]{:S(2)}) collective-permute-start(f32[64,128]{0,1:T(8,128)S(1)} %copy.4), channel_id=1, source_target_pairs={{400,0},{1,1},{162,2},{242,3},{4,4},{388,5},{406,6},{102,7},{9,8},... | collective-permute-start | bytes 98312 | tf_op jit(solution)/shard_map/ppermute | solution.py:186
  97.2 8.3 %collective-permute-start.9 = (f32[64,128]{0,1:T(8,128)S(1)}, f32[64,128]{0,1:T(8,128)S(1)}, u32[]{:S(2)}, u32[]{:S(2)}) collective-permute-start(f32[64,128]{0,1:T(8,128)S(1)} %copy.4), channel_id=1, source_target_pairs={{496,0},{33,1},{130,2},{146,3},{36,4},{484,5},{502,6},{6,7},{41,8}... | collective-permute-start | bytes 98312 | tf_op jit(solution)/shard_map/ppermute | solution.py:187

commit v8 on v7

--- a/solution.py
+++ b/solution.py
@@ -16,9 +16,8 @@
     return aux * 2 * CHIPS + (chip % CHIPS) * 2 + core
 
 
-PLACES = {(0, 0): (0, 0), (1, 1): (0, 1), (2, 1): (1, 0), (3, 1): (1, 1)}
-PLACES |= {(4, 0): (2, 0), (3, 0): (2, 1), (2, 0): (3, 0), (1, 0): (3, 1)}
-PAIRS = [0, 3, 1, 2]
+TILES = [(0, 0, 0), (0, 0, 1)]
+TILES += [(s, e, e ^ f) for s in range(1, CHIPS // 2) for f in range(2) for e in range(2)] + [(4, 0, 0), (4, 0, 1)]
 POWER, MIRRORED = 2, 1.0
 
 
@@ -37,12 +36,7 @@
 
 
 def chunks():
-    at = {place: tile for tile, place in PLACES.items()}
-    return [
-        [((*at[pair, q], m), g) for q in ((1, 0) if pair > 1 else (0, 1)) for g in range(2)]
-        for pair in PAIRS
-        for m in range(2)
-    ]
+    return [[(tile, n) for tile in TILES[k : k + 2] for n in range(2)] for k in range(0, len(TILES), 2)]
 
 
 def hops(a, b):
@@ -59,8 +53,7 @@
         for Y in range(CHIPS):
             for i in range(2):
                 (core, tile), other = sources(X, j, Y, i)
-                for g in range(2):
-                    to.setdefault((Y, core, tile, g), []).append((1.0, (A, 2 * Y + i)))
+                to.setdefault((Y, core, tile, h), []).append((1.0, (A, 2 * Y + i)))
                 if other is not None:
                     to.setdefault((X, *other, h), []).append((MIRRORED, (A, 2 * Y + i)))
     return to
@@ -107,18 +100,16 @@
 
 
 def deliveries():
-    direct = ([], [])
-    mirrored = []
+    direct, mirrored = [], []
     for A in range(AX * AZ):
         X, j, h = A // 4, A // 2 % 2, A % 2
         for Y in range(CHIPS):
             for i in range(2):
                 own, other = sources(X, j, Y, i)
-                for p in range(2):
-                    direct[p].append((holder(Y, *own, h ^ p), dev(A, Y, i)))
+                direct.append((holder(Y, *own, h), dev(A, Y, i)))
                 if other is not None:
                     mirrored.append((holder(X, *other, h), dev(A, Y, i)))
-    return direct[0], direct[1], mirrored
+    return direct, mirrored
 
 
 def local(slabs, significant):
@@ -126,7 +117,6 @@
     half = aux_here // 2
     depth = half * occupied
     row = lax.axis_index("row")
-    aux = lax.axis_index("aux")
     chip, core = row // 2, row % 2
 
     blocks = cols // BS
@@ -174,21 +164,19 @@
             low = chip < CHIPS // 2
             tiles[4, 0, 0] = dot(jnp.where(low, left[0], left[1]), jnp.where(low, near_a, near_b))
             tiles[4, 0, 1] = dot(left[0], near_b)
-    pieces = [tiles[tile] for chunk in chunks() for tile, g in chunk if g == 0]
-    pieces = jnp.concatenate(pieces, axis=0).reshape(2 * AX, AZ // 2, BS, cols)
+    pieces = jnp.concatenate([tiles[tile] for tile in TILES], axis=0).reshape(2 * AX, 2 * cols, cols)
 
     first, second = summing_groups()
     got = lax.all_to_all(pieces, BOTH, 0, 0, axis_index_groups=first, tiled=True).sum(axis=0)
+    got = got.reshape(2, 2, BS, cols)
+    packed = [jnp.concatenate([got[:, 0, :, n * BS : (n + 1) * BS], got[:, 1, :, n * BS : (n + 1) * BS]], axis=2) for n in range(2)]
+    got = jnp.concatenate([got, jnp.stack(packed, axis=1)], axis=2).reshape(4, cols, cols)
     got = lax.all_to_all(got, BOTH, 0, 0, axis_index_groups=second, tiled=True).sum(axis=0)
 
-    near, next_to, mirrored = deliveries()
-    t = lax.optimization_barrier(lax.ppermute(got, BOTH, mirrored).T)
-    d0 = lax.ppermute(got, BOTH, near)
-    d1 = lax.ppermute(got, BOTH, next_to)
-    odd = aux % 2 == 1
-    top = jnp.where(odd, d1[:, BS:], d0[:, :BS])
-    bottom = jnp.where(odd, d0[:, BS:], d1[:, :BS])
-    return jnp.concatenate([top, bottom], axis=0) + t
+    direct, mirrored = deliveries()
+    t = lax.ppermute(got[:BS], BOTH, mirrored).T
+    d = lax.ppermute(got[BS:], BOTH, direct)
+    return jnp.concatenate([d[:, :BS], d[:, BS:]], axis=0) + t
 
 
 def solution(mesh):

time: 107 us -> 107 us (level)
  the two profiles are of different devices: /device:TPU:14 before, /device:TPU:40 now
where the time goes in v8:
time: 107 us; the launch traced here: 106 us
  starting transfers between devices  42.6 us (40%)
  blocking collectives  38 us (36%)
  waiting for transfers between devices  14.7 us (14%)
  matrix products  5.24 us (5%)
  local copies, waits for them, and re-layouts  3.54 us (3%)
  other arithmetic  1.48 us (1%)
    all_to_all x1, blocking collectives, local(): lax.all_to_all(got, BOTH, 0, 0, axis_index_groups=second, tiled=True)  21.2 us
    all_to_all x1, blocking collectives, local(): lax.all_to_all(pieces, BOTH, 0, 0, axis_index_groups=first, tiled=True)  16.8 us
    ppermute x3, starting transfers between devices, local(): lax.ppermute(far_a, 'row', ring)  15.6 us
    ppermute x3, starting transfers between devices, local(): lax.ppermute(far_b, 'row', ring)  11.2 us
    ppermute x1, waiting for transfers between devices, local(): t = lax.ppermute(got[:BS], BOTH, mirrored).T  7.44 us
    ppermute x1, starting transfers between devices, local(): t = lax.ppermute(got[:BS], BOTH, mirrored).T  6.62 us
    dot_general x16, matrix products, dot(): return jnp.dot(x, y, preferred_element_type=jnp.float32)  5.24 us
    ppermute x2, starting transfers between devices, local(): far_a, far_b = (lax.ppermute(a, 'row', ring), lax.ppermute(b, 'row', cross))  4.77 us
  transfers between devices with their start and end apart: 11, of which 6 were waited for; matrix products, arithmetic and copies ran while one was open for 6% of the time, Pallas kernels for 0%

profile of v8, /device:TPU:40, one launch (start us, length us, event | category | flops | bytes accessed | tf_op | source)
XLA Modules:
  0.0 106.1 jit_solution(6793443812468664548)
XLA Ops:
  0.0 1.2 %constant_dynamic-slice_fusion = (bf16[4,400,128]{2,1,0:T(8,128)(2,1)S(1)}, bf16[4,400,128]{2,1,0:T(8,128)(2,1)S(1)}) fusion(bf16[8,400,128]{2,1,0:T(8,128)(2,1)} %param.2, s32[]{:T(128)S(6)} %select_n.273, s32[]{:T(128)S(6)} %select_n.271), kind=kLoop, calls=%fused_computation.80 | loop fusion | bytes 1638408 | tf_op jit(solution)/shard_map/dynamic_slice | solution.py:134
  1.2 2.6 %collective-permute-start.1 = (bf16[1600,128]{1,0:T(8,128)(2,1)S(1)}, bf16[1600,128]{1,0:T(8,128)(2,1)S(1)}, u32[]{:S(2)}, u32[]{:S(2)}) collective-permute-start(bf16[1600,128]{1,0:T(8,128)(2,1)S(1)} %bitcast.86), channel_id=1, source_target_pairs={{0,2},{1,15},{2,4},{3,1},{4,6},{5,3},{6,8},{7,5},{8,10},{9,7},{10,... | collective-permute-start | bytes 1228808 | tf_op jit(solution)/shard_map/ppermute | solution.py:144
  3.8 2.2 %collective-permute-start.2 = (bf16[1600,128]{1,0:T(8,128)(2,1)S(1)}, bf16[1600,128]{1,0:T(8,128)(2,1)S(1)}, u32[]{:S(2)}, u32[]{:S(2)}) collective-permute-start(bf16[1600,128]{1,0:T(8,128)(2,1)S(1)} %bitcast.84), channel_id=1, source_target_pairs={{1,2},{0,15},{3,4},{2,1},{5,6},{4,3},{7,8},{6,5},{9,10},{8,7},{11,... | collective-permute-start | bytes 1228808 | tf_op jit(solution)/shard_map/ppermute | solution.py:144
  6.2 0.7 copy-done.1
  8.2 2.6 %collective-permute-start = (bf16[1600,128]{1,0:T(8,128)(2,1)S(1)}, bf16[1600,128]{1,0:T(8,128)(2,1)S(1)}, u32[]{:S(2)}, u32[]{:S(2)}) collective-permute-start(bf16[1600,128]{1,0:T(8,128)(2,1)S(1)} %bitcast_select_fusion.8), channel_id=1, source_target_pairs={{0,1},{1,0},{2,3},{3,2},{4,5},{5,4},{6,7},{7,6},{8,9},{9,8},{10,11... | collective-permute-start | bytes 1228808 | tf_op jit(solution)/shard_map/ppermute | solution.py:147
  11.2 0.4 fusion
  11.6 1.7 %collective-permute-done.1 = bf16[1600,128]{1,0:T(8,128)(2,1)S(1)} collective-permute-done((bf16[1600,128]{1,0:T(8,128)(2,1)S(1)}, bf16[1600,128]{1,0:T(8,128)(2,1)S(1)}, u32[]{:S(2)}, u32[]{:S(2)}) %collective-permute-start.1) | collective-permute-done | bytes 409632 | tf_op jit(solution)/shard_map/ppermute | solution.py:144
  13.3 5.4 %collective-permute-start.3 = (bf16[1600,128]{1,0:T(8,128)(2,1)S(1)}, bf16[1600,128]{1,0:T(8,128)(2,1)S(1)}, u32[]{:S(2)}, u32[]{:S(2)}) collective-permute-start(bf16[1600,128]{1,0:T(8,128)(2,1)S(1)} %collective-permute-done.1), channel_id=1, source_target_pairs={{0,2},{1,15},{2,4},{3,1},{4,6},{5,3},{6,8},{7,5},{8,10},{9,7},{10,... | collective-permute-start | bytes 1228808 | tf_op jit(solution)/shard_map/ppermute | solution.py:160
  19.4 3.2 %collective-permute-start.4 = (bf16[1600,128]{1,0:T(8,128)(2,1)S(1)}, bf16[1600,128]{1,0:T(8,128)(2,1)S(1)}, u32[]{:S(2)}, u32[]{:S(2)}) collective-permute-start(bf16[1600,128]{1,0:T(8,128)(2,1)S(1)} %collective-permute-done.2), channel_id=1, source_target_pairs={{0,2},{1,15},{2,4},{3,1},{4,6},{5,3},{6,8},{7,5},{8,10},{9,7},{10,... | collective-permute-start | bytes 1228808 | tf_op jit(solution)/shard_map/ppermute | solution.py:160
  22.6 0.3 convolution_dynamic-update-slice_fusion.12
  23.6 0.5 collective-permute-done.3
  24.1 5.1 %collective-permute-start.5 = (bf16[1600,128]{1,0:T(8,128)(2,1)S(1)}, bf16[1600,128]{1,0:T(8,128)(2,1)S(1)}, u32[]{:S(2)}, u32[]{:S(2)}) collective-permute-start(bf16[1600,128]{1,0:T(8,128)(2,1)S(1)} %collective-permute-done.3), channel_id=1, source_target_pairs={{0,2},{1,15},{2,4},{3,1},{4,6},{5,3},{6,8},{7,5},{8,10},{9,7},{10,... | collective-permute-start | bytes 1228808 | tf_op jit(solution)/shard_map/ppermute | solution.py:160
  29.6 4.0 %collective-permute-start.6 = (bf16[1600,128]{1,0:T(8,128)(2,1)S(1)}, bf16[1600,128]{1,0:T(8,128)(2,1)S(1)}, u32[]{:S(2)}, u32[]{:S(2)}) collective-permute-start(bf16[1600,128]{1,0:T(8,128)(2,1)S(1)} %collective-permute-done.4), channel_id=1, source_target_pairs={{0,2},{1,15},{2,4},{3,1},{4,6},{5,3},{6,8},{7,5},{8,10},{9,7},{10,... | collective-permute-start | bytes 1228808 | tf_op jit(solution)/shard_map/ppermute | solution.py:160
  34.8 5.2 %collective-permute-start.7 = (bf16[1600,128]{1,0:T(8,128)(2,1)S(1)}, bf16[1600,128]{1,0:T(8,128)(2,1)S(1)}, u32[]{:S(2)}, u32[]{:S(2)}) collective-permute-start(bf16[1600,128]{1,0:T(8,128)(2,1)S(1)} %collective-permute-done.5), channel_id=1, source_target_pairs={{0,2},{1,15},{2,4},{3,1},{4,6},{5,3},{6,8},{7,5},{8,10},{9,7},{10,... | collective-permute-start | bytes 1228808 | tf_op jit(solution)/shard_map/ppermute | solution.py:160
  40.3 4.0 %collective-permute-start.8 = (bf16[1600,128]{1,0:T(8,128)(2,1)S(1)}, bf16[1600,128]{1,0:T(8,128)(2,1)S(1)}, u32[]{:S(2)}, u32[]{:S(2)}) collective-permute-start(bf16[1600,128]{1,0:T(8,128)(2,1)S(1)} %collective-permute-done.6), channel_id=1, source_target_pairs={{0,2},{1,15},{2,4},{3,1},{4,6},{5,3},{6,8},{7,5},{8,10},{9,7},{10,... | collective-permute-start | bytes 1228808 | tf_op jit(solution)/shard_map/ppermute | solution.py:160
  45.3 0.5 collective-permute-done.7
  45.8 4.4 %collective-permute-done.8 = bf16[1600,128]{1,0:T(8,128)(2,1)S(1)} collective-permute-done((bf16[1600,128]{1,0:T(8,128)(2,1)S(1)}, bf16[1600,128]{1,0:T(8,128)(2,1)S(1)}, u32[]{:S(2)}, u32[]{:S(2)}) %collective-permute-start.8) | collective-permute-done | bytes 409632 | tf_op jit(solution)/shard_map/ppermute | solution.py:160
  50.3 0.3 convolution_dynamic-update-slice_fusion.1
  50.9 16.8 %all_to_all.10 = f32[8,256,128]{2,1,0:T(8,128)S(1)} all-to-all(f32[8,256,128]{2,1,0:T(8,128)S(1)} %bitcast.88), channel_id=1, replica_groups={{128,384,272,0,400,256,144,16},{257,17,385,273,129,145,1,401},{274,2,14..., dimensions={0} | all-to-all | bytes 2097152 | tf_op jit(solution)/shard_map/all_to_all | solution.py:170
  68.1 21.2 %all_to_all.11 = f32[4,128,128]{2,1,0:T(8,128)S(1)} all-to-all(f32[4,128,128]{2,1,0:T(8,128)S(1)} %pad_maximum_fusion), channel_id=1, replica_groups={{224,192,128,160},{480,384,416,448},{368,272,304,336},{96,0,32,64},{496..., dimensions={0} | all-to-all | bytes 524288 | tf_op jit(solution)/shard_map/all_to_all | solution.py:174
  89.3 1.9 %collective-permute-start.9 = (f32[64,128]{1,0:T(8,128)S(1)}, f32[64,128]{1,0:T(8,128)S(1)}, u32[]{:S(2)}, u32[]{:S(2)}) collective-permute-start(f32[64,128]{1,0:T(8,128)S(1)} %get-tuple-element.40), channel_id=1, source_target_pairs={{224,0},{257,1},{34,2},{242,3},{228,4},{84,5},{38,6},{246,7},{249,... | collective-permute-start | bytes 98312 | tf_op jit(solution)/shard_map/ppermute | solution.py:178
  91.3 6.6 %collective-permute-start.10 = (f32[64,128]{1,0:T(8,128)S(1)}, f32[64,128]{1,0:T(8,128)S(1)}, u32[]{:S(2)}, u32[]{:S(2)}) collective-permute-start(f32[64,128]{1,0:T(8,128)S(1)} %get-tuple-element.39), channel_id=1, source_target_pairs={{128,1},{113,2},{481,3},{369,4},{129,5},{241,6},{97,7},{112,8},{80... | collective-permute-start | bytes 98312 | tf_op jit(solution)/shard_map/ppermute | solution.py:177
  98.0 7.4 %collective-permute-done.10 = f32[64,128]{1,0:T(8,128)S(1)} collective-permute-done((f32[64,128]{1,0:T(8,128)S(1)}, f32[64,128]{1,0:T(8,128)S(1)}, u32[]{:S(2)}, u32[]{:S(2)}) %collective-permute-start.10) | collective-permute-done | bytes 32800 | tf_op jit(solution)/shard_map/ppermute | solution.py:177
  105.5 0.6 bitcast_add_fusion
  (55 shorter events, 6.8 us)
Async XLA Ops:
  1.2 12.1 %collective-permute-start.1 = (bf16[1600,128]{1,0:T(8,128)(2,1)S(1)}, bf16[1600,128]{1,0:T(8,128)(2,1)S(1)}, u32[]{:S(2)}, u32[]{:S(2)}) collective-permute-start(bf16[1600,128]{1,0:T(8,128)(2,1)S(1)} %bitcast.86), channel_id=1, source_target_pairs={{0,2},{1,15},{2,4},{3,1},{4,6},{5,3},{6,8},{7,5},{8,10},{9,7},{10,... | collective-permute-start | bytes 1228808 | tf_op jit(solution)/shard_map/ppermute | solution.py:144
  3.8 15.6 %collective-permute-start.2 = (bf16[1600,128]{1,0:T(8,128)(2,1)S(1)}, bf16[1600,128]{1,0:T(8,128)(2,1)S(1)}, u32[]{:S(2)}, u32[]{:S(2)}) collective-permute-start(bf16[1600,128]{1,0:T(8,128)(2,1)S(1)} %bitcast.84), channel_id=1, source_target_pairs={{1,2},{0,15},{3,4},{2,1},{5,6},{4,3},{7,8},{6,5},{9,10},{8,7},{11,... | collective-permute-start | bytes 1228808 | tf_op jit(solution)/shard_map/ppermute | solution.py:144
  6.1 0.7 copy-start.1
  8.1 3.1 %copy-start = (bf16[8,400,128]{2,1,0:T(8,128)(2,1)S(1)}, bf16[8,400,128]{2,1,0:T(8,128)(2,1)}, u32[]{:S(2)}) copy-start(bf16[8,400,128]{2,1,0:T(8,128)(2,1)} %param.2) | copy-start | bytes 2457604
  8.2 10.6 %collective-permute-start = (bf16[1600,128]{1,0:T(8,128)(2,1)S(1)}, bf16[1600,128]{1,0:T(8,128)(2,1)S(1)}, u32[]{:S(2)}, u32[]{:S(2)}) collective-permute-start(bf16[1600,128]{1,0:T(8,128)(2,1)S(1)} %bitcast_select_fusion.8), channel_id=1, source_target_pairs={{0,1},{1,0},{2,3},{3,2},{4,5},{5,4},{6,7},{7,6},{8,9},{9,8},{10,11... | collective-permute-start | bytes 1228808 | tf_op jit(solution)/shard_map/ppermute | solution.py:147
  13.3 10.8 %collective-permute-start.3 = (bf16[1600,128]{1,0:T(8,128)(2,1)S(1)}, bf16[1600,128]{1,0:T(8,128)(2,1)S(1)}, u32[]{:S(2)}, u32[]{:S(2)}) collective-permute-start(bf16[1600,128]{1,0:T(8,128)(2,1)S(1)} %collective-permute-done.1), channel_id=1, source_target_pairs={{0,2},{1,15},{2,4},{3,1},{4,6},{5,3},{6,8},{7,5},{8,10},{9,7},{10,... | collective-permute-start | bytes 1228808 | tf_op jit(solution)/shard_map/ppermute | solution.py:160
  19.4 10.2 %collective-permute-start.4 = (bf16[1600,128]{1,0:T(8,128)(2,1)S(1)}, bf16[1600,128]{1,0:T(8,128)(2,1)S(1)}, u32[]{:S(2)}, u32[]{:S(2)}) collective-permute-start(bf16[1600,128]{1,0:T(8,128)(2,1)S(1)} %collective-permute-done.2), channel_id=1, source_target_pairs={{0,2},{1,15},{2,4},{3,1},{4,6},{5,3},{6,8},{7,5},{8,10},{9,7},{10,... | collective-permute-start | bytes 1228808 | tf_op jit(solution)/shard_map/ppermute | solution.py:160
  24.1 10.6 %collective-permute-start.5 = (bf16[1600,128]{1,0:T(8,128)(2,1)S(1)}, bf16[1600,128]{1,0:T(8,128)(2,1)S(1)}, u32[]{:S(2)}, u32[]{:S(2)}) collective-permute-start(bf16[1600,128]{1,0:T(8,128)(2,1)S(1)} %collective-permute-done.3), channel_id=1, source_target_pairs={{0,2},{1,15},{2,4},{3,1},{4,6},{5,3},{6,8},{7,5},{8,10},{9,7},{10,... | collective-permute-start | bytes 1228808 | tf_op jit(solution)/shard_map/ppermute | solution.py:160
  29.6 10.7 %collective-permute-start.6 = (bf16[1600,128]{1,0:T(8,128)(2,1)S(1)}, bf16[1600,128]{1,0:T(8,128)(2,1)S(1)}, u32[]{:S(2)}, u32[]{:S(2)}) collective-permute-start(bf16[1600,128]{1,0:T(8,128)(2,1)S(1)} %collective-permute-done.4), channel_id=1, source_target_pairs={{0,2},{1,15},{2,4},{3,1},{4,6},{5,3},{6,8},{7,5},{8,10},{9,7},{10,... | collective-permute-start | bytes 1228808 | tf_op jit(solution)/shard_map/ppermute | solution.py:160
  34.8 11.0 %collective-permute-start.7 = (bf16[1600,128]{1,0:T(8,128)(2,1)S(1)}, bf16[1600,128]{1,0:T(8,128)(2,1)S(1)}, u32[]{:S(2)}, u32[]{:S(2)}) collective-permute-start(bf16[1600,128]{1,0:T(8,128)(2,1)S(1)} %collective-permute-done.5), channel_id=1, source_target_pairs={{0,2},{1,15},{2,4},{3,1},{4,6},{5,3},{6,8},{7,5},{8,10},{9,7},{10,... | collective-permute-start | bytes 1228808 | tf_op jit(solution)/shard_map/ppermute | solution.py:160
  40.3 9.9 %collective-permute-start.8 = (bf16[1600,128]{1,0:T(8,128)(2,1)S(1)}, bf16[1600,128]{1,0:T(8,128)(2,1)S(1)}, u32[]{:S(2)}, u32[]{:S(2)}) collective-permute-start(bf16[1600,128]{1,0:T(8,128)(2,1)S(1)} %collective-permute-done.6), channel_id=1, source_target_pairs={{0,2},{1,15},{2,4},{3,1},{4,6},{5,3},{6,8},{7,5},{8,10},{9,7},{10,... | collective-permute-start | bytes 1228808 | tf_op jit(solution)/shard_map/ppermute | solution.py:160
  89.3 8.6 %collective-permute-start.9 = (f32[64,128]{1,0:T(8,128)S(1)}, f32[64,128]{1,0:T(8,128)S(1)}, u32[]{:S(2)}, u32[]{:S(2)}) collective-permute-start(f32[64,128]{1,0:T(8,128)S(1)} %get-tuple-element.40), channel_id=1, source_target_pairs={{224,0},{257,1},{34,2},{242,3},{228,4},{84,5},{38,6},{246,7},{249,... | collective-permute-start | bytes 98312 | tf_op jit(solution)/shard_map/ppermute | solution.py:178
  91.3 14.2 %collective-permute-start.10 = (f32[64,128]{1,0:T(8,128)S(1)}, f32[64,128]{1,0:T(8,128)S(1)}, u32[]{:S(2)}, u32[]{:S(2)}) collective-permute-start(f32[64,128]{1,0:T(8,128)S(1)} %get-tuple-element.39), channel_id=1, source_target_pairs={{128,1},{113,2},{481,3},{369,4},{129,5},{241,6},{97,7},{112,8},{80... | collective-permute-start | bytes 98312 | tf_op jit(solution)/shard_map/ppermute | solution.py:177

commit v9 on v7

--- a/solution.py
+++ b/solution.py
@@ -19,7 +19,7 @@
 PLACES = {(0, 0): (0, 0), (1, 1): (0, 1), (2, 1): (1, 0), (3, 1): (1, 1)}
 PLACES |= {(4, 0): (2, 0), (3, 0): (2, 1), (2, 0): (3, 0), (1, 0): (3, 1)}
 PAIRS = [0, 3, 1, 2]
-POWER, MIRRORED = 2, 1.0
+POWER, MIRRORED = 2, 1.25
 
 
 def sources(X, j, Y, i):

time: 107 us -> 108 us (level)
  no operation moved by 1% of the time
where the time goes in v9:
time: 108 us; the launch traced here: 107 us
  starting transfers between devices  52.5 us (49%)
  blocking collectives  30.8 us (29%)
  waiting for transfers between devices  13.3 us (12%)
  matrix products  5.23 us (5%)
  local copies, waits for them, and re-layouts  3.38 us (3%)
  other arithmetic  1.36 us (1%)
    all_to_all x1, blocking collectives, local(): lax.all_to_all(pieces, BOTH, 0, 0, axis_index_groups=first, tiled=True)  17.9 us
    ppermute x3, starting transfers between devices, local(): lax.ppermute(far_a, 'row', ring)  14.3 us
    all_to_all x1, blocking collectives, local(): lax.all_to_all(got, BOTH, 0, 0, axis_index_groups=second, tiled=True)  12.9 us
    ppermute x3, starting transfers between devices, local(): lax.ppermute(far_b, 'row', ring)  10.3 us
    ppermute x1, starting transfers between devices, local(): t = lax.optimization_barrier(lax.ppermute(got, BOTH, mirrored).T)  8.83 us
    ppermute x1, starting transfers between devices, local(): d0 = lax.ppermute(got, BOTH, near)  8.05 us
    ppermute x2, starting transfers between devices, local(): far_a, far_b = (lax.ppermute(a, 'row', ring), lax.ppermute(b, 'row', cross))  6.89 us
    ppermute x1, waiting for transfers between devices, local(): d1 = lax.ppermute(got, BOTH, next_to)  6.31 us
  transfers between devices with their start and end apart: 12, of which 5 were waited for; matrix products, arithmetic and copies ran while one was open for 6% of the time, Pallas kernels for 0%

profile of v9, /device:TPU:14, one launch (start us, length us, event | category | flops | bytes accessed | tf_op | source)
XLA Modules:
  0.0 107.1 jit_solution(2517035033715505310)
XLA Ops:
  0.0 1.2 %constant_dynamic-slice_fusion = (bf16[4,400,128]{2,1,0:T(8,128)(2,1)S(1)}, bf16[4,400,128]{2,1,0:T(8,128)(2,1)S(1)}) fusion(bf16[8,400,128]{2,1,0:T(8,128)(2,1)} %param.2, s32[]{:T(128)S(6)} %select_n.289, s32[]{:T(128)S(6)} %select_n.291), kind=kLoop, calls=%fused_computation.73 | loop fusion | bytes 1638408 | tf_op jit(solution)/shard_map/dynamic_slice | solution.py:144
  1.2 3.5 %collective-permute-start.1 = (bf16[1600,128]{1,0:T(8,128)(2,1)S(1)}, bf16[1600,128]{1,0:T(8,128)(2,1)S(1)}, u32[]{:S(2)}, u32[]{:S(2)}) collective-permute-start(bf16[1600,128]{1,0:T(8,128)(2,1)S(1)} %bitcast.62), channel_id=1, source_target_pairs={{0,2},{1,15},{2,4},{3,1},{4,6},{5,3},{6,8},{7,5},{8,10},{9,7},{10,... | collective-permute-start | bytes 1228808 | tf_op jit(solution)/shard_map/ppermute | solution.py:154
  4.7 3.4 %collective-permute-start.2 = (bf16[1600,128]{1,0:T(8,128)(2,1)S(1)}, bf16[1600,128]{1,0:T(8,128)(2,1)S(1)}, u32[]{:S(2)}, u32[]{:S(2)}) collective-permute-start(bf16[1600,128]{1,0:T(8,128)(2,1)S(1)} %bitcast.60), channel_id=1, source_target_pairs={{1,2},{0,15},{3,4},{2,1},{5,6},{4,3},{7,8},{6,5},{9,10},{8,7},{11,... | collective-permute-start | bytes 1228808 | tf_op jit(solution)/shard_map/ppermute | solution.py:154
  8.3 0.7 copy-done.1
  9.4 2.2 %collective-permute-start = (bf16[1600,128]{1,0:T(8,128)(2,1)S(1)}, bf16[1600,128]{1,0:T(8,128)(2,1)S(1)}, u32[]{:S(2)}, u32[]{:S(2)}) collective-permute-start(bf16[1600,128]{1,0:T(8,128)(2,1)S(1)} %bitcast_select_fusion.9), channel_id=1, source_target_pairs={{0,1},{1,0},{2,3},{3,2},{4,5},{5,4},{6,7},{7,6},{8,9},{9,8},{10,11... | collective-permute-start | bytes 1228808 | tf_op jit(solution)/shard_map/ppermute | solution.py:157
  13.0 0.4 fusion
  13.4 4.7 %collective-permute-start.3 = (bf16[1600,128]{1,0:T(8,128)(2,1)S(1)}, bf16[1600,128]{1,0:T(8,128)(2,1)S(1)}, u32[]{:S(2)}, u32[]{:S(2)}) collective-permute-start(bf16[1600,128]{1,0:T(8,128)(2,1)S(1)} %collective-permute-done.1), channel_id=1, source_target_pairs={{0,2},{1,15},{2,4},{3,1},{4,6},{5,3},{6,8},{7,5},{8,10},{9,7},{10,... | collective-permute-start | bytes 1228808 | tf_op jit(solution)/shard_map/ppermute | solution.py:170
  18.2 2.6 %collective-permute-start.4 = (bf16[1600,128]{1,0:T(8,128)(2,1)S(1)}, bf16[1600,128]{1,0:T(8,128)(2,1)S(1)}, u32[]{:S(2)}, u32[]{:S(2)}) collective-permute-start(bf16[1600,128]{1,0:T(8,128)(2,1)S(1)} %collective-permute-done.2), channel_id=1, source_target_pairs={{0,2},{1,15},{2,4},{3,1},{4,6},{5,3},{6,8},{7,5},{8,10},{9,7},{10,... | collective-permute-start | bytes 1228808 | tf_op jit(solution)/shard_map/ppermute | solution.py:170
  22.1 1.4 %collective-permute-done.3 = bf16[1600,128]{1,0:T(8,128)(2,1)S(1)} collective-permute-done((bf16[1600,128]{1,0:T(8,128)(2,1)S(1)}, bf16[1600,128]{1,0:T(8,128)(2,1)S(1)}, u32[]{:S(2)}, u32[]{:S(2)}) %collective-permute-start.3) | collective-permute-done | bytes 409632 | tf_op jit(solution)/shard_map/ppermute | solution.py:170
  23.6 4.4 %collective-permute-start.5 = (bf16[1600,128]{1,0:T(8,128)(2,1)S(1)}, bf16[1600,128]{1,0:T(8,128)(2,1)S(1)}, u32[]{:S(2)}, u32[]{:S(2)}) collective-permute-start(bf16[1600,128]{1,0:T(8,128)(2,1)S(1)} %collective-permute-done.3), channel_id=1, source_target_pairs={{0,2},{1,15},{2,4},{3,1},{4,6},{5,3},{6,8},{7,5},{8,10},{9,7},{10,... | collective-permute-start | bytes 1228808 | tf_op jit(solution)/shard_map/ppermute | solution.py:170
  28.7 3.7 %collective-permute-start.6 = (bf16[1600,128]{1,0:T(8,128)(2,1)S(1)}, bf16[1600,128]{1,0:T(8,128)(2,1)S(1)}, u32[]{:S(2)}, u32[]{:S(2)}) collective-permute-start(bf16[1600,128]{1,0:T(8,128)(2,1)S(1)} %collective-permute-done.4), channel_id=1, source_target_pairs={{0,2},{1,15},{2,4},{3,1},{4,6},{5,3},{6,8},{7,5},{8,10},{9,7},{10,... | collective-permute-start | bytes 1228808 | tf_op jit(solution)/shard_map/ppermute | solution.py:170
  33.1 0.4 collective-permute-done.5
  33.5 5.2 %collective-permute-start.7 = (bf16[1600,128]{1,0:T(8,128)(2,1)S(1)}, bf16[1600,128]{1,0:T(8,128)(2,1)S(1)}, u32[]{:S(2)}, u32[]{:S(2)}) collective-permute-start(bf16[1600,128]{1,0:T(8,128)(2,1)S(1)} %collective-permute-done.5), channel_id=1, source_target_pairs={{0,2},{1,15},{2,4},{3,1},{4,6},{5,3},{6,8},{7,5},{8,10},{9,7},{10,... | collective-permute-start | bytes 1228808 | tf_op jit(solution)/shard_map/ppermute | solution.py:170
  39.4 4.0 %collective-permute-start.8 = (bf16[1600,128]{1,0:T(8,128)(2,1)S(1)}, bf16[1600,128]{1,0:T(8,128)(2,1)S(1)}, u32[]{:S(2)}, u32[]{:S(2)}) collective-permute-start(bf16[1600,128]{1,0:T(8,128)(2,1)S(1)} %collective-permute-done.6), channel_id=1, source_target_pairs={{0,2},{1,15},{2,4},{3,1},{4,6},{5,3},{6,8},{7,5},{8,10},{9,7},{10,... | collective-permute-start | bytes 1228808 | tf_op jit(solution)/shard_map/ppermute | solution.py:170
  44.1 0.4 collective-permute-done.7
  44.5 4.7 %collective-permute-done.8 = bf16[1600,128]{1,0:T(8,128)(2,1)S(1)} collective-permute-done((bf16[1600,128]{1,0:T(8,128)(2,1)S(1)}, bf16[1600,128]{1,0:T(8,128)(2,1)S(1)}, u32[]{:S(2)}, u32[]{:S(2)}) %collective-permute-start.8) | collective-permute-done | bytes 409632 | tf_op jit(solution)/shard_map/ppermute | solution.py:170
  49.3 0.3 convolution_dynamic-update-slice_fusion.2
  50.3 17.9 %all_to_all.10 = f32[8,4,64,128]{3,2,1,0:T(8,128)S(1)} all-to-all(f32[8,4,64,128]{3,2,1,0:T(8,128)S(1)} %bitcast.64), channel_id=1, replica_groups={{272,16,0,384,256,400,144,128},{385,1,401,17,145,129,257,273},{146,18,1..., dimensions={0} | all-to-all | bytes 2097152 | tf_op jit(solution)/shard_map/all_to_all | solution.py:181
  68.3 12.9 %all_to_all.11 = f32[4,64,128]{2,1,0:T(8,128)S(1)} all-to-all(f32[4,64,128]{2,1,0:T(8,128)S(1)} %reduce_sum.18), channel_id=1, replica_groups={{272,368,304,336},{16,48,112,80},{96,64,0,32},{480,448,384,416},{256,35..., dimensions={0} | all-to-all | bytes 262144 | tf_op jit(solution)/shard_map/all_to_all | solution.py:182
  81.2 8.8 %collective-permute-start.11 = (f32[64,128]{1,0:T(8,128)S(1)}, f32[64,128]{1,0:T(8,128)S(1)}, u32[]{:S(2)}, u32[]{:S(2)}) collective-permute-start(f32[64,128]{1,0:T(8,128)S(1)} %reduce_sum.19), channel_id=1, source_target_pairs={{16,1},{97,2},{481,3},{129,4},{209,5},{225,6},{241,7},{240,8},{128... | collective-permute-start | bytes 98312 | tf_op jit(solution)/shard_map/ppermute | solution.py:185
  90.1 8.0 %collective-permute-start.10 = (f32[64,128]{0,1:T(8,128)S(1)}, f32[64,128]{0,1:T(8,128)S(1)}, u32[]{:S(2)}, u32[]{:S(2)}) collective-permute-start(f32[64,128]{0,1:T(8,128)S(1)} %copy.4), channel_id=1, source_target_pairs={{272,0},{1,1},{162,2},{242,3},{132,4},{388,5},{406,6},{102,7},{121... | collective-permute-start | bytes 98312 | tf_op jit(solution)/shard_map/ppermute | solution.py:186
  98.2 1.9 %collective-permute-start.9 = (f32[64,128]{0,1:T(8,128)S(1)}, f32[64,128]{0,1:T(8,128)S(1)}, u32[]{:S(2)}, u32[]{:S(2)}) collective-permute-start(f32[64,128]{0,1:T(8,128)S(1)} %copy.4), channel_id=1, source_target_pairs={{368,0},{33,1},{130,2},{146,3},{164,4},{484,5},{502,6},{6,7},{25,8... | collective-permute-start | bytes 98312 | tf_op jit(solution)/shard_map/ppermute | solution.py:187
  100.1 6.3 %collective-permute-done.9 = f32[64,128]{0,1:T(8,128)S(1)} collective-permute-done((f32[64,128]{0,1:T(8,128)S(1)}, f32[64,128]{0,1:T(8,128)S(1)}, u32[]{:S(2)}, u32[]{:S(2)}) %collective-permute-start.9) | collective-permute-done | bytes 32800 | tf_op jit(solution)/shard_map/ppermute | solution.py:187
  106.5 0.7 maximum_add_fusion
  (49 shorter events, 6.7 us)
Async XLA Ops:
  1.2 12.2 %collective-permute-start.1 = (bf16[1600,128]{1,0:T(8,128)(2,1)S(1)}, bf16[1600,128]{1,0:T(8,128)(2,1)S(1)}, u32[]{:S(2)}, u32[]{:S(2)}) collective-permute-start(bf16[1600,128]{1,0:T(8,128)(2,1)S(1)} %bitcast.62), channel_id=1, source_target_pairs={{0,2},{1,15},{2,4},{3,1},{4,6},{5,3},{6,8},{7,5},{8,10},{9,7},{10,... | collective-permute-start | bytes 1228808 | tf_op jit(solution)/shard_map/ppermute | solution.py:154
  4.7 13.5 %collective-permute-start.2 = (bf16[1600,128]{1,0:T(8,128)(2,1)S(1)}, bf16[1600,128]{1,0:T(8,128)(2,1)S(1)}, u32[]{:S(2)}, u32[]{:S(2)}) collective-permute-start(bf16[1600,128]{1,0:T(8,128)(2,1)S(1)} %bitcast.60), channel_id=1, source_target_pairs={{1,2},{0,15},{3,4},{2,1},{5,6},{4,3},{7,8},{6,5},{9,10},{8,7},{11,... | collective-permute-start | bytes 1228808 | tf_op jit(solution)/shard_map/ppermute | solution.py:154
  8.3 0.7 copy-start.1
  9.3 3.6 %copy-start = (bf16[8,400,128]{2,1,0:T(8,128)(2,1)S(1)}, bf16[8,400,128]{2,1,0:T(8,128)(2,1)}, u32[]{:S(2)}) copy-start(bf16[8,400,128]{2,1,0:T(8,128)(2,1)} %param.2) | copy-start | bytes 2457604
  9.4 11.4 %collective-permute-start = (bf16[1600,128]{1,0:T(8,128)(2,1)S(1)}, bf16[1600,128]{1,0:T(8,128)(2,1)S(1)}, u32[]{:S(2)}, u32[]{:S(2)}) collective-permute-start(bf16[1600,128]{1,0:T(8,128)(2,1)S(1)} %bitcast_select_fusion.9), channel_id=1, source_target_pairs={{0,1},{1,0},{2,3},{3,2},{4,5},{5,4},{6,7},{7,6},{8,9},{9,8},{10,11... | collective-permute-start | bytes 1228808 | tf_op jit(solution)/shard_map/ppermute | solution.py:157
  13.4 10.2 %collective-permute-start.3 = (bf16[1600,128]{1,0:T(8,128)(2,1)S(1)}, bf16[1600,128]{1,0:T(8,128)(2,1)S(1)}, u32[]{:S(2)}, u32[]{:S(2)}) collective-permute-start(bf16[1600,128]{1,0:T(8,128)(2,1)S(1)} %collective-permute-done.1), channel_id=1, source_target_pairs={{0,2},{1,15},{2,4},{3,1},{4,6},{5,3},{6,8},{7,5},{8,10},{9,7},{10,... | collective-permute-start | bytes 1228808 | tf_op jit(solution)/shard_map/ppermute | solution.py:170
  18.2 10.5 %collective-permute-start.4 = (bf16[1600,128]{1,0:T(8,128)(2,1)S(1)}, bf16[1600,128]{1,0:T(8,128)(2,1)S(1)}, u32[]{:S(2)}, u32[]{:S(2)}) collective-permute-start(bf16[1600,128]{1,0:T(8,128)(2,1)S(1)} %collective-permute-done.2), channel_id=1, source_target_pairs={{0,2},{1,15},{2,4},{3,1},{4,6},{5,3},{6,8},{7,5},{8,10},{9,7},{10,... | collective-permute-start | bytes 1228808 | tf_op jit(solution)/shard_map/ppermute | solution.py:170
  23.6 9.9 %collective-permute-start.5 = (bf16[1600,128]{1,0:T(8,128)(2,1)S(1)}, bf16[1600,128]{1,0:T(8,128)(2,1)S(1)}, u32[]{:S(2)}, u32[]{:S(2)}) collective-permute-start(bf16[1600,128]{1,0:T(8,128)(2,1)S(1)} %collective-permute-done.3), channel_id=1, source_target_pairs={{0,2},{1,15},{2,4},{3,1},{4,6},{5,3},{6,8},{7,5},{8,10},{9,7},{10,... | collective-permute-start | bytes 1228808 | tf_op jit(solution)/shard_map/ppermute | solution.py:170
  28.7 10.7 %collective-permute-start.6 = (bf16[1600,128]{1,0:T(8,128)(2,1)S(1)}, bf16[1600,128]{1,0:T(8,128)(2,1)S(1)}, u32[]{:S(2)}, u32[]{:S(2)}) collective-permute-start(bf16[1600,128]{1,0:T(8,128)(2,1)S(1)} %collective-permute-done.4), channel_id=1, source_target_pairs={{0,2},{1,15},{2,4},{3,1},{4,6},{5,3},{6,8},{7,5},{8,10},{9,7},{10,... | collective-permute-start | bytes 1228808 | tf_op jit(solution)/shard_map/ppermute | solution.py:170
  33.5 11.0 %collective-permute-start.7 = (bf16[1600,128]{1,0:T(8,128)(2,1)S(1)}, bf16[1600,128]{1,0:T(8,128)(2,1)S(1)}, u32[]{:S(2)}, u32[]{:S(2)}) collective-permute-start(bf16[1600,128]{1,0:T(8,128)(2,1)S(1)} %collective-permute-done.5), channel_id=1, source_target_pairs={{0,2},{1,15},{2,4},{3,1},{4,6},{5,3},{6,8},{7,5},{8,10},{9,7},{10,... | collective-permute-start | bytes 1228808 | tf_op jit(solution)/shard_map/ppermute | solution.py:170
  39.4 9.8 %collective-permute-start.8 = (bf16[1600,128]{1,0:T(8,128)(2,1)S(1)}, bf16[1600,128]{1,0:T(8,128)(2,1)S(1)}, u32[]{:S(2)}, u32[]{:S(2)}) collective-permute-start(bf16[1600,128]{1,0:T(8,128)(2,1)S(1)} %collective-permute-done.6), channel_id=1, source_target_pairs={{0,2},{1,15},{2,4},{3,1},{4,6},{5,3},{6,8},{7,5},{8,10},{9,7},{10,... | collective-permute-start | bytes 1228808 | tf_op jit(solution)/shard_map/ppermute | solution.py:170
  81.2 18.9 %collective-permute-start.11 = (f32[64,128]{1,0:T(8,128)S(1)}, f32[64,128]{1,0:T(8,128)S(1)}, u32[]{:S(2)}, u32[]{:S(2)}) collective-permute-start(f32[64,128]{1,0:T(8,128)S(1)} %reduce_sum.19), channel_id=1, source_target_pairs={{16,1},{97,2},{481,3},{129,4},{209,5},{225,6},{241,7},{240,8},{128... | collective-permute-start | bytes 98312 | tf_op jit(solution)/shard_map/ppermute | solution.py:185
  90.1 10.0 %collective-permute-start.10 = (f32[64,128]{0,1:T(8,128)S(1)}, f32[64,128]{0,1:T(8,128)S(1)}, u32[]{:S(2)}, u32[]{:S(2)}) collective-permute-start(f32[64,128]{0,1:T(8,128)S(1)} %copy.4), channel_id=1, source_target_pairs={{272,0},{1,1},{162,2},{242,3},{132,4},{388,5},{406,6},{102,7},{121... | collective-permute-start | bytes 98312 | tf_op jit(solution)/shard_map/ppermute | solution.py:186
  98.2 8.3 %collective-permute-start.9 = (f32[64,128]{0,1:T(8,128)S(1)}, f32[64,128]{0,1:T(8,128)S(1)}, u32[]{:S(2)}, u32[]{:S(2)}) collective-permute-start(f32[64,128]{0,1:T(8,128)S(1)} %copy.4), channel_id=1, source_target_pairs={{368,0},{33,1},{130,2},{146,3},{164,4},{484,5},{502,6},{6,7},{25,8... | collective-permute-start | bytes 98312 | tf_op jit(solution)/shard_map/ppermute | solution.py:187
